TPU v7x, 32 devices: a whole 2x2x4 slice. The times are simulated.
32 devices in a mesh: strip: 8 (over z, x), col: 4 (over y, core).
Axes of the slice: x: 2, y: 2, z: 4, core: 2. Of those that a mesh axis runs over, the one named last changes fastest.
Arguments:
- net_box: int32 [32768, 4], P(('strip', 'col')), may hold values from 0 to 1023, as said below
- net_weight: float32 [32768], P(('strip', 'col')), may hold values from 0.5 to 2
- pin_bin: int32 [32768, 4, 2], P(('strip', 'col')), may hold values from 0 to 1023, as said below
- conv_first: bfloat16 [3, 3, 32, 3], replicated, may hold values from -1.25 to 1.25
- bias_first: float32 [32], replicated, may hold values from -3 to 3
- conv_second: bfloat16 [3, 3, 32, 32], replicated, may hold values from -0.375 to 0.375
- bias_second: float32 [32], replicated, may hold values from -3 to 3
- cotangent: bfloat16 [512, 32, 1024], P('col', None, 'strip'), may hold values from -6 to 6
Outputs:
- congestion: bfloat16 [512, 32, 1024], P('col', None, 'strip')
- net_grad: float32 [32768], P(('strip', 'col'))
Inputs may be any that keep to these rules, and one draw needn't show every extreme that they name: `net_box`: box n = (x0, x1, y0, y1) has x0 <= x1 < x0 + 16 and y0 <= y1 < y0 + 16; y0 lies in rows s * 128 to (s + 1) * 128 - 1, where s = n // 4096 is the strip whose devices hold net n. Some box is 16 bins tall and wide. `pin_bin`: every pin of net n lies in net n's box.
All inputs are finite; a program needn't handle non-finite values.
Results may differ from a plain program's by a relative error of at most 0.0054.
Values may be sent and summed in bfloat16 or wider, within the bound.
No kernel may reach another device: no remote copies, remote signals or barrier semaphores. Data moves between devices by JAX's collectives and lax.ppermute only.
A program may use at most 192 MiB of HBM per device.

v0:
```python
import math

import jax
import jax.numpy as jnp
from jax import lax
from jax.sharding import PartitionSpec as P


def from_behind(x, axis, by):
    size = lax.axis_size(axis)
    pairs = [(i, i + by) for i in range(size) if 0 <= i + by < size]
    return lax.ppermute(x, axis, pairs)


def with_halo(block, sides, width):
    for axis, dim in sides:
        count = lax.axis_size(axis)
        forward = [(i, i + 1) for i in range(count - 1)]
        backward = [(target, source) for source, target in forward]
        low = lax.ppermute(
            lax.slice_in_dim(block, block.shape[dim] - width, None, axis=dim), axis, forward
        )
        high = lax.ppermute(lax.slice_in_dim(block, 0, width, axis=dim), axis, backward)
        block = jnp.concatenate([low, block, high], axis=dim)
    return block


def silu_slope(pre_act):
    sigmoid = jax.nn.sigmoid(pre_act)
    return sigmoid * (1.0 + pre_act * (1.0 - sigmoid))


def conv_valid(padded, weights, out_cols, out_rows):
    summed = None
    for shift_row in range(3):
        for shift_col in range(3):
            window = padded[shift_col : shift_col + out_cols, :, shift_row : shift_row + out_rows]
            product = jnp.einsum(
                "oi,xiy->xoy",
                weights[shift_row, shift_col],
                window,
                preferred_element_type=jnp.float32,
            )
            summed = product if summed is None else summed + product
    return summed


def conv_back(padded, weights, out_cols, out_rows):
    summed = None
    for shift_row in range(3):
        for shift_col in range(3):
            window = padded[
                2 - shift_col : 2 - shift_col + out_cols,
                :,
                2 - shift_row : 2 - shift_row + out_rows,
            ]
            product = jnp.einsum(
                "oi,xoy->xiy",
                weights[shift_row, shift_col],
                window,
                preferred_element_type=jnp.float32,
            )
            summed = product if summed is None else summed + product
    return summed


def strip_factors(box_rows, weights, pin_list, first_row, span):
    row_ids = first_row + jnp.arange(2 * span, dtype=jnp.int32)
    top_row = box_rows[:, 2]
    bottom_row = box_rows[:, 3]
    inside = (top_row[:, None] <= row_ids[None, :]) & (row_ids[None, :] <= bottom_row[:, None])
    box_height = (bottom_row - top_row + 1).astype(jnp.float32)
    box_width = (box_rows[:, 1] - box_rows[:, 0] + 1).astype(jnp.float32)
    values = jnp.stack([weights / box_height, weights / box_width], axis=1).astype(jnp.bfloat16)
    row_factor = inside.astype(jnp.bfloat16).reshape(-1, 2, 1, span) * values[:, None, :, None]
    pin_rows = pin_list[:, :, 0].reshape(-1)
    pin_factor = (pin_rows[:, None] == row_ids[None, :]).astype(jnp.bfloat16).reshape(-1, 2, span)
    return (row_factor, pin_list[:, :, 1].reshape(-1), pin_factor)


def column_block(col_ids, left_col, right_col, row_factor, pin_col, pin_factor):
    net_cols = (
        (left_col[:, None] <= col_ids[None, :]) & (col_ids[None, :] <= right_col[:, None])
    ).astype(jnp.bfloat16)
    pin_cols = (pin_col[:, None] == col_ids[None, :]).astype(jnp.bfloat16)
    demand = jnp.einsum("nk,nhcr->khcr", net_cols, row_factor, preferred_element_type=jnp.float32)
    density = jnp.einsum("pk,phr->khr", pin_cols, pin_factor, preferred_element_type=jnp.float32)
    return jnp.concatenate([demand, density[:, :, None, :]], axis=2)


def shards(
    net_box, net_weight, pin_bin, conv_first, bias_first, conv_second, bias_second, cotangent
):
    tile_cols = cotangent.shape[0]
    span = cotangent.shape[2]
    net_total = net_box.shape[0]
    strip_index = lax.axis_index("strip")
    col_index = lax.axis_index("col")
    all_rows = span * lax.axis_size("strip")
    all_cols = tile_cols * lax.axis_size("col")
    first_row = strip_index * span
    pin_width = pin_bin.shape[1]
    packed = jnp.concatenate(
        [
            net_box.astype(jnp.float32),
            pin_bin.reshape(net_total, 2 * pin_width).astype(jnp.float32),
            net_weight[:, None],
        ],
        axis=1,
    )
    own_cols = col_index * tile_cols + jnp.arange(tile_cols, dtype=jnp.int32)
    start_terms = jnp.zeros((tile_cols, 2, 3, span), jnp.float32)
    shard_piece = lax.all_gather(packed, "col", axis=0, tiled=True)
    piece_rows = shard_piece.shape[0]
    block_size = math.gcd(piece_rows, 1024)
    grouped = shard_piece.reshape(piece_rows // block_size, block_size, shard_piece.shape[1])

    def one_group(summed, net_group):
        box_rows = net_group[:, :4].astype(jnp.int32)
        pin_list = (
            net_group[:, 4 : 4 + 2 * pin_width].reshape(block_size, pin_width, 2).astype(jnp.int32)
        )
        weights = net_group[:, 4 + 2 * pin_width]
        row_factor, pin_col, pin_factor = strip_factors(
            box_rows, weights, pin_list, first_row, span
        )
        return (
            summed
            + column_block(
                own_cols, box_rows[:, 0], box_rows[:, 1], row_factor, pin_col, pin_factor
            ),
            None,
        )

    summed, unused = lax.scan(one_group, start_terms, grouped)
    spilled = from_behind(summed[:, 1].astype(jnp.bfloat16), "strip", 1).astype(jnp.float32)
    features = (summed[:, 0] + spilled).astype(jnp.bfloat16)
    stacked = jnp.concatenate([features, cotangent], axis=1)
    padded = with_halo(stacked, (("strip", 2), ("col", 0)), 2)
    in_channels = features.shape[1]
    col_ids = col_index * tile_cols - 1 + jnp.arange(tile_cols + 2, dtype=jnp.int32)
    row_ids = first_row - 1 + jnp.arange(span + 2, dtype=jnp.int32)
    inside = ((col_ids >= 0) & (col_ids < all_cols))[:, None, None] & (
        (row_ids >= 0) & (row_ids < all_rows)
    )[None, None, :]
    pre_act = (
        conv_valid(padded[:, :in_channels], conv_first, tile_cols + 2, span + 2)
        + bias_first[None, :, None]
    )
    hidden = jnp.where(inside, jax.nn.silu(pre_act), 0.0).astype(jnp.bfloat16)
    congestion = (
        conv_valid(hidden, conv_second, tile_cols, span) + bias_second[None, :, None]
    ).astype(jnp.bfloat16)
    back_hidden = conv_back(padded[:, in_channels:], conv_second, tile_cols + 2, span + 2)
    back_pre = jnp.where(inside, back_hidden * silu_slope(pre_act), 0.0).astype(jnp.bfloat16)
    back_maps = conv_back(back_pre, conv_first[:, :, :, :2], tile_cols, span).astype(jnp.bfloat16)
    from_below = from_behind(back_maps, "strip", -1)
    both_halves = jnp.stack([back_maps, from_below], axis=1).reshape(tile_cols, 4 * span)
    left_col = net_box[:, 0]
    right_col = net_box[:, 1]
    shard_piece = lax.all_gather(both_halves, "col", axis=0, tiled=True)
    piece_cols = jnp.arange(shard_piece.shape[0], dtype=jnp.int32)
    net_cols = (
        (left_col[:, None] <= piece_cols[None, :]) & (piece_cols[None, :] <= right_col[:, None])
    ).astype(jnp.bfloat16)
    column_sums = jnp.dot(net_cols, shard_piece, preferred_element_type=jnp.float32)
    column_sums = column_sums.reshape(net_total, 2, 2, span)
    net_rows = first_row + jnp.arange(2 * span, dtype=jnp.int32)
    in_rows = (
        (
            (net_box[:, 2][:, None] <= net_rows[None, :])
            & (net_rows[None, :] <= net_box[:, 3][:, None])
        )
        .astype(jnp.float32)
        .reshape(net_total, 2, span)
    )
    box_height = (net_box[:, 3] - net_box[:, 2] + 1).astype(jnp.float32)
    box_width = (right_col - left_col + 1).astype(jnp.float32)
    per_row = (
        column_sums[:, :, 0] / box_height[:, None, None]
        + column_sums[:, :, 1] / box_width[:, None, None]
    )
    net_grad = jnp.sum(in_rows * per_row, axis=(1, 2))
    return (congestion, net_grad)


def solution(mesh):
    placed = (
        P(("strip", "col"), None),
        P(("strip", "col")),
        P(("strip", "col"), None, None),
        P(),
        P(),
        P(),
        P(),
        P("col", None, "strip"),
    )
    return jax.shard_map(
        shards,
        mesh=mesh,
        in_specs=placed,
        out_specs=(P("col", None, "strip"), P(("strip", "col"))),
        check_vma=False,
    )
```

profile of v0, /device:TPU:16, one launch (start us, length us, event | category | flops | bytes accessed | tf_op | source)
XLA Modules:
  0.0 179.4 jit_solution(665664036078959381)
XLA Ops:
  2.9 5.8 %all_gather.6 = f32[4096,13]{0,1:T(8,128)S(1)} all-gather(f32[1024,13]{0,1:T(8,128)S(1)} %pad_maximum_fusion.10), channel_id=1, replica_groups=mesh['strip'=8,'col'=4] {'col'}, dimensions={0}, use_global_device_ids=true | all-gather | bytes 266240 | tf_op jit(solution)/shard_map/all_gather | solution.py:113
  8.8 13.7 %while.11 = (s32[]{:T(128)}, f32[128,2,3,128]{3,0,2,1:T(8,128)S(1)}, f32[4,1024,13]{1,0,2:T(4,128)S(1)}, s32[]{:T(128)}, s32[]{:T(128)}, /*index=5*/s32[]{:T(128)}, s32[]{:T(128)}) while((s32[]{:T(128)}, f32[128,2,3,128]{3,0,2,1:T(8,128)S(1)}, f32[4,1024,13]{1,0,2:T(4,128)S(1)}, s32[]{:T(128)}, s32[]{:T(128)}, ...), condition=%wide.region_1.2_spmd.clone, body=%wide.region_0.1_spmd.clone.sunk | while | flops 408091520 | bytes 3318379 | solution.py:135
  22.8 3.4 %collective-permute-start = (bf16[128,3,128]{0,2,1:T(8,128)(2,1)S(1)}, bf16[128,3,128]{0,2,1:T(8,128)(2,1)S(1)}, u32[]{:S(2)}, u32[]{:S(2)}) collective-permute-start(bf16[128,3,128]{0,2,1:T(8,128)(2,1)S(1)} %fusion.144), channel_id=1, source_target_pairs={{0,4},{4,8},{8,12},{12,16},{16,20},{20,24},{24,28},{1,5},{5,9},{9,... | collective-permute-start | bytes 294920 | tf_op jit(solution)/shard_map/ppermute | solution.py:12
  27.3 3.3 %collective-permute-done = bf16[128,3,128]{0,2,1:T(8,128)(2,1)S(1)} collective-permute-done((bf16[128,3,128]{0,2,1:T(8,128)(2,1)S(1)}, bf16[128,3,128]{0,2,1:T(8,128)(2,1)S(1)}, u32[]{:S(2)}, u32[]{:S(2)}) %collective-permute-start) | collective-permute-done | bytes 98336 | tf_op jit(solution)/shard_map/ppermute | solution.py:12
  30.7 2.4 %collective-permute-start.2 = (bf16[128,35,2]{0,2,1:T(2,128)(2,1)S(1)}, bf16[128,35,2]{0,2,1:T(2,128)(2,1)S(1)}, u32[]{:S(2)}, u32[]{:S(2)}) collective-permute-start(bf16[128,35,2]{0,2,1:T(2,128)(2,1)S(1)} %get-tuple-element.87), channel_id=1, source_target_pairs={{4,0},{8,4},{12,8},{16,12},{20,16},{24,20},{28,24},{5,1},{9,5},{13... | collective-permute-start | bytes 53768 | tf_op jit(solution)/shard_map/ppermute | solution.py:23
  33.1 3.5 %collective-permute-start.1 = (bf16[128,35,2]{0,2,1:T(2,128)(2,1)S(1)}, bf16[128,35,2]{0,2,1:T(2,128)(2,1)S(1)}, u32[]{:S(2)}, u32[]{:S(2)}) collective-permute-start(bf16[128,35,2]{0,2,1:T(2,128)(2,1)S(1)} %get-tuple-element.86), channel_id=1, source_target_pairs={{0,4},{4,8},{8,12},{12,16},{16,20},{20,24},{24,28},{1,5},{5,9},{9,... | collective-permute-start | bytes 53768 | tf_op jit(solution)/shard_map/ppermute | solution.py:20
  36.6 3.0 %collective-permute-done.1 = bf16[128,35,2]{0,2,1:T(2,128)(2,1)S(1)} collective-permute-done((bf16[128,35,2]{0,2,1:T(2,128)(2,1)S(1)}, bf16[128,35,2]{0,2,1:T(2,128)(2,1)S(1)}, u32[]{:S(2)}, u32[]{:S(2)}) %collective-permute-start.1) | collective-permute-done | bytes 17952 | tf_op jit(solution)/shard_map/ppermute | solution.py:20
  41.2 3.6 %copy.58 = bf16[128,35,132]{2,1,0:T(8,128)(2,1)S(1)} copy(bf16[128,35,132]{0,2,1:T(8,128)(2,1)} %pad_maximum_fusion.8) | data formatting | bytes 2365440 | tf_op jit(solution)/shard_map/concatenate | solution.py:24
  47.7 2.7 %fusion.110 = f32[130,130,32]{1,2,0:T(8,128)} fusion(bf16[128,35,132]{2,1,0:T(8,128)(2,1)S(1)} %copy.58, bf16[2,35,132]{2,1,0:T(8,128)(2,1)S(1)} %collective-permute-done.3, bf16[3,3,32,3]{2,3,1,0:T(4,128)(2,1)S(1)} %copy-done.10), kind=kOutput, calls=%fused_computation.139 | convolution fusion | flops 3447600 | bytes 4826624 | tf_op jit(solution)/shard_map/oi,xiy->xoy/dot_general | solution.py:38
  51.0 2.9 %fusion.104 = f32[130,130,32]{1,2,0:T(8,128)} fusion(bf16[2,35,132]{2,1,0:T(8,128)(2,1)S(1)} %collective-permute-done.4, bf16[128,35,132]{2,1,0:T(8,128)(2,1)S(1)} %copy.58, bf16[2,35,132]{2,1,0:T(8,128)(2,1)S(1)} %collective-permute-done.3, bf16[3,3,32,3]{2,3,1,0:T(4,128)(2,1)S(1)} %copy-done.10), kind=kOutput, calls=%fused_computation.133 | convolution fusion | flops 3549000 | bytes 4867584 | tf_op jit(solution)/shard_map/oi,xiy->xoy/dot_general | solution.py:38
  53.9 2.8 %fusion.114 = f32[130,130,32]{1,2,0:T(8,128)} fusion(bf16[2,35,132]{2,1,0:T(8,128)(2,1)S(1)} %collective-permute-done.4, bf16[128,35,132]{2,1,0:T(8,128)(2,1)S(1)} %copy.58, bf16[3,3,32,3]{2,3,1,0:T(4,128)(2,1)S(1)} %copy-done.10), kind=kOutput, calls=%fused_computation.143 | convolution fusion | flops 3447600 | bytes 4826624 | tf_op jit(solution)/shard_map/oi,xiy->xoy/dot_general | solution.py:38
  56.7 2.8 %fusion.118 = f32[130,130,32]{1,2,0:T(8,128)} fusion(bf16[2,35,132]{2,1,0:T(8,128)(2,1)S(1)} %collective-permute-done.4, bf16[128,35,132]{2,1,0:T(8,128)(2,1)S(1)} %copy.58, bf16[2,35,132]{2,1,0:T(8,128)(2,1)S(1)} %collective-permute-done.3, bf16[3,3,32,3]{2,3,1,0:T(4,128)(2,1)S(1)} %copy-done.10), kind=kOutput, calls=%fused_computation.147 | convolution fusion | flops 3549000 | bytes 4867584 | tf_op jit(solution)/shard_map/oi,xiy->xoy/dot_general | solution.py:38
  59.5 2.7 %fusion.124 = f32[130,130,32]{1,2,0:T(8,128)} fusion(bf16[128,35,132]{2,1,0:T(8,128)(2,1)S(1)} %copy.58, bf16[2,35,132]{2,1,0:T(8,128)(2,1)S(1)} %collective-permute-done.3, bf16[3,3,32,3]{2,3,1,0:T(4,128)(2,1)S(1)} %copy-done.10), kind=kOutput, calls=%fused_computation.153 | convolution fusion | flops 3447600 | bytes 4826624 | tf_op jit(solution)/shard_map/oi,xiy->xoy/dot_general | solution.py:38
  62.2 2.7 %fusion.128 = f32[130,130,32]{1,2,0:T(8,128)} fusion(bf16[2,35,132]{2,1,0:T(8,128)(2,1)S(1)} %collective-permute-done.4, bf16[128,35,132]{2,1,0:T(8,128)(2,1)S(1)} %copy.58, bf16[3,3,32,3]{2,3,1,0:T(4,128)(2,1)S(1)} %copy-done.10), kind=kOutput, calls=%fused_computation.157 | convolution fusion | flops 3447600 | bytes 4826624 | tf_op jit(solution)/shard_map/oi,xiy->xoy/dot_general | solution.py:38
  65.0 2.8 %fusion.138 = f32[130,130,32]{1,2,0:T(8,128)} fusion(bf16[128,35,132]{2,1,0:T(8,128)(2,1)S(1)} %copy.58, bf16[2,35,132]{2,1,0:T(8,128)(2,1)S(1)} %collective-permute-done.3, bf16[3,3,32,3]{2,3,1,0:T(4,128)(2,1)S(1)} %copy-done.10), kind=kOutput, calls=%fused_computation.167 | convolution fusion | flops 3447600 | bytes 4826624 | tf_op jit(solution)/shard_map/oi,xiy->xoy/dot_general | solution.py:38
  67.8 2.8 %fusion.132 = f32[130,130,32]{1,2,0:T(8,128)} fusion(bf16[2,35,132]{2,1,0:T(8,128)(2,1)S(1)} %collective-permute-done.4, bf16[128,35,132]{2,1,0:T(8,128)(2,1)S(1)} %copy.58, bf16[2,35,132]{2,1,0:T(8,128)(2,1)S(1)} %collective-permute-done.3, bf16[3,3,32,3]{2,3,1,0:T(4,128)(2,1)S(1)} %copy-done.10), kind=kOutput, calls=%fused_computation.161 | convolution fusion | flops 3549000 | bytes 4867584 | tf_op jit(solution)/shard_map/oi,xiy->xoy/dot_general | solution.py:38
  70.6 14.8 %fusion.34 = (bf16[130,32,130]{2,1,0:T(8,128)(2,1)S(1)}, f32[130,130,32]{1,2,0:T(8,128)}) fusion(pred[130,130]{1,0:T(8,128)(4,1)S(1)} %broadcast_and_fusion, f32[32]{0:T(128)S(1)} %copy-done.12, bf16[3,3,32,3]{2,3,1,0:T(4,128)(2,1)S(1)} %copy-done.10, bf16[2,35,132]{2,1,0:T(8,128)(2,1)S(1)} %collective-permute-done.4, bf16[128,35,132]{2,1,0:T(8,128)(2,1)S(1)} %copy.58, ...), kind=kOutput, calls=%fused_computation.44 | convolution fusion | flops 11559600 | bytes 23249152 | tf_op jit(solution)/shard_map/oi,xiy->xoy/dot_general | solution.py:38
  100.6 2.7 %fusion.51 = f32[130,130,32]{1,2,0:T(8,128)} fusion(bf16[132,35,132]{2,1,0:T(8,128)(2,1)S(1)} %pad_maximum_fusion.1, bf16[3,3,32,32]{3,2,1,0:T(8,128)(2,1)S(1)} %copy-done.8), kind=kOutput, calls=%fused_computation.68 | convolution fusion | flops 34611200 | bytes 4301312 | tf_op jit(solution)/shard_map/oi,xoy->xiy/dot_general | solution.py:57
  103.3 3.1 %fusion.55 = f32[130,130,32]{1,2,0:T(8,128)} fusion(bf16[132,35,132]{2,1,0:T(8,128)(2,1)S(1)} %pad_maximum_fusion.1, bf16[3,3,32,32]{3,2,1,0:T(8,128)(2,1)S(1)} %copy-done.8), kind=kOutput, calls=%fused_computation.73 | convolution fusion | flops 34611200 | bytes 4301312 | tf_op jit(solution)/shard_map/oi,xoy->xiy/dot_general | solution.py:57
  106.5 3.2 %fusion.57 = f32[130,130,32]{1,2,0:T(8,128)} fusion(bf16[132,35,132]{2,1,0:T(8,128)(2,1)S(1)} %pad_maximum_fusion.1, bf16[3,3,32,32]{3,2,1,0:T(8,128)(2,1)S(1)} %copy-done.8), kind=kOutput, calls=%fused_computation.75 | convolution fusion | flops 34611200 | bytes 4301312 | tf_op jit(solution)/shard_map/oi,xoy->xiy/dot_general | solution.py:57
  109.6 2.8 %fusion.53 = f32[130,130,32]{1,2,0:T(8,128)} fusion(bf16[2,35,132]{2,1,0:T(8,128)(2,1)S(1)} %collective-permute-done.4, bf16[128,35,132]{2,1,0:T(8,128)(2,1)S(1)} %copy.58, bf16[3,3,32,32]{3,2,1,0:T(8,128)(2,1)S(1)} %copy-done.8), kind=kOutput, calls=%fused_computation.71 | convolution fusion | flops 36774400 | bytes 4833792 | tf_op jit(solution)/shard_map/oi,xoy->xiy/dot_general | solution.py:57
  112.5 3.6 %fusion.44 = f32[130,130,32]{1,2,0:T(8,128)} fusion(bf16[128,35,132]{2,1,0:T(8,128)(2,1)S(1)} %copy.58, bf16[2,35,132]{2,1,0:T(8,128)(2,1)S(1)} %collective-permute-done.3, bf16[3,3,32,32]{3,2,1,0:T(8,128)(2,1)S(1)} %copy-done.8), kind=kOutput, calls=%fused_computation.62 | convolution fusion | flops 35152000 | bytes 4833792 | tf_op jit(solution)/shard_map/oi,xoy->xiy/dot_general | solution.py:57
  116.1 3.6 %fusion.38 = f32[130,130,32]{1,2,0:T(8,128)} fusion(bf16[128,35,132]{2,1,0:T(8,128)(2,1)S(1)} %copy.58, bf16[2,35,132]{2,1,0:T(8,128)(2,1)S(1)} %collective-permute-done.4, bf16[3,3,32,32]{3,2,1,0:T(8,128)(2,1)S(1)} %copy-done.8), kind=kOutput, calls=%fused_computation.58 | convolution fusion | flops 35152000 | bytes 4833792 | tf_op jit(solution)/shard_map/oi,xoy->xiy/dot_general | solution.py:57
  119.7 3.9 %fusion.47 = f32[130,130,32]{1,2,0:T(8,128)} fusion(bf16[128,35,132]{2,1,0:T(8,128)(2,1)S(1)} %copy.58, bf16[2,35,132]{2,1,0:T(8,128)(2,1)S(1)} %collective-permute-done.3, bf16[3,3,32,32]{3,2,1,0:T(8,128)(2,1)S(1)} %copy-done.8), kind=kOutput, calls=%fused_computation.64 | convolution fusion | flops 35152000 | bytes 4833792 | tf_op jit(solution)/shard_map/oi,xoy->xiy/dot_general | solution.py:57
  123.6 3.7 %fusion.41 = f32[130,130,32]{1,2,0:T(8,128)} fusion(bf16[128,35,132]{2,1,0:T(8,128)(2,1)S(1)} %copy.58, bf16[2,35,132]{2,1,0:T(8,128)(2,1)S(1)} %collective-permute-done.4, bf16[3,3,32,32]{3,2,1,0:T(8,128)(2,1)S(1)} %copy-done.8), kind=kOutput, calls=%fused_computation.60 | convolution fusion | flops 35152000 | bytes 4833792 | tf_op jit(solution)/shard_map/oi,xoy->xiy/dot_general | solution.py:57
  127.3 15.3 %fusion.29 = bf16[130,32,130]{2,1,0:T(8,128)(2,1)} fusion(f32[130,130,32]{1,2,0:T(8,128)} %get-tuple-element.93, f32[130,130,32]{1,2,0:T(8,128)} %fusion.51, f32[130,130,32]{1,2,0:T(8,128)} %fusion.53, f32[130,130,32]{1,2,0:T(8,128)} %fusion.44, f32[130,130,32]{1,2,0:T(8,128)} %fusion.55, f32[130,130,32]{1,2,0:T(8,128)} %fusion.38, ...), kind=kOutput, calls=%fused_computation.36 | convolution fusion | flops 46508800 | bytes 23255808 | tf_op jit(solution)/shard_map/oi,xoy->xiy/dot_general | solution.py:57
  144.8 2.2 %convolution_add_fusion.7 = f32[128,128,2]{1,2,0:T(2,128)S(1)} fusion(f32[128,128,2]{1,2,0:T(2,128)S(1)} %fusion.76, bf16[130,32,130]{2,1,0:T(8,128)(2,1)} %fusion.29, bf16[3,3,32,3]{2,3,1,0:T(4,128)(2,1)S(1)} %copy-done.10), kind=kOutput, calls=%fused_computation.91 | convolution fusion | flops 2129920 | bytes 1311232 | tf_op jit(solution)/shard_map/oi,xoy->xiy/dot_general | solution.py:57
  151.3 2.2 %convolution_add_fusion.4 = f32[128,128,2]{1,2,0:T(2,128)S(1)} fusion(f32[128,128,2]{1,2,0:T(2,128)S(1)} %convolution_add_fusion.5, bf16[130,32,130]{2,1,0:T(8,128)(2,1)} %fusion.29, bf16[3,3,32,3]{2,3,1,0:T(4,128)(2,1)S(1)} %copy-done.10), kind=kOutput, calls=%fused_computation.88 | convolution fusion | flops 2129920 | bytes 1311232 | tf_op jit(solution)/shard_map/oi,xoy->xiy/dot_general | solution.py:57
  153.6 2.2 %convolution_add_fusion.3 = f32[128,128,2]{1,2,0:T(2,128)S(1)} fusion(f32[128,128,2]{1,2,0:T(2,128)S(1)} %convolution_add_fusion.4, bf16[130,32,130]{2,1,0:T(8,128)(2,1)} %fusion.29, bf16[3,3,32,3]{2,3,1,0:T(4,128)(2,1)S(1)} %copy-done.10), kind=kOutput, calls=%fused_computation.87 | convolution fusion | flops 2129920 | bytes 1311232 | tf_op jit(solution)/shard_map/oi,xoy->xiy/dot_general | solution.py:57
  160.3 2.4 %collective-permute-start.5 = (bf16[128,2,128]{2,1,0:T(2,128)(2,1)S(1)}, bf16[128,2,128]{2,1,0:T(2,128)(2,1)S(1)}, u32[]{:S(2)}, u32[]{:S(2)}) collective-permute-start(bf16[128,2,128]{2,1,0:T(2,128)(2,1)S(1)} %bitcast.290), channel_id=1, source_target_pairs={{4,0},{8,4},{12,8},{16,12},{20,16},{24,20},{28,24},{5,1},{9,5},{13... | collective-permute-start | bytes 196616 | tf_op jit(solution)/shard_map/ppermute | solution.py:12
  162.8 4.2 %fusion.62 = bf16[128,32,128]{2,1,0:T(8,128)(2,1)} fusion(f32[128,128,32]{1,2,0:T(8,128)S(1)} %copy-done, f32[128,128,32]{1,2,0:T(8,128)S(1)} %copy-done.1, f32[128,128,32]{1,2,0:T(8,128)S(1)} %copy-done.2, f32[128,128,32]{1,2,0:T(8,128)S(1)} %copy-done.3, f32[128,128,32]{1,2,0:T(8,128)S(1)} %copy-done.4, f32[128,128,32]{1,2,0:T(8,128)S(1)} %copy-done.5, ...), kind=kOutput, calls=%fused_computation.82 | convolution fusion | flops 38797312 | bytes 18883072 | tf_op jit(solution)/shard_map/oi,xiy->xoy/dot_general | solution.py:38
  167.3 9.6 %all_gather.7 = bf16[512,512]{0,1:T(8,128)(2,1)S(1)} all-gather(bf16[128,512]{0,1:T(8,128)(2,1)S(1)} %bitcast.285), channel_id=1, replica_groups=mesh['strip'=8,'col'=4] {'col'}, dimensions={0}, use_global_device_ids=true | all-gather | bytes 655360 | tf_op jit(solution)/shard_map/all_gather | solution.py:161
  (145 shorter events, 50.6 us)
Async XLA Ops:
  8.8 17.5 %copy-start.9 = (s32[1024,4]{0,1:T(4,128)S(1)}, s32[1024,4]{0,1:T(4,128)}, u32[]{:S(2)}) copy-start(s32[1024,4]{0,1:T(4,128)} %param.10) | copy-start | bytes 49156
  8.8 17.5 %copy-start.7 = (bf16[128,32,128]{2,1,0:T(8,128)(2,1)S(1)}, bf16[128,32,128]{2,1,0:T(8,128)(2,1)}, u32[]{:S(2)}) copy-start(bf16[128,32,128]{2,1,0:T(8,128)(2,1)} %param.17) | copy-start | bytes 3145732
  22.8 7.8 %collective-permute-start = (bf16[128,3,128]{0,2,1:T(8,128)(2,1)S(1)}, bf16[128,3,128]{0,2,1:T(8,128)(2,1)S(1)}, u32[]{:S(2)}, u32[]{:S(2)}) collective-permute-start(bf16[128,3,128]{0,2,1:T(8,128)(2,1)S(1)} %fusion.144), channel_id=1, source_target_pairs={{0,4},{4,8},{8,12},{12,16},{16,20},{20,24},{24,28},{1,5},{5,9},{9,... | collective-permute-start | bytes 294920 | tf_op jit(solution)/shard_map/ppermute | solution.py:12
  30.7 5.9 %collective-permute-start.2 = (bf16[128,35,2]{0,2,1:T(2,128)(2,1)S(1)}, bf16[128,35,2]{0,2,1:T(2,128)(2,1)S(1)}, u32[]{:S(2)}, u32[]{:S(2)}) collective-permute-start(bf16[128,35,2]{0,2,1:T(2,128)(2,1)S(1)} %get-tuple-element.87), channel_id=1, source_target_pairs={{4,0},{8,4},{12,8},{16,12},{20,16},{24,20},{28,24},{5,1},{9,5},{13... | collective-permute-start | bytes 53768 | tf_op jit(solution)/shard_map/ppermute | solution.py:23
  33.1 6.5 %collective-permute-start.1 = (bf16[128,35,2]{0,2,1:T(2,128)(2,1)S(1)}, bf16[128,35,2]{0,2,1:T(2,128)(2,1)S(1)}, u32[]{:S(2)}, u32[]{:S(2)}) collective-permute-start(bf16[128,35,2]{0,2,1:T(2,128)(2,1)S(1)} %get-tuple-element.86), channel_id=1, source_target_pairs={{0,4},{4,8},{8,12},{12,16},{16,20},{20,24},{24,28},{1,5},{5,9},{9,... | collective-permute-start | bytes 53768 | tf_op jit(solution)/shard_map/ppermute | solution.py:20
  36.6 11.1 %copy-start.10 = (bf16[3,3,32,3]{2,3,1,0:T(4,128)(2,1)S(1)}, bf16[3,3,32,3]{2,3,1,0:T(4,128)(2,1)}, u32[]{:S(2)}) copy-start(bf16[3,3,32,3]{2,3,1,0:T(4,128)(2,1)} %param.13) | copy-start | bytes 5188
  44.9 2.8 %collective-permute-start.3 = (bf16[2,35,132]{2,1,0:T(8,128)(2,1)S(1)}, bf16[2,35,132]{2,1,0:T(8,128)(2,1)S(1)}, u32[]{:S(2)}, u32[]{:S(2)}) collective-permute-start(bf16[2,35,132]{2,1,0:T(8,128)(2,1)S(1)} %get-tuple-element.84), channel_id=1, source_target_pairs={{0,1},{1,2},{2,3},{4,5},{5,6},{6,7},{8,9},{9,10},{10,11},{12,13},{... | collective-permute-start | bytes 55448 | tf_op jit(solution)/shard_map/ppermute | solution.py:20
  46.2 4.9 %collective-permute-start.4 = (bf16[2,35,132]{2,1,0:T(8,128)(2,1)S(1)}, bf16[2,35,132]{2,1,0:T(8,128)(2,1)S(1)}, u32[]{:S(2)}, u32[]{:S(2)}) collective-permute-start(bf16[2,35,132]{2,1,0:T(8,128)(2,1)S(1)} %get-tuple-element.85), channel_id=1, source_target_pairs={{1,0},{2,1},{3,2},{5,4},{6,5},{7,6},{9,8},{10,9},{11,10},{13,12},{... | collective-permute-start | bytes 55448 | tf_op jit(solution)/shard_map/ppermute | solution.py:23
  67.8 2.8 %copy-start.12 = (f32[32]{0:T(128)S(1)}, f32[32]{0:T(128)}, u32[]{:S(2)}) copy-start(f32[32]{0:T(128)} %param.14) | copy-start | bytes 388
  70.6 14.8 %copy-start.8 = (bf16[3,3,32,32]{3,2,1,0:T(8,128)(2,1)S(1)}, bf16[3,3,32,32]{3,2,1,0:T(8,128)(2,1)}, u32[]{:S(2)}) copy-start(bf16[3,3,32,32]{3,2,1,0:T(8,128)(2,1)} %param.15) | copy-start | bytes 55300
  127.3 35.4 %copy-start.5 = (f32[128,128,32]{1,2,0:T(8,128)S(1)}, f32[128,128,32]{1,2,0:T(8,128)}, u32[]{:S(2)}) copy-start(f32[128,128,32]{1,2,0:T(8,128)} %fusion.89) | copy-start | bytes 6291460
  127.3 35.4 %copy-start.6 = (f32[128,128,32]{1,2,0:T(8,128)S(1)}, f32[128,128,32]{1,2,0:T(8,128)}, u32[]{:S(2)}) copy-start(f32[128,128,32]{1,2,0:T(8,128)} %fusion.93) | copy-start | bytes 6291460
  144.8 18.0 %copy-start.4 = (f32[128,128,32]{1,2,0:T(8,128)S(1)}, f32[128,128,32]{1,2,0:T(8,128)}, u32[]{:S(2)}) copy-start(f32[128,128,32]{1,2,0:T(8,128)} %fusion.87) | copy-start | bytes 6291460
  147.0 15.8 %copy-start.3 = (f32[128,128,32]{1,2,0:T(8,128)S(1)}, f32[128,128,32]{1,2,0:T(8,128)}, u32[]{:S(2)}) copy-start(f32[128,128,32]{1,2,0:T(8,128)} %fusion.85) | copy-start | bytes 6291460
  151.3 11.4 %copy-start.2 = (f32[128,128,32]{1,2,0:T(8,128)S(1)}, f32[128,128,32]{1,2,0:T(8,128)}, u32[]{:S(2)}) copy-start(f32[128,128,32]{1,2,0:T(8,128)} %fusion.83) | copy-start | bytes 6291460
  153.6 9.2 %copy-start = (f32[128,128,32]{1,2,0:T(8,128)S(1)}, f32[128,128,32]{1,2,0:T(8,128)}, u32[]{:S(2)}) copy-start(f32[128,128,32]{1,2,0:T(8,128)} %fusion.79) | copy-start | bytes 6291460
  153.6 9.2 %copy-start.1 = (f32[128,128,32]{1,2,0:T(8,128)S(1)}, f32[128,128,32]{1,2,0:T(8,128)}, u32[]{:S(2)}) copy-start(f32[128,128,32]{1,2,0:T(8,128)} %fusion.81) | copy-start | bytes 6291460
  153.6 9.2 %copy-start.11 = (f32[32]{0:T(128)S(1)}, f32[32]{0:T(128)}, u32[]{:S(2)}) copy-start(f32[32]{0:T(128)} %param.16) | copy-start | bytes 388
  160.3 6.7 %collective-permute-start.5 = (bf16[128,2,128]{2,1,0:T(2,128)(2,1)S(1)}, bf16[128,2,128]{2,1,0:T(2,128)(2,1)S(1)}, u32[]{:S(2)}, u32[]{:S(2)}) collective-permute-start(bf16[128,2,128]{2,1,0:T(2,128)(2,1)S(1)} %bitcast.290), channel_id=1, source_target_pairs={{4,0},{8,4},{12,8},{16,12},{20,16},{24,20},{28,24},{5,1},{9,5},{13... | collective-permute-start | bytes 196616 | tf_op jit(solution)/shard_map/ppermute | solution.py:12
where the time goes:
time: 181 us; the launch traced here: 179 us
  matrix products  124 us (69%)
  blocking collectives  15.4 us (9%)
  starting transfers between devices  14.4 us (8%)
  local copies, waits for them, and re-layouts  9.63 us (5%)
  other arithmetic  7.78 us (4%)
  waiting for transfers between devices  6.95 us (4%)
    dot_general x18, matrix products, conv_back(): jnp.einsum('oi,xoy->xiy', weights[shift_row, shift_col], window, preferre...  59.7 us
    dot_general x18, matrix products, conv_valid(): jnp.einsum('oi,xiy->xoy', weights[shift_row, shift_col], window, preferre...  55.9 us
    all_gather x1, blocking collectives, shards(): shard_piece = lax.all_gather(both_halves, 'col', axis=0, tiled=True)  9.57 us
    ppermute x2, starting transfers between devices, from_behind(): return lax.ppermute(x, axis, pairs)  5.84 us
    all_gather x1, blocking collectives, shards(): shard_piece = lax.all_gather(packed, 'col', axis=0, tiled=True)  5.79 us
    ppermute x2, starting transfers between devices, with_halo(): lax.ppermute(lax.slice_in_dim(block, block.shape[dim] - width, None, axis...  4.75 us
    dot_general x4, matrix products, column_block(): jnp.einsum('pk,phr->khr', pin_cols, pin_factor, preferred_element_type=jn...  4.31 us
    ppermute x2, starting transfers between devices, with_halo(): lax.ppermute(lax.slice_in_dim(block, 0, width, axis=dim), axis, backward)  3.86 us
  transfers between devices with their start and end apart: 6, of which 3 were waited for; matrix products, arithmetic and copies ran while one was open for 4% of the time, Pallas kernels for 0%

commit v1 on v0

v1 whole, which is shorter than its diff:
```python
import functools

import jax
import jax.numpy as jnp
from jax import lax
from jax.experimental import pallas as pl
from jax.experimental.pallas import tpu as pltpu
from jax.sharding import PartitionSpec as P

F32 = jnp.float32
BF16 = jnp.bfloat16
BOX = 16
REACH = BOX + 1
LANES = 256
NROWS = 144
JCOLS = 144
FIELDS = 16
GROUP = 6
WINDOW = 8
EDGE = 24
VMEM = 56 * 1024 * 1024

NN = (((1,), (0,)), ((), ()))
NT = (((1,), (1,)), ((), ()))
TN = (((0,), (0,)), ((), ()))


def dot(a, b, dims=NN):
    return lax.dot_general(a, b, dims, preferred_element_type=F32)


def iota(shape, dim):
    return lax.broadcasted_iota(jnp.int32, shape, dim)


def onehot(pred):
    return jnp.where(pred, 1.0, 0.0).astype(BF16)


def call(body, out, n_in, scratch=(), cost=None, in_specs=None):
    whole = pl.BlockSpec(memory_space=pltpu.VMEM)
    outs = jax.tree.map(lambda x: whole, out)
    return pl.pallas_call(
        body,
        out_shape=out,
        in_specs=in_specs or [whole] * n_in,
        out_specs=outs,
        scratch_shapes=list(scratch),
        compiler_params=pltpu.CompilerParams(vmem_limit_bytes=VMEM),
        cost_estimate=cost,
    )


def cost(flops, nbytes):
    return pl.CostEstimate(flops=flops, bytes_accessed=nbytes, transcendentals=0)


def pack_body(pins, box, weight, pin, first, last, to_right, to_left, plain):
    rows = [box[...].astype(F32), weight[...]]
    rows += [pin[p].astype(F32) for p in range(pins)]
    nets = box.shape[1]
    used = 5 + 2 * pins
    rows.append(jnp.zeros((FIELDS - used, nets), F32))
    fields = jnp.concatenate(rows, axis=0)
    plain[...] = fields
    to_right[0:FIELDS, :] = fields
    to_left[0:FIELDS, :] = fields
    for ref, edge in ((to_right, last), (to_left, first)):
        e = edge[...].astype(F32)
        for k in range(8):
            ref[FIELDS : FIELDS + 8, 128 * k : 128 * (k + 1)] = e[8 * k : 8 * k + 8, :]


def cot_edge_body(cot, up, down):
    span = cot.shape[1]
    m = iota((32, span), 0)
    lane = iota((32, span), 1)
    sel = onehot(((m < REACH) & (lane == m)) | ((m >= EDGE) & (lane == span - 2 + m - EDGE)))
    step = 512
    for k in range(cot.shape[0] // step):
        got = dot(sel, cot[step * k : step * (k + 1), :], NT).astype(BF16)
        up[:, step * k : step * (k + 1)] = got[:EDGE]
        down[:, step * k : step * (k + 1)] = got[EDGE:]


def weight_body(second, first, fwd, bwd, first_fwd, first_bwd):
    chans = second.shape[1]
    tile = onehot(iota((chans, WINDOW * chans), 1) % chans == iota((chans, WINDOW * chans), 0))
    lane_t = iota((chans, WINDOW * chans), 1) // chans
    cin = first.shape[1]
    ftile = onehot(iota((cin, cin * 16), 1) // 16 == iota((cin, cin * 16), 0))
    ft = iota((chans, cin * 16), 1) % 16
    row8 = iota((8, WINDOW * chans), 0)
    lane8 = iota((8, WINDOW * chans), 1) // chans
    for r in range(3):
        taps = [dot(second[3 * r + c], tile) for c in range(3)]
        flipped = [dot(second[3 * r + c], tile, TN) for c in range(3)]
        for jo in range(GROUP):
            lo = (r * GROUP + jo) * chans
            acc = jnp.zeros((chans, WINDOW * chans), F32)
            acc2 = acc
            for c in range(3):
                acc = jnp.where(lane_t == jo + c, taps[c], acc)
                acc2 = jnp.where(lane_t == jo + 2 - c, flipped[c], acc2)
            fwd[lo : lo + chans, :] = acc.astype(BF16)
            bwd[lo : lo + chans, :] = acc2.astype(BF16)
        ftaps = [dot(first[3 * r + c], ftile, TN) for c in range(3)]
        parts = []
        for jo in range(8):
            acc = jnp.zeros((chans, cin * 16), F32)
            for c in range(3):
                acc = jnp.where(ft == jo + c, ftaps[c], acc)
            parts.append(acc)
        first_fwd[r] = jnp.concatenate(parts, axis=0).astype(BF16)
        fback = [dot(first[3 * r + c], tile) for c in range(3)]
        for ch in range(2):
            acc = jnp.zeros((8, WINDOW * chans), F32)
            for c in range(3):
                row = jnp.broadcast_to(fback[c][ch : ch + 1, :], acc.shape)
                acc = jnp.where((lane8 == row8 + 2 - c) & (row8 < GROUP), row, acc)
            first_bwd[16 * r + 8 * ch : 16 * r + 8 * ch + 8, :] = acc


def relative(ref, m, col0, row0):
    f = ref[m, 0:FIELDS, :]
    x = lambda v: jnp.clip(v - (col0 - 2.0), -2.0, 250.0)
    y = lambda v: jnp.clip(v - row0, -2.0, 250.0)
    return f, x, y


def raster_body(pins, n_nets, *refs):
    pos = refs[0]
    net_refs = refs[1 : 1 + n_nets]
    left_ref, right_ref, maps, up, down = refs[1 + n_nets :]
    col0 = pos[0].astype(F32)
    row0 = pos[1].astype(F32)
    maps[...] = jnp.zeros_like(maps)
    nets = net_refs[0].shape[2]
    step = nets
    jcol = iota((JCOLS, step), 0).astype(F32).astype(BF16)
    one = jnp.ones((), BF16)
    zero = jnp.zeros((), BF16)

    def chunk(ref, m):
        f, x, y = relative(ref, m, col0, row0)
        x0, x1 = x(f[0:1]).astype(BF16), x(f[1:2]).astype(BF16)
        y0, y1 = y(f[2:3]).astype(BF16), y(f[3:4]).astype(BF16)
        vh = (f[4:5] / (f[3:4] - f[2:3] + 1.0)).astype(BF16)
        vv = (f[4:5] / (f[1:2] - f[0:1] + 1.0)).astype(BF16)
        in_col = (x0 <= jcol) & (jcol <= x1)
        in_row = jnp.where((y0 <= jcol) & (jcol <= y1), one, zero)
        maps[0, :, 0:NROWS] += dot(jnp.where(in_col, vh, zero), in_row, NT)
        maps[1, :, 0:NROWS] += dot(jnp.where(in_col, vv, zero), in_row, NT)
        acc = jnp.zeros((JCOLS, NROWS), F32)
        for p in range(pins):
            py = y(f[5 + 2 * p : 6 + 2 * p]).astype(BF16)
            px = x(f[6 + 2 * p : 7 + 2 * p]).astype(BF16)
            acc += dot(
                jnp.where(px == jcol, one, zero), jnp.where(py == jcol, one, zero), NT
            )
        maps[2, :, 0:NROWS] += acc

    for ref in net_refs:
        if ref.shape[0] == 1:
            chunk(ref, 0)
        else:
            lax.fori_loop(0, ref.shape[0], lambda m, c: (chunk(ref, m), c)[1], 0)
    span = left_ref.shape[1]
    m = iota((EDGE, LANES), 0)
    lane = iota((EDGE, LANES), 1)
    sel_up = onehot((m < REACH) & (lane == m))
    sel_dn = onehot((m < REACH) & (lane == span - 2 + m))
    side = jnp.concatenate([left_ref[...], right_ref[...]], axis=0)
    side = jnp.concatenate([side, jnp.zeros((side.shape[0], LANES - span), BF16)], axis=1)
    feat = maps[...].reshape(3 * JCOLS, LANES).astype(BF16)
    n = 3 * JCOLS
    for sel, out in ((sel_up, up), (sel_dn, down)):
        out[:, 0:n] = dot(sel, feat, NT).astype(BF16)
        out[:, n:] = dot(sel, side, NT).astype(BF16)


def network_body(
    pins, n_nets, *refs
):
    pos = refs[0]
    net_refs = refs[1 : 1 + n_nets]
    (
        maps, from_up, from_down, cot, cot_below, cot_above, left_ref, right_ref,
        fwd, bwd, first_fwd, first_bwd, bias1, bias2,
    ) = refs[1 + n_nets : 15 + n_nets]
    rest = refs[15 + n_nets :]
    congestion = rest[0]
    grads = rest[1 : 1 + n_nets]
    cotx, feats, back_h, hid, back_p, grad_maps = rest[1 + n_nets :]
    chans = bias1.shape[0]
    span = cot.shape[1]
    cols = cot.shape[0] // chans
    col0, row0, all_cols, all_rows = pos[0], pos[1], pos[2], pos[3]
    n = 3 * JCOLS

    e = jnp.concatenate([from_up[...], from_down[...]], axis=0)
    m = iota((2 * EDGE, LANES), 0)
    lane = iota((2 * EDGE, LANES), 1)
    place = onehot(
        ((m < REACH) & (lane == (m - 2) % LANES))
        | ((m >= EDGE) & (m < EDGE + REACH) & (lane == span + m - EDGE))
    )
    total = maps[...].reshape(n, LANES) + dot(e[:, 0:n], place, TN)
    total = total.astype(BF16).astype(F32).reshape(3, JCOLS, LANES)
    feats[1] = total
    feats[0] = pltpu.roll(total, 1, 2)
    feats[2] = pltpu.roll(total, LANES - 1, 2)

    mm = iota((32, span), 0)
    ll = iota((32, span), 1)
    place2 = onehot(((mm < REACH) & (ll == mm)) | ((mm >= EDGE) & (ll == span - 2 + mm - EDGE)))
    first_row = 2 * chans
    cotx[first_row : first_row + cols * chans, 0:span] = cot[...]
    step = 512
    for k in range(cols * chans // step):
        s = slice(step * k, step * (k + 1))
        ends = jnp.concatenate([cot_below[:, s], cot_above[:, s]], axis=0)
        cotx[first_row + step * k : first_row + step * (k + 1), span:LANES] = dot(
            ends, place2, TN
        ).astype(BF16)
    edge_place = dot(e[:, n:], jnp.where(m < EDGE, jnp.where(m < 2, place, 0), place), TN).astype(BF16)
    tail = first_row + cols * chans
    cotx[0:first_row, 0:span] = left_ref[...]
    cotx[0:first_row, span:LANES] = edge_place[0:first_row, span:LANES]
    cotx[tail : tail + first_row, 0:span] = right_ref[...]
    cotx[tail : tail + first_row, span:LANES] = edge_place[first_row : 2 * first_row, span:LANES]
    cotx[tail + first_row :, :] = jnp.zeros((cotx.shape[0] - tail - first_row, LANES), BF16)

    block = GROUP * chans
    window = WINDOW * chans
    groups = pl.cdiv(cols + 2, GROUP)
    back_h[groups * block :, :] = jnp.zeros((back_h.shape[0] - groups * block, LANES), F32)

    def step_a(g, carry):
        lo = pl.multiple_of(g * block, block)
        p = dot(bwd[...], cotx[pl.ds(lo, window), :])
        back_h[pl.ds(lo, block), :] = (
            p[block : 2 * block]
            + pltpu.roll(p[0:block], LANES - 1, 1)
            + pltpu.roll(p[2 * block :], 1, 1)
        )
        return carry

    lax.fori_loop(0, groups, step_a, 0)

    lanes1 = iota((1, LANES), 1)
    row_of = jnp.where(lanes1 < LANES - 64, lanes1, lanes1 - LANES)
    grow = row_of + row0
    row_ok = (row_of >= -1) & (row_of < span + BOX) & (grow >= 0) & (grow < all_rows)
    bias_col = bias1[...].astype(F32)
    bias_rep = jnp.concatenate([bias_col] * 8, axis=0)
    jo_rows = iota((8 * chans, 1), 0) // chans

    def step_b(g, carry):
        lo8 = pl.multiple_of(g * 8, 8)
        pre = bias_rep
        for r in range(3):
            f = feats[r, :, pl.ds(lo8, 16), :].reshape(3 * 16, LANES).astype(BF16)
            pre = pre + dot(first_fwd[r], f)
        lo = pl.multiple_of(g * 8 * chans, 8 * chans)
        slot = 8 * g + 1 + jo_rows
        gcol = slot - 2 + col0
        col_ok = (slot <= cols + 2) & (gcol >= 0) & (gcol < all_cols)
        ok = col_ok & row_ok
        s = 0.5 + 0.5 * jnp.tanh(0.5 * pre)
        h = pre * s
        slope = s + h * (1.0 - s)
        bh = back_h[pl.ds(lo, 8 * chans), :]
        hid[pl.ds(lo, 8 * chans), :] = jnp.where(ok, h, 0.0).astype(BF16)
        back_p[pl.ds(lo, 8 * chans), :] = jnp.where(ok, bh * slope, 0.0).astype(BF16)
        return carry

    lax.fori_loop(0, pl.cdiv(cols + 2, 8), step_b, 0)

    bias_out = jnp.concatenate([bias2[...]] * GROUP, axis=0)
    groups_c = pl.cdiv(cols, GROUP)

    def back(g, lo):
        q = dot(first_bwd[...].astype(BF16), back_p[pl.ds(lo, window), :])
        gm = q[16:32] + pltpu.roll(q[0:16], LANES - 1, 1) + pltpu.roll(q[32:48], 1, 1)
        grad_maps[pl.ds(pl.multiple_of(16 * g, 16), 16), :] = gm.astype(BF16)

    def conv(lo):
        p = dot(fwd[...], hid[pl.ds(lo, window), :])
        out = (
            p[block : 2 * block]
            + pltpu.roll(p[0:block], 1, 1)
            + pltpu.roll(p[2 * block :], LANES - 1, 1)
        )
        return (out[:, 0:span] + bias_out).astype(BF16)

    def step_c(g, carry):
        lo = pl.multiple_of(g * block, block)
        congestion[pl.ds(lo, block), :] = conv(lo)
        back(g, lo)
        return carry

    full = cols // GROUP
    lax.fori_loop(0, full, step_c, 0)
    if groups_c > full:
        lo = full * block
        last = (cols - full * GROUP) * chans
        congestion[lo : lo + last, :] = conv(lo)[0:last]
        back(full, lo)

    x_rows = iota((8 * groups_c, 1), 0)
    slot = GROUP * (x_rows // 8) + x_rows % 8 + 2
    slot = jnp.where((x_rows % 8 < GROUP) & (slot < cols + 2), slot, 512).astype(F32)
    nets = net_refs[0].shape[2]
    fcol = col0.astype(F32)
    frow = row0.astype(F32)
    rows = iota((NROWS, nets), 0).astype(F32).astype(BF16)
    one = jnp.ones((), BF16)
    zero = jnp.zeros((), BF16)

    def net_chunk(ref, out, k):
        f, x, y = relative(ref, k, fcol, frow)
        y0, y1 = y(f[2:3]).astype(BF16), y(f[3:4]).astype(BF16)
        in_row = jnp.where((y0 <= rows) & (rows <= y1), one, zero)
        h = dot(grad_maps[:, 0:NROWS], in_row).reshape(groups_c, 2, 8, nets)
        x0, x1 = x(f[0:1]), x(f[1:2])
        in_col = ((x0 <= slot) & (slot <= x1)).reshape(groups_c, 8, nets)
        s0 = jnp.sum(jnp.sum(jnp.where(in_col, h[:, 0], 0.0), axis=0), axis=0, keepdims=True)
        s1 = jnp.sum(jnp.sum(jnp.where(in_col, h[:, 1], 0.0), axis=0), axis=0, keepdims=True)
        out[k, 0:1, :] = s0 / (f[3:4] - f[2:3] + 1.0) + s1 / (f[1:2] - f[0:1] + 1.0)

    for ref, out in zip(net_refs, grads):
        if ref.shape[0] == 1:
            net_chunk(ref, out, 0)
        else:
            lax.fori_loop(0, ref.shape[0], lambda k, c: (net_chunk(ref, out, k), c)[1], 0)


def shards(
    net_box, net_weight, pin_bin, conv_first, bias_first, conv_second, bias_second, cotangent
):
    cols, chans, span = cotangent.shape
    nets, pins = pin_bin.shape[:2]
    strips = lax.axis_size("strip")
    ncol = lax.axis_size("col")
    strip_index = lax.axis_index("strip")
    col_index = lax.axis_index("col")
    pos = jnp.stack(
        [col_index * cols, strip_index * span, cols * ncol, span * strips]
    ).astype(jnp.int32)
    cot = cotangent.reshape(cols * chans, span)
    edge = 2 * chans
    one_block = pl.BlockSpec((edge, span), lambda i: (0, 0))
    last_block = pl.BlockSpec((edge, span), lambda i: (cols * chans // edge - 1, 0))

    def full(*shape):
        return pl.BlockSpec(shape, lambda i: (0,) * len(shape))

    right, left, plain = pl.pallas_call(
        functools.partial(pack_body, pins),
        grid=(1,),
        in_specs=[full(4, nets), full(1, nets), full(pins, 2, nets), one_block, last_block],
        out_specs=[full(FIELDS + 8, nets), full(FIELDS + 8, nets), full(FIELDS, nets)],
        out_shape=[
            jax.ShapeDtypeStruct((FIELDS + 8, nets), F32),
            jax.ShapeDtypeStruct((FIELDS + 8, nets), F32),
            jax.ShapeDtypeStruct((FIELDS, nets), F32),
        ],
        cost_estimate=cost(10000, 400000),
    )(net_box.T, net_weight.reshape(1, nets), pin_bin.transpose(1, 2, 0), cot, cot)

    def ring(k):
        return [(i, (i + k) % ncol) for i in range(ncol)]

    from_left = lax.ppermute(right, "col", ring(1))
    from_right = lax.ppermute(left, "col", ring(ncol - 1))
    few = ncol == 4
    if few:
        far = lax.ppermute(plain, "col", ring(2))
        groups = [plain[None], from_left[None], from_right[None], far[None]]
    else:
        groups = [lax.all_gather(plain, "col", axis=0)]

    def unpack(buf, has):
        e = buf[FIELDS:].reshape(8, 8, span).transpose(1, 0, 2).reshape(edge, span)
        return jnp.where(has, e, 0.0).astype(BF16)

    left_cols = unpack(from_left, col_index > 0)
    right_cols = unpack(from_right, col_index < ncol - 1)
    up_pairs = [(i + 1, i) for i in range(strips - 1)]
    down_pairs = [(i, i + 1) for i in range(strips - 1)]

    cot_up, cot_down = call(
        cot_edge_body,
        [
            jax.ShapeDtypeStruct((EDGE, cols * chans), BF16),
            jax.ShapeDtypeStruct((8, cols * chans), BF16),
        ],
        1,
        cost=cost(40000000, 1300000),
    )(cot)
    cot_below = lax.ppermute(cot_up, "strip", up_pairs)
    cot_above = lax.ppermute(cot_down, "strip", down_pairs)

    cin = conv_first.shape[3]
    weights = call(
        weight_body,
        [
            jax.ShapeDtypeStruct((3 * GROUP * chans, WINDOW * chans), BF16),
            jax.ShapeDtypeStruct((3 * GROUP * chans, WINDOW * chans), BF16),
            jax.ShapeDtypeStruct((3, 8 * chans, cin * 16), BF16),
            jax.ShapeDtypeStruct((48, WINDOW * chans), F32),
        ],
        2,
        cost=cost(40000000, 1000000),
    )(
        conv_second.reshape(9, chans, chans),
        conv_first.reshape(9, chans, cin).transpose(0, 2, 1),
    )

    smem = pl.BlockSpec(memory_space=pltpu.SMEM)
    vmem = pl.BlockSpec(memory_space=pltpu.VMEM)
    width = 3 * JCOLS + 2 * edge
    maps, up, down = call(
        functools.partial(raster_body, pins, len(groups)),
        [
            jax.ShapeDtypeStruct((3, JCOLS, LANES), F32),
            jax.ShapeDtypeStruct((EDGE, width), BF16),
            jax.ShapeDtypeStruct((EDGE, width), BF16),
        ],
        0,
        in_specs=[smem] + [vmem] * (len(groups) + 2),
        cost=cost(1500000000, 1500000),
    )(pos, *groups, left_cols, right_cols)

    from_down = lax.ppermute(up, "strip", up_pairs)
    from_up = lax.ppermute(down, "strip", down_pairs)

    rows_x = (cols + 16) * chans
    outs = call(
        functools.partial(network_body, pins, len(groups)),
        [jax.ShapeDtypeStruct((cols * chans, span), BF16)]
        + [jax.ShapeDtypeStruct((g.shape[0], 1, nets), F32) for g in groups],
        0,
        in_specs=[smem] + [vmem] * (len(groups) + 14),
        scratch=[
            pltpu.VMEM((rows_x, LANES), BF16),
            pltpu.VMEM((3, 3, JCOLS, LANES), F32),
            pltpu.VMEM((rows_x, LANES), F32),
            pltpu.VMEM((rows_x, LANES), BF16),
            pltpu.VMEM((rows_x, LANES), BF16),
            pltpu.VMEM((16 * pl.cdiv(cols, GROUP), LANES), BF16),
        ],
        cost=cost(3000000000, 4000000),
    )(
        pos, *groups, maps, from_up, from_down, cot, cot_below, cot_above,
        left_cols, right_cols, *weights,
        bias_first.reshape(chans, 1), bias_second.reshape(chans, 1),
    )
    congestion = outs[0].reshape(cols, chans, span)
    if few:
        own, to_left, to_right, to_far = outs[1:]
        net_grad = (
            own
            + lax.ppermute(to_left, "col", ring(3))
            + lax.ppermute(to_right, "col", ring(1))
            + lax.ppermute(to_far, "col", ring(2))
        )
    else:
        net_grad = lax.psum_scatter(outs[1], "col", scatter_dimension=0, tiled=True)
    return congestion, net_grad.reshape(nets)


def solution(mesh):
    placed = (
        P(("strip", "col"), None),
        P(("strip", "col")),
        P(("strip", "col"), None, None),
        P(),
        P(),
        P(),
        P(),
        P("col", None, "strip"),
    )
    return jax.shard_map(
        shards,
        mesh=mesh,
        in_specs=placed,
        out_specs=(P("col", None, "strip"), P(("strip", "col"))),
        check_vma=False,
    )
```

time: 181 us -> 63.2 us (0.35)
  matrix products: 124 us -> 0 us
  Pallas kernels: 0 us -> 34.9 us
  blocking collectives: 15.4 us -> 0 us
  local copies, waits for them, and re-layouts: 9.63 us -> 3.34 us
  other arithmetic: 7.78 us -> 2.52 us
  waiting for transfers between devices: 6.95 us -> 3.34 us
  starting transfers between devices: 14.4 us -> 17.8 us
    dot_general x45 -> x0, matrix products: 124 us -> none  [the longest x18 59.7 us: conv_back(): jnp.einsum('oi,xoy->xiy', weights[shift_row, shift_col], window, preferre...]
    pallas_call x0 -> x5, Pallas kernels: none -> 34.9 us  [the longest x1 24.6 us: shards(): call(functools.partial(network_body, pins, len(groups)), [jax.ShapeDtypeS...]
    all_gather x2 -> x0, blocking collectives: 15.4 us -> none  [the longest x1 9.57 us: shards(): shard_piece = lax.all_gather(both_halves, 'col', axis=0, tiled=True)]
    ppermute x6 -> x10, waiting for transfers between devices: 6.95 us -> 3.34 us  [the longest x1 1.76 us: shards(): lax.ppermute(to_right, 'col', ring(1))]
    concatenate x1 -> x0, local copies, waits for them, and re-layouts: 3.6 us -> none  [with_halo(): block = jnp.concatenate([low, block, high], axis=dim)]
    ppermute x6 -> x10, starting transfers between devices: 14.4 us -> 17.8 us  [the longest x1 4.24 us: shards(): from_down = lax.ppermute(up, 'strip', up_pairs)]
    concatenate x3 -> x0, other arithmetic: 2.88 us -> none  [the longest x2 2.18 us: with_halo(): block = jnp.concatenate([low, block, high], axis=dim)]
    eq x8 -> x0, local copies, waits for them, and re-layouts: 2.17 us -> none  [the longest x4 1.08 us: strip_factors(): pin_rows[:, None] == row_ids[None, :]]
  transfers between devices with their start and end apart: 6 -> 10, of which waited for: 3 -> 3; matrix products, arithmetic and copies ran while one was open for 4% -> 5% of each run, Pallas kernels for 0% -> 14%
where the time goes in v1:
time: 63.2 us; the launch traced here: 62.6 us
  Pallas kernels  34.9 us (55%)
  starting transfers between devices  17.8 us (28%)
  waiting for transfers between devices  3.34 us (5%)
  local copies, waits for them, and re-layouts  3.34 us (5%)
  other arithmetic  2.52 us (4%)
  between operations  0.76 us (1%)
    pallas_call x1, Pallas kernels, shards(): call(functools.partial(network_body, pins, len(groups)), [jax.ShapeDtypeS...  24.6 us
    ppermute x1, starting transfers between devices, shards(): from_down = lax.ppermute(up, 'strip', up_pairs)  4.24 us
    pallas_call x1, Pallas kernels, shards(): call(functools.partial(raster_body, pins, len(groups)), [jax.ShapeDtypeSt...  4.21 us
    ppermute x1, starting transfers between devices, shards(): cot_above = lax.ppermute(cot_down, 'strip', down_pairs)  3.39 us
    ppermute x1, starting transfers between devices, shards(): cot_below = lax.ppermute(cot_up, 'strip', up_pairs)  3.34 us
    ppermute x1, starting transfers between devices, shards(): from_up = lax.ppermute(down, 'strip', down_pairs)  2.48 us
    pallas_call x1, Pallas kernels, shards(): call(cot_edge_body, [jax.ShapeDtypeStruct((EDGE, cols * chans), BF16), ja...  2.37 us
    pallas_call x1, Pallas kernels, shards(): call(weight_body, [jax.ShapeDtypeStruct((3 * GROUP * chans, WINDOW * chan...  2.13 us
  transfers between devices with their start and end apart: 10, of which 3 were waited for; matrix products, arithmetic and copies ran while one was open for 5% of the time, Pallas kernels for 14%

profile of v1, /device:TPU:16, one launch (start us, length us, event | category | flops | bytes accessed | tf_op | source)
XLA Modules:
  0.0 62.6 jit_solution(3288435847439175773)
XLA Ops:
  0.6 1.6 %shard_map.95 = (f32[24,1024]{1,0:T(8,128)}, f32[24,1024]{1,0:T(8,128)}, f32[16,1024]{1,0:T(8,128)}) custom-call(s32[4,1024]{1,0:T(4,128)} %bitcast.35, f32[1,1024]{1,0:T(1,128)} %bitcast.36, s32[4,2,1024]{2,1,0:T(2,128)} %bitcast.34, bf16[4096,128]{1,0:T(8,128)(2,1)} %bitcast.30, bf16[4096,128]{1,0:T(8,128)(2,1)} %bitcast.31), custom_call_target="tpu_custom_call" | custom-call | flops 10000 | bytes 400000 | tf_op jit(solution)/shard_map/pallas_call | solution.py:359
  2.2 1.5 %collective-permute-start.2 = (f32[16,1024]{1,0:T(8,128)}, f32[16,1024]{1,0:T(8,128)S(1)}, u32[]{:S(2)}, u32[]{:S(2)}) collective-permute-start(f32[16,1024]{1,0:T(8,128)} %get-tuple-element.19), channel_id=1, source_target_pairs={{0,2},{1,3},{2,0},{3,1},{4,6},{5,7},{6,4},{7,5},{8,10},{9,11},{10,... | collective-permute-start | bytes 196616 | tf_op jit(solution)/shard_map/ppermute | solution.py:379
  3.7 1.7 %collective-permute-start.1 = (f32[24,1024]{1,0:T(8,128)}, f32[24,1024]{1,0:T(8,128)S(1)}, u32[]{:S(2)}, u32[]{:S(2)}) collective-permute-start(f32[24,1024]{1,0:T(8,128)} %get-tuple-element.21), channel_id=1, source_target_pairs={{0,3},{1,0},{2,1},{3,2},{4,7},{5,4},{6,5},{7,6},{8,11},{9,8},{10,9... | collective-permute-start | bytes 294920 | tf_op jit(solution)/shard_map/ppermute | solution.py:376
  5.5 2.4 %shard_map.97 = (bf16[24,4096]{1,0:T(8,128)(2,1)}, bf16[8,4096]{1,0:T(8,128)(2,1)}) custom-call(bf16[4096,128]{1,0:T(8,128)(2,1)} %bitcast.32), custom_call_target="tpu_custom_call" | custom-call | flops 40000000 | bytes 1300000 | tf_op jit(solution)/shard_map/pallas_call | solution.py:393
  7.8 3.4 %collective-permute-start.6 = (bf16[8,4096]{1,0:T(8,128)(2,1)}, bf16[8,4096]{1,0:T(8,128)(2,1)S(1)}, u32[]{:S(2)}, u32[]{:S(2)}) collective-permute-start(bf16[8,4096]{1,0:T(8,128)(2,1)} %get-tuple-element.26), channel_id=1, source_target_pairs={{0,4},{4,8},{8,12},{12,16},{16,20},{20,24},{24,28},{1,5},{5,9},{9,... | collective-permute-start | bytes 196616 | tf_op jit(solution)/shard_map/ppermute | solution.py:403
  11.2 3.3 %collective-permute-start.5 = (bf16[24,4096]{1,0:T(8,128)(2,1)}, bf16[24,4096]{1,0:T(8,128)(2,1)S(1)}, u32[]{:S(2)}, u32[]{:S(2)}) collective-permute-start(bf16[24,4096]{1,0:T(8,128)(2,1)} %get-tuple-element.25), channel_id=1, source_target_pairs={{4,0},{8,4},{12,8},{16,12},{20,16},{24,20},{28,24},{5,1},{9,5},{13... | collective-permute-start | bytes 589832 | tf_op jit(solution)/shard_map/ppermute | solution.py:402
  14.6 0.7 %pad_add_fusion.refs_0_ = s32[4]{0:T(128)} fusion(s32[1]{0:T(128)} %constant.8.clone.1, s32[1]{0:T(128)} %constant.7.clone.1, s32[1]{0:T(128)} %bitcast.1, s32[1]{0:T(128)} %bitcast), kind=kLoop, calls=%fused_computation.7 | loop fusion | flops 12 | bytes 32 | tf_op jit(solution)/shard_map/stack | solution.py:348
  15.2 0.6 %fusion.2.refs_5_.refs_11_ = bf16[64,128]{1,0:T(8,128)(2,1)} fusion(f32[24,1024]{1,0:T(8,128)S(1)} %collective-permute-done, pred[]{:T(512)S(6)} %gt.3), kind=kLoop, calls=%fused_computation.4 | loop fusion | flops 8192 | bytes 32769 | tf_op jit(solution)/shard_map/convert_element_type | solution.py:386
  15.9 0.6 %fusion.3.refs_6_.refs_12_ = bf16[64,128]{1,0:T(8,128)(2,1)} fusion(f32[24,1024]{1,0:T(8,128)S(1)} %collective-permute-done.1, pred[]{:T(512)S(6)} %lt.3), kind=kLoop, calls=%fused_computation.5 | loop fusion | flops 8192 | bytes 32769 | tf_op jit(solution)/shard_map/convert_element_type | solution.py:386
  16.5 0.0 collective-permute-done.2
  16.5 0.6 copy-done.6
  17.1 4.2 %shard_map.96 = (f32[3,144,256]{2,1,0:T(8,128)}, bf16[24,560]{1,0:T(8,128)(2,1)}, bf16[24,560]{1,0:T(8,128)(2,1)}) custom-call(s32[4]{0:T(128)} %pad_add_fusion.refs_0_, f32[1,16,1024]{2,1,0:T(8,128)} %bitcast.45, f32[1,24,1024]{2,1,0:T(8,128)} %bitcast.38, f32[1,24,1024]{2,1,0:T(8,128)} %bitcast.40, f32[1,16,1024]{2,1,0:T(8,128)} %bitcast.47, ...), custom_call_target="tpu_custom_call" | custom-call | flops 1500000000 | bytes 1500000 | tf_op jit(solution)/shard_map/pallas_call | solution.py:424
  21.3 2.5 %collective-permute-start.3 = (bf16[24,560]{1,0:T(8,128)(2,1)}, bf16[24,560]{1,0:T(8,128)(2,1)S(1)}, u32[]{:S(2)}, u32[]{:S(2)}) collective-permute-start(bf16[24,560]{1,0:T(8,128)(2,1)} %get-tuple-element.23), channel_id=1, source_target_pairs={{0,4},{4,8},{8,12},{12,16},{16,20},{20,24},{24,28},{1,5},{5,9},{9,... | collective-permute-start | bytes 80648 | tf_op jit(solution)/shard_map/ppermute | solution.py:437
  23.8 0.0 copy-start.3
  23.8 4.2 %collective-permute-start.4 = (bf16[24,560]{1,0:T(8,128)(2,1)}, bf16[24,560]{1,0:T(8,128)(2,1)S(1)}, u32[]{:S(2)}, u32[]{:S(2)}) collective-permute-start(bf16[24,560]{1,0:T(8,128)(2,1)} %get-tuple-element.24), channel_id=1, source_target_pairs={{4,0},{8,4},{12,8},{16,12},{20,16},{24,20},{28,24},{5,1},{9,5},{13... | collective-permute-start | bytes 80648 | tf_op jit(solution)/shard_map/ppermute | solution.py:436
  28.1 0.7 %copy.10.refs_17_ = f32[32,1]{1,0:T(8,128)} copy(f32[32,1]{0,1:T(1,128)S(1)} %bitcast.42) | data formatting | bytes 256 | tf_op jit(solution)/shard_map/reshape | solution.py:458
  28.8 0.7 %copy-done.4 = f32[32]{0:T(128)S(1)} copy-done((f32[32]{0:T(128)S(1)}, f32[32]{0:T(128)}, u32[]{:S(2)}) %copy-start.4) | copy-done | bytes 152
  29.4 0.7 %copy.11.refs_18_ = f32[32,1]{1,0:T(8,128)} copy(f32[32,1]{0,1:T(1,128)S(1)} %bitcast.43) | data formatting | bytes 256 | tf_op jit(solution)/shard_map/reshape | solution.py:458
  30.1 2.1 %shard_map.98 = (bf16[576,256]{1,0:T(8,128)(2,1)}, bf16[576,256]{1,0:T(8,128)(2,1)}, bf16[3,256,48]{2,1,0:T(8,128)(2,1)}, f32[48,256]{1,0:T(8,128)}) custom-call(bf16[9,32,32]{2,1,0:T(8,128)(2,1)} %bitcast.44, bf16[9,3,32]{2,1,0:T(4,128)(2,1)} %bitcast.49), custom_call_target="tpu_custom_call" | custom-call | flops 40000000 | bytes 1000000 | tf_op jit(solution)/shard_map/pallas_call | solution.py:406
  32.3 0.0 collective-permute-done.4.refs_7_
  32.3 0.6 copy-done.7
  32.9 0.0 copy-done.8
  32.9 0.0 copy-done.9
  32.9 0.1 copy-done.5
  33.0 24.6 %shard_map.99 = (bf16[4096,128]{1,0:T(8,128)(2,1)}, f32[1,1,1024]{2,1,0:T(1,128)}, f32[1,1,1024]{2,1,0:T(1,128)}, f32[1,1,1024]{2,1,0:T(1,128)}, f32[1,1,1024]{2,1,0:T(1,128)}) custom-call(s32[4]{0:T(128)} %pad_add_fusion.refs_0_, f32[1,16,1024]{2,1,0:T(8,128)} %bitcast.46, f32[1,24,1024]{2,1,0:T(8,128)} %bitcast.39, f32[1,24,1024]{2,1,0:T(8,128)} %bitcast.41, ...), custom_call_target="tpu_custom_call" | custom-call | flops 3000000000 | bytes 4000000 | tf_op jit(solution)/shard_map/pallas_call | solution.py:440
  57.6 0.1 collective-permute-start.7
  57.7 0.5 collective-permute-start.8
  58.2 0.5 collective-permute-start.9
  58.7 0.5 collective-permute-done.7
  59.2 1.8 %collective-permute-done.8 = f32[1,1,1024]{2,1,0:T(1,128)S(1)} collective-permute-done((f32[1,1,1024]{2,1,0:T(1,128)}, f32[1,1,1024]{2,1,0:T(1,128)S(1)}, u32[]{:S(2)}, u32[]{:S(2)}) %collective-permute-start.8) | collective-permute-done | bytes 4128 | tf_op jit(solution)/shard_map/ppermute | solution.py:466
  61.0 1.0 %collective-permute-done.9 = f32[1,1,1024]{2,1,0:T(1,128)S(1)} collective-permute-done((f32[1,1,1024]{2,1,0:T(1,128)}, f32[1,1,1024]{2,1,0:T(1,128)S(1)}, u32[]{:S(2)}, u32[]{:S(2)}) %collective-permute-start.9) | collective-permute-done | bytes 4128 | tf_op jit(solution)/shard_map/ppermute | solution.py:467
  62.0 0.6 add_add_fusion
  (19 shorter events, 0.0 us)
Async XLA Ops:
  2.2 14.3 %collective-permute-start.2 = (f32[16,1024]{1,0:T(8,128)}, f32[16,1024]{1,0:T(8,128)S(1)}, u32[]{:S(2)}, u32[]{:S(2)}) collective-permute-start(f32[16,1024]{1,0:T(8,128)} %get-tuple-element.19), channel_id=1, source_target_pairs={{0,2},{1,3},{2,0},{3,1},{4,6},{5,7},{6,4},{7,5},{8,10},{9,11},{10,... | collective-permute-start | bytes 196616 | tf_op jit(solution)/shard_map/ppermute | solution.py:379
  3.7 11.5 %collective-permute-start = (f32[24,1024]{1,0:T(8,128)}, f32[24,1024]{1,0:T(8,128)S(1)}, u32[]{:S(2)}, u32[]{:S(2)}) collective-permute-start(f32[24,1024]{1,0:T(8,128)} %get-tuple-element.20), channel_id=1, source_target_pairs={{0,1},{1,2},{2,3},{3,0},{4,5},{5,6},{6,7},{7,4},{8,9},{9,10},{10,1... | collective-permute-start | bytes 294920 | tf_op jit(solution)/shard_map/ppermute | solution.py:375
  3.7 12.2 %collective-permute-start.1 = (f32[24,1024]{1,0:T(8,128)}, f32[24,1024]{1,0:T(8,128)S(1)}, u32[]{:S(2)}, u32[]{:S(2)}) collective-permute-start(f32[24,1024]{1,0:T(8,128)} %get-tuple-element.21), channel_id=1, source_target_pairs={{0,3},{1,0},{2,1},{3,2},{4,7},{5,4},{6,5},{7,6},{8,11},{9,8},{10,9... | collective-permute-start | bytes 294920 | tf_op jit(solution)/shard_map/ppermute | solution.py:376
  7.8 24.4 %collective-permute-start.6 = (bf16[8,4096]{1,0:T(8,128)(2,1)}, bf16[8,4096]{1,0:T(8,128)(2,1)S(1)}, u32[]{:S(2)}, u32[]{:S(2)}) collective-permute-start(bf16[8,4096]{1,0:T(8,128)(2,1)} %get-tuple-element.26), channel_id=1, source_target_pairs={{0,4},{4,8},{8,12},{12,16},{16,20},{20,24},{24,28},{1,5},{5,9},{9,... | collective-permute-start | bytes 196616 | tf_op jit(solution)/shard_map/ppermute | solution.py:403
  11.2 21.1 %collective-permute-start.5 = (bf16[24,4096]{1,0:T(8,128)(2,1)}, bf16[24,4096]{1,0:T(8,128)(2,1)S(1)}, u32[]{:S(2)}, u32[]{:S(2)}) collective-permute-start(bf16[24,4096]{1,0:T(8,128)(2,1)} %get-tuple-element.25), channel_id=1, source_target_pairs={{4,0},{8,4},{12,8},{16,12},{20,16},{24,20},{28,24},{5,1},{9,5},{13... | collective-permute-start | bytes 589832 | tf_op jit(solution)/shard_map/ppermute | solution.py:402
  15.2 1.3 %copy-start.1 = (f32[24,1024]{1,0:T(8,128)}, f32[24,1024]{1,0:T(8,128)S(1)}, u32[]{:S(2)}) copy-start(f32[24,1024]{1,0:T(8,128)S(1)} %collective-permute-done) | copy-start | bytes 294916
  15.9 0.6 %copy-start.2 = (f32[24,1024]{1,0:T(8,128)}, f32[24,1024]{1,0:T(8,128)S(1)}, u32[]{:S(2)}) copy-start(f32[24,1024]{1,0:T(8,128)S(1)} %collective-permute-done.1) | copy-start | bytes 294916
  16.5 0.6 copy-start.6
  21.3 10.9 %collective-permute-start.3 = (bf16[24,560]{1,0:T(8,128)(2,1)}, bf16[24,560]{1,0:T(8,128)(2,1)S(1)}, u32[]{:S(2)}, u32[]{:S(2)}) collective-permute-start(bf16[24,560]{1,0:T(8,128)(2,1)} %get-tuple-element.23), channel_id=1, source_target_pairs={{0,4},{4,8},{8,12},{12,16},{16,20},{20,24},{24,28},{1,5},{5,9},{9,... | collective-permute-start | bytes 80648 | tf_op jit(solution)/shard_map/ppermute | solution.py:437
  23.8 4.3 %copy-start.3 = (f32[32]{0:T(128)S(1)}, f32[32]{0:T(128)}, u32[]{:S(2)}) copy-start(f32[32]{0:T(128)} %param.12) | copy-start | bytes 388
  23.8 8.4 %collective-permute-start.4 = (bf16[24,560]{1,0:T(8,128)(2,1)}, bf16[24,560]{1,0:T(8,128)(2,1)S(1)}, u32[]{:S(2)}, u32[]{:S(2)}) collective-permute-start(bf16[24,560]{1,0:T(8,128)(2,1)} %get-tuple-element.24), channel_id=1, source_target_pairs={{4,0},{8,4},{12,8},{16,12},{20,16},{24,20},{28,24},{5,1},{9,5},{13... | collective-permute-start | bytes 80648 | tf_op jit(solution)/shard_map/ppermute | solution.py:436
  28.8 0.7 %copy-start.4 = (f32[32]{0:T(128)S(1)}, f32[32]{0:T(128)}, u32[]{:S(2)}) copy-start(f32[32]{0:T(128)} %param.14) | copy-start | bytes 388
  32.3 0.6 copy-start.7
  32.3 0.6 %copy-start.8 = (bf16[24,560]{1,0:T(8,128)(2,1)}, bf16[24,560]{1,0:T(8,128)(2,1)S(1)}, u32[]{:S(2)}) copy-start(bf16[24,560]{1,0:T(8,128)(2,1)S(1)} %collective-permute-done.3.refs_6_) | copy-start | bytes 80644
  32.3 0.6 copy-start.9
  32.3 0.7 %copy-start.5 = (bf16[24,4096]{1,0:T(8,128)(2,1)}, bf16[24,4096]{1,0:T(8,128)(2,1)S(1)}, u32[]{:S(2)}) copy-start(bf16[24,4096]{1,0:T(8,128)(2,1)S(1)} %collective-permute-done.5.refs_9_) | copy-start | bytes 589828
  57.6 4.4 %copy-start = (f32[1,1,1024]{2,1,0:T(1,128)S(1)}, f32[1,1,1024]{2,1,0:T(1,128)}, u32[]{:S(2)}) copy-start(f32[1,1,1024]{2,1,0:T(1,128)} %get-tuple-element.32) | copy-start | bytes 12292
  57.6 1.6 %collective-permute-start.7 = (f32[1,1,1024]{2,1,0:T(1,128)}, f32[1,1,1024]{2,1,0:T(1,128)S(1)}, u32[]{:S(2)}, u32[]{:S(2)}) collective-permute-start(f32[1,1,1024]{2,1,0:T(1,128)} %get-tuple-element.33), channel_id=1, source_target_pairs={{0,3},{1,0},{2,1},{3,2},{4,7},{5,4},{6,5},{7,6},{8,11},{9,8},{10,9... | collective-permute-start | bytes 12296 | tf_op jit(solution)/shard_map/ppermute | solution.py:465
  57.7 3.3 %collective-permute-start.8 = (f32[1,1,1024]{2,1,0:T(1,128)}, f32[1,1,1024]{2,1,0:T(1,128)S(1)}, u32[]{:S(2)}, u32[]{:S(2)}) collective-permute-start(f32[1,1,1024]{2,1,0:T(1,128)} %get-tuple-element.34), channel_id=1, source_target_pairs={{0,1},{1,2},{2,3},{3,0},{4,5},{5,6},{6,7},{7,4},{8,9},{9,10},{10,1... | collective-permute-start | bytes 12296 | tf_op jit(solution)/shard_map/ppermute | solution.py:466
  58.2 3.8 %collective-permute-start.9 = (f32[1,1,1024]{2,1,0:T(1,128)}, f32[1,1,1024]{2,1,0:T(1,128)S(1)}, u32[]{:S(2)}, u32[]{:S(2)}) collective-permute-start(f32[1,1,1024]{2,1,0:T(1,128)} %get-tuple-element.35), channel_id=1, source_target_pairs={{0,2},{1,3},{2,0},{3,1},{4,6},{5,7},{6,4},{7,5},{8,10},{9,11},{10,... | collective-permute-start | bytes 12296 | tf_op jit(solution)/shard_map/ppermute | solution.py:467

commit v2 on v1

--- a/solution.py
+++ b/solution.py
@@ -55,7 +55,8 @@
     return pl.CostEstimate(flops=flops, bytes_accessed=nbytes, transcendentals=0)
 
 
-def pack_body(pins, box, weight, pin, first, last, to_right, to_left, plain):
+def pack_body(pins, box, weight, pin, first, last, to_even, to_odd, plain):
+    odd = lax.axis_index("col") % 2 == 1
     rows = [box[...].astype(F32), weight[...]]
     rows += [pin[p].astype(F32) for p in range(pins)]
     nets = box.shape[1]
@@ -63,24 +64,45 @@
     rows.append(jnp.zeros((FIELDS - used, nets), F32))
     fields = jnp.concatenate(rows, axis=0)
     plain[...] = fields
-    to_right[0:FIELDS, :] = fields
-    to_left[0:FIELDS, :] = fields
-    for ref, edge in ((to_right, last), (to_left, first)):
-        e = edge[...].astype(F32)
+    to_even[0:FIELDS, :] = fields
+    to_odd[0:FIELDS, :] = fields
+    a, b = first[...].astype(F32), last[...].astype(F32)
+    for ref, e in ((to_even, jnp.where(odd, a, b)), (to_odd, jnp.where(odd, b, a))):
         for k in range(8):
             ref[FIELDS : FIELDS + 8, 128 * k : 128 * (k + 1)] = e[8 * k : 8 * k + 8, :]
 
 
-def cot_edge_body(cot, up, down):
+def cot_edge_body(cot, to_even, to_odd):
+    odd = lax.axis_index("strip") % 2
     span = cot.shape[1]
-    m = iota((32, span), 0)
-    lane = iota((32, span), 1)
-    sel = onehot(((m < REACH) & (lane == m)) | ((m >= EDGE) & (lane == span - 2 + m - EDGE)))
+    m = iota((2 * EDGE, span), 0)
+    lane = iota((2 * EDGE, span), 1)
+    up = (m % EDGE < REACH) & (lane == m % EDGE)
+    down = (m % EDGE < 2) & (lane == span - 2 + m % EDGE)
+    sel = onehot(((m // EDGE == odd) & down) | ((m // EDGE != odd) & up))
     step = 512
     for k in range(cot.shape[0] // step):
         got = dot(sel, cot[step * k : step * (k + 1), :], NT).astype(BF16)
-        up[:, step * k : step * (k + 1)] = got[:EDGE]
-        down[:, step * k : step * (k + 1)] = got[EDGE:]
+        to_even[:, step * k : step * (k + 1)] = got[:EDGE]
+        to_odd[:, step * k : step * (k + 1)] = got[EDGE:]
+
+
+def block_origin(cols, span):
+    return lax.axis_index("col") * cols, lax.axis_index("strip") * span
+
+
+def side_columns(even_ref, odd_ref, span):
+    c = lax.axis_index("col")
+    odd = c % 2 == 1
+
+    def unpack(ref):
+        e = ref[0, FIELDS : FIELDS + 8, :]
+        return jnp.concatenate([e[:, span * k : span * (k + 1)] for k in range(8)], axis=0)
+
+    a, b = unpack(even_ref), unpack(odd_ref)
+    left = jnp.where(c > 0, jnp.where(odd, a, b), 0.0)
+    right = jnp.where(c < lax.axis_size("col") - 1, jnp.where(odd, b, a), 0.0)
+    return left.astype(BF16), right.astype(BF16)
 
 
 def weight_body(second, first, fwd, bwd, first_fwd, first_bwd):
@@ -128,12 +150,10 @@
     return f, x, y
 
 
-def raster_body(pins, n_nets, *refs):
-    pos = refs[0]
-    net_refs = refs[1 : 1 + n_nets]
-    left_ref, right_ref, maps, up, down = refs[1 + n_nets :]
-    col0 = pos[0].astype(F32)
-    row0 = pos[1].astype(F32)
+def raster_body(pins, cols, span, n_nets, *refs):
+    net_refs = refs[:n_nets]
+    even_ref, odd_ref, maps, to_even, to_odd = refs[n_nets:]
+    col0, row0 = (v.astype(F32) for v in block_origin(cols, span))
     maps[...] = jnp.zeros_like(maps)
     nets = net_refs[0].shape[2]
     step = nets
@@ -165,16 +185,16 @@
             chunk(ref, 0)
         else:
             lax.fori_loop(0, ref.shape[0], lambda m, c: (chunk(ref, m), c)[1], 0)
-    span = left_ref.shape[1]
     m = iota((EDGE, LANES), 0)
     lane = iota((EDGE, LANES), 1)
-    sel_up = onehot((m < REACH) & (lane == m))
-    sel_dn = onehot((m < REACH) & (lane == span - 2 + m))
-    side = jnp.concatenate([left_ref[...], right_ref[...]], axis=0)
+    odd = lax.axis_index("strip") % 2
+    sel_even = onehot((m < REACH) & (lane == m + (span - 2) * (1 - odd)))
+    sel_odd = onehot((m < REACH) & (lane == m + (span - 2) * odd))
+    side = jnp.concatenate(side_columns(even_ref, odd_ref, span), axis=0)
     side = jnp.concatenate([side, jnp.zeros((side.shape[0], LANES - span), BF16)], axis=1)
     feat = maps[...].reshape(3 * JCOLS, LANES).astype(BF16)
     n = 3 * JCOLS
-    for sel, out in ((sel_up, up), (sel_dn, down)):
+    for sel, out in ((sel_even, to_even), (sel_odd, to_odd)):
         out[:, 0:n] = dot(sel, feat, NT).astype(BF16)
         out[:, n:] = dot(sel, side, NT).astype(BF16)
 
@@ -182,28 +202,41 @@
 def network_body(
     pins, n_nets, *refs
 ):
-    pos = refs[0]
-    net_refs = refs[1 : 1 + n_nets]
+    net_refs = refs[:n_nets]
     (
-        maps, from_up, from_down, cot, cot_below, cot_above, left_ref, right_ref,
+        maps, from_even, from_odd, cot, cot_even, cot_odd, even_ref, odd_ref,
         fwd, bwd, first_fwd, first_bwd, bias1, bias2,
-    ) = refs[1 + n_nets : 15 + n_nets]
-    rest = refs[15 + n_nets :]
+    ) = refs[n_nets : 14 + n_nets]
+    rest = refs[14 + n_nets :]
     congestion = rest[0]
     grads = rest[1 : 1 + n_nets]
     cotx, feats, back_h, hid, back_p, grad_maps = rest[1 + n_nets :]
-    chans = bias1.shape[0]
+    chans = bias1.shape[1]
     span = cot.shape[1]
     cols = cot.shape[0] // chans
-    col0, row0, all_cols, all_rows = pos[0], pos[1], pos[2], pos[3]
+    col0, row0 = block_origin(cols, span)
+    all_cols = cols * lax.axis_size("col")
+    all_rows = span * lax.axis_size("strip")
+    strip = lax.axis_index("strip")
+    odd = strip % 2
+    has_above = (strip > 0).astype(jnp.int32)
+    has_below = (strip < lax.axis_size("strip") - 1).astype(jnp.int32)
+    left_cols, right_cols = side_columns(even_ref, odd_ref, span)
     n = 3 * JCOLS
 
-    e = jnp.concatenate([from_up[...], from_down[...]], axis=0)
+    e = jnp.concatenate([from_even[...], from_odd[...]], axis=0)
     m = iota((2 * EDGE, LANES), 0)
     lane = iota((2 * EDGE, LANES), 1)
+    k = m % EDGE
+    below = (m // EDGE == odd) & (has_below == 1)
+    above = (m // EDGE != odd) & (has_above == 1)
     place = onehot(
-        ((m < REACH) & (lane == (m - 2) % LANES))
-        | ((m >= EDGE) & (m < EDGE + REACH) & (lane == span + m - EDGE))
+        (above & (k < REACH) & (lane == (k - 2) % LANES))
+        | (below & (k < REACH) & (lane == span + k))
+    )
+    side_place = onehot(
+        (above & (k < 2) & (lane == (k - 2) % LANES))
+        | (below & (k < REACH) & (lane == span + k))
     )
     total = maps[...].reshape(n, LANES) + dot(e[:, 0:n], place, TN)
     total = total.astype(BF16).astype(F32).reshape(3, JCOLS, LANES)
@@ -211,23 +244,21 @@
     feats[0] = pltpu.roll(total, 1, 2)
     feats[2] = pltpu.roll(total, LANES - 1, 2)
 
-    mm = iota((32, span), 0)
-    ll = iota((32, span), 1)
-    place2 = onehot(((mm < REACH) & (ll == mm)) | ((mm >= EDGE) & (ll == span - 2 + mm - EDGE)))
+    place2 = side_place[:, span:]
     first_row = 2 * chans
     cotx[first_row : first_row + cols * chans, 0:span] = cot[...]
     step = 512
     for k in range(cols * chans // step):
         s = slice(step * k, step * (k + 1))
-        ends = jnp.concatenate([cot_below[:, s], cot_above[:, s]], axis=0)
+        ends = jnp.concatenate([cot_even[:, s], cot_odd[:, s]], axis=0)
         cotx[first_row + step * k : first_row + step * (k + 1), span:LANES] = dot(
             ends, place2, TN
         ).astype(BF16)
-    edge_place = dot(e[:, n:], jnp.where(m < EDGE, jnp.where(m < 2, place, 0), place), TN).astype(BF16)
+    edge_place = dot(e[:, n:], side_place, TN).astype(BF16)
     tail = first_row + cols * chans
-    cotx[0:first_row, 0:span] = left_ref[...]
+    cotx[0:first_row, 0:span] = left_cols
     cotx[0:first_row, span:LANES] = edge_place[0:first_row, span:LANES]
-    cotx[tail : tail + first_row, 0:span] = right_ref[...]
+    cotx[tail : tail + first_row, 0:span] = right_cols
     cotx[tail : tail + first_row, span:LANES] = edge_place[first_row : 2 * first_row, span:LANES]
     cotx[tail + first_row :, :] = jnp.zeros((cotx.shape[0] - tail - first_row, LANES), BF16)
 
@@ -246,13 +277,13 @@
         )
         return carry
 
-    lax.fori_loop(0, groups, step_a, 0)
+    lax.fori_loop(0, groups, step_a, 0, unroll=True)
 
     lanes1 = iota((1, LANES), 1)
     row_of = jnp.where(lanes1 < LANES - 64, lanes1, lanes1 - LANES)
     grow = row_of + row0
     row_ok = (row_of >= -1) & (row_of < span + BOX) & (grow >= 0) & (grow < all_rows)
-    bias_col = bias1[...].astype(F32)
+    bias_col = bias1[...].T
     bias_rep = jnp.concatenate([bias_col] * 8, axis=0)
     jo_rows = iota((8 * chans, 1), 0) // chans
 
@@ -275,9 +306,9 @@
         back_p[pl.ds(lo, 8 * chans), :] = jnp.where(ok, bh * slope, 0.0).astype(BF16)
         return carry
 
-    lax.fori_loop(0, pl.cdiv(cols + 2, 8), step_b, 0)
-
-    bias_out = jnp.concatenate([bias2[...]] * GROUP, axis=0)
+    lax.fori_loop(0, pl.cdiv(cols + 2, 8), step_b, 0, unroll=True)
+
+    bias_out = jnp.concatenate([bias2[...].T] * GROUP, axis=0)
     groups_c = pl.cdiv(cols, GROUP)
 
     def back(g, lo):
@@ -301,7 +332,7 @@
         return carry
 
     full = cols // GROUP
-    lax.fori_loop(0, full, step_c, 0)
+    lax.fori_loop(0, full, step_c, 0, unroll=True)
     if groups_c > full:
         lo = full * block
         last = (cols - full * GROUP) * chans
@@ -343,11 +374,6 @@
     nets, pins = pin_bin.shape[:2]
     strips = lax.axis_size("strip")
     ncol = lax.axis_size("col")
-    strip_index = lax.axis_index("strip")
-    col_index = lax.axis_index("col")
-    pos = jnp.stack(
-        [col_index * cols, strip_index * span, cols * ncol, span * strips]
-    ).astype(jnp.int32)
     cot = cotangent.reshape(cols * chans, span)
     edge = 2 * chans
     one_block = pl.BlockSpec((edge, span), lambda i: (0, 0))
@@ -356,7 +382,7 @@
     def full(*shape):
         return pl.BlockSpec(shape, lambda i: (0,) * len(shape))
 
-    right, left, plain = pl.pallas_call(
+    to_even, to_odd, plain = pl.pallas_call(
         functools.partial(pack_body, pins),
         grid=(1,),
         in_specs=[full(4, nets), full(1, nets), full(pins, 2, nets), one_block, last_block],
@@ -369,38 +395,43 @@
         cost_estimate=cost(10000, 400000),
     )(net_box.T, net_weight.reshape(1, nets), pin_bin.transpose(1, 2, 0), cot, cot)
 
-    def ring(k):
-        return [(i, (i + k) % ncol) for i in range(ncol)]
-
-    from_left = lax.ppermute(right, "col", ring(1))
-    from_right = lax.ppermute(left, "col", ring(ncol - 1))
+    def swapped(i, n, phase):
+        return (i ^ 1) if phase == 0 else (((i + 1) ^ 1) - 1) % n
+
+    def swap_col(x, phase):
+        return lax.ppermute(x, "col", [(i, swapped(i, ncol, phase)) for i in range(ncol)])
+
+    def swap_strip(x, phase):
+        pairs = []
+        for i in range(strips):
+            for c in range(ncol):
+                j = swapped(i, strips, phase)
+                target = i * ncol + (c ^ 1) if abs(i - j) != 1 else j * ncol + c
+                pairs.append((i * ncol + c, target))
+        return lax.ppermute(x, ("strip", "col"), pairs)
+
     few = ncol == 4
+    by_even = swap_col(to_even, 0)
+    by_odd = swap_col(to_odd, 1)
+    opposite = [(i, i ^ 2) for i in range(ncol)]
     if few:
-        far = lax.ppermute(plain, "col", ring(2))
-        groups = [plain[None], from_left[None], from_right[None], far[None]]
+        far = lax.ppermute(plain, "col", opposite)
+        groups = [plain[None], by_even[None], by_odd[None], far[None]]
     else:
         groups = [lax.all_gather(plain, "col", axis=0)]
-
-    def unpack(buf, has):
-        e = buf[FIELDS:].reshape(8, 8, span).transpose(1, 0, 2).reshape(edge, span)
-        return jnp.where(has, e, 0.0).astype(BF16)
-
-    left_cols = unpack(from_left, col_index > 0)
-    right_cols = unpack(from_right, col_index < ncol - 1)
-    up_pairs = [(i + 1, i) for i in range(strips - 1)]
-    down_pairs = [(i, i + 1) for i in range(strips - 1)]
-
-    cot_up, cot_down = call(
+    sides = (by_even[None], by_odd[None])
+
+    cot_to_even, cot_to_odd = call(
         cot_edge_body,
         [
             jax.ShapeDtypeStruct((EDGE, cols * chans), BF16),
-            jax.ShapeDtypeStruct((8, cols * chans), BF16),
+            jax.ShapeDtypeStruct((EDGE, cols * chans), BF16),
         ],
         1,
         cost=cost(40000000, 1300000),
     )(cot)
-    cot_below = lax.ppermute(cot_up, "strip", up_pairs)
-    cot_above = lax.ppermute(cot_down, "strip", down_pairs)
+    cot_even = swap_strip(cot_to_even, 0)
+    cot_odd = swap_strip(cot_to_odd, 1)
 
     cin = conv_first.shape[3]
     weights = call(
@@ -418,31 +449,27 @@
         conv_first.reshape(9, chans, cin).transpose(0, 2, 1),
     )
 
-    smem = pl.BlockSpec(memory_space=pltpu.SMEM)
-    vmem = pl.BlockSpec(memory_space=pltpu.VMEM)
     width = 3 * JCOLS + 2 * edge
-    maps, up, down = call(
-        functools.partial(raster_body, pins, len(groups)),
+    maps, edge_even, edge_odd = call(
+        functools.partial(raster_body, pins, cols, span, len(groups)),
         [
             jax.ShapeDtypeStruct((3, JCOLS, LANES), F32),
             jax.ShapeDtypeStruct((EDGE, width), BF16),
             jax.ShapeDtypeStruct((EDGE, width), BF16),
         ],
-        0,
-        in_specs=[smem] + [vmem] * (len(groups) + 2),
+        len(groups) + 2,
         cost=cost(1500000000, 1500000),
-    )(pos, *groups, left_cols, right_cols)
-
-    from_down = lax.ppermute(up, "strip", up_pairs)
-    from_up = lax.ppermute(down, "strip", down_pairs)
+    )(*groups, *sides)
+
+    from_even = swap_strip(edge_even, 0)
+    from_odd = swap_strip(edge_odd, 1)
 
     rows_x = (cols + 16) * chans
     outs = call(
         functools.partial(network_body, pins, len(groups)),
         [jax.ShapeDtypeStruct((cols * chans, span), BF16)]
         + [jax.ShapeDtypeStruct((g.shape[0], 1, nets), F32) for g in groups],
-        0,
-        in_specs=[smem] + [vmem] * (len(groups) + 14),
+        len(groups) + 14,
         scratch=[
             pltpu.VMEM((rows_x, LANES), BF16),
             pltpu.VMEM((3, 3, JCOLS, LANES), F32),
@@ -453,18 +480,17 @@
         ],
         cost=cost(3000000000, 4000000),
     )(
-        pos, *groups, maps, from_up, from_down, cot, cot_below, cot_above,
-        left_cols, right_cols, *weights,
-        bias_first.reshape(chans, 1), bias_second.reshape(chans, 1),
+        *groups, maps, from_even, from_odd, cot, cot_even, cot_odd, *sides, *weights,
+        bias_first.reshape(1, chans), bias_second.reshape(1, chans),
     )
     congestion = outs[0].reshape(cols, chans, span)
     if few:
-        own, to_left, to_right, to_far = outs[1:]
+        own, for_even, for_odd, for_far = outs[1:]
         net_grad = (
             own
-            + lax.ppermute(to_left, "col", ring(3))
-            + lax.ppermute(to_right, "col", ring(1))
-            + lax.ppermute(to_far, "col", ring(2))
+            + swap_col(for_even, 0)
+            + swap_col(for_odd, 1)
+            + lax.ppermute(for_far, "col", opposite)
         )
     else:
         net_grad = lax.psum_scatter(outs[1], "col", scatter_dimension=0, tiled=True)

time: 63.2 us -> 40.3 us (0.64)
  Pallas kernels: 34.9 us -> 22.2 us
  starting transfers between devices: 17.8 us -> 8.66 us
  waiting for transfers between devices: 3.34 us -> 6.41 us
  other arithmetic: 2.52 us -> 0.6 us
  local copies, waits for them, and re-layouts: 3.34 us -> 1.42 us
    pallas_call x1, Pallas kernels: 24.6 us -> 11.8 us  [shards(): call(functools.partial(network_body, pins, len(groups)), [jax.ShapeDtypeS...]
    ppermute x10, starting transfers between devices: 17.8 us -> 8.66 us  [the longest x4 4.31 us: swap_strip(): return lax.ppermute(x, ('strip', 'col'), pairs)]
    ppermute x10, waiting for transfers between devices: 3.34 us -> 6.41 us  [the longest x4 2.86 us: swap_strip(): return lax.ppermute(x, ('strip', 'col'), pairs)]
    reshape x2 -> x0, local copies, waits for them, and re-layouts: 1.37 us -> none  [the longest x1 0.69 us: shards(): bias_first.reshape(chans, 1)]
    convert_element_type x2 -> x0, other arithmetic: 1.27 us -> none  [unpack(): return jnp.where(has, e, 0.0).astype(BF16)]
    another operation x1 -> x0, other arithmetic: 0.65 us -> none  [shards(): jnp.stack([col_index * cols, strip_index * span, cols * ncol, span * stri...]
    unnamed x20 -> x16, local copies, waits for them, and re-layouts: 1.97 us -> 1.42 us
  transfers between devices with their start and end apart: 10 -> 10, of which waited for: 3 -> 4; matrix products, arithmetic and copies ran while one was open for 5% -> 0% of each run, Pallas kernels for 14% -> 22%
where the time goes in v2:
time: 40.3 us; the launch traced here: 40 us
  Pallas kernels  22.2 us (55%)
  starting transfers between devices  8.66 us (21%)
  waiting for transfers between devices  6.41 us (16%)
  local copies, waits for them, and re-layouts  1.42 us (4%)
  between operations  0.7 us (2%)
  other arithmetic  0.6 us (1%)
    pallas_call x1, Pallas kernels, shards(): call(functools.partial(network_body, pins, len(groups)), [jax.ShapeDtypeS...  11.8 us
    ppermute x4, starting transfers between devices, swap_strip(): return lax.ppermute(x, ('strip', 'col'), pairs)  4.31 us
    pallas_call x1, Pallas kernels, shards(): call(functools.partial(raster_body, pins, cols, span, len(groups)), [jax....  4.3 us
    ppermute x4, starting transfers between devices, swap_col(): lax.ppermute(x, 'col', [(i, swapped(i, ncol, phase)) for i in range(ncol)])  3.34 us
    ppermute x4, waiting for transfers between devices, swap_strip(): return lax.ppermute(x, ('strip', 'col'), pairs)  2.86 us
    pallas_call x1, Pallas kernels, shards(): call(cot_edge_body, [jax.ShapeDtypeStruct((EDGE, cols * chans), BF16), ja...  2.43 us
    ppermute x1, waiting for transfers between devices, shards(): lax.ppermute(for_far, 'col', opposite)  2.14 us
    pallas_call x1, Pallas kernels, shards(): call(weight_body, [jax.ShapeDtypeStruct((3 * GROUP * chans, WINDOW * chan...  2.14 us
  transfers between devices with their start and end apart: 10, of which 4 were waited for; matrix products, arithmetic and copies ran while one was open for 0% of the time, Pallas kernels for 22%

profile of v2, /device:TPU:16, one launch (start us, length us, event | category | flops | bytes accessed | tf_op | source)
XLA Modules:
  0.0 40.0 jit_solution(8731627023658745768)
XLA Ops:
  0.6 1.5 %shard_map.95 = (f32[24,1024]{1,0:T(8,128)}, f32[24,1024]{1,0:T(8,128)}, f32[16,1024]{1,0:T(8,128)}) custom-call(s32[4,1024]{1,0:T(4,128)} %bitcast.21, f32[1,1024]{1,0:T(1,128)} %bitcast.22, s32[4,2,1024]{2,1,0:T(2,128)} %bitcast.20, bf16[4096,128]{1,0:T(8,128)(2,1)} %bitcast.16, bf16[4096,128]{1,0:T(8,128)(2,1)} %bitcast.17), custom_call_target="tpu_custom_call" | custom-call | flops 10000 | bytes 400000 | tf_op jit(solution)/shard_map/pallas_call | solution.py:385
  2.2 0.0 collective-permute-start
  2.2 1.6 %collective-permute-start.1 = (f32[24,1024]{1,0:T(8,128)}, f32[24,1024]{1,0:T(8,128)S(1)}, u32[]{:S(2)}, u32[]{:S(2)}) collective-permute-start(f32[24,1024]{1,0:T(8,128)} %get-tuple-element.21), channel_id=1, source_target_pairs={{0,3},{1,2},{2,1},{3,0},{4,7},{5,6},{6,5},{7,4},{8,11},{9,10},{10,... | collective-permute-start | bytes 294920 | tf_op jit(solution)/shard_map/ppermute | solution.py:402
  3.8 0.5 %collective-permute-start.2 = (f32[16,1024]{1,0:T(8,128)}, f32[16,1024]{1,0:T(8,128)S(1)}, u32[]{:S(2)}, u32[]{:S(2)}) collective-permute-start(f32[16,1024]{1,0:T(8,128)} %get-tuple-element.19), channel_id=1, source_target_pairs={{0,2},{1,3},{2,0},{3,1},{4,6},{5,7},{6,4},{7,5},{8,10},{9,11},{10,... | collective-permute-start | bytes 196616 | tf_op jit(solution)/shard_map/ppermute | solution.py:418
  4.3 2.4 %shard_map.97 = (bf16[24,4096]{1,0:T(8,128)(2,1)}, bf16[24,4096]{1,0:T(8,128)(2,1)}) custom-call(bf16[4096,128]{1,0:T(8,128)(2,1)} %bitcast.18), custom_call_target="tpu_custom_call" | custom-call | flops 40000000 | bytes 1300000 | tf_op jit(solution)/shard_map/pallas_call | solution.py:424
  6.7 1.5 %collective-permute-start.5 = (bf16[24,4096]{1,0:T(8,128)(2,1)}, bf16[24,4096]{1,0:T(8,128)(2,1)S(1)}, u32[]{:S(2)}, u32[]{:S(2)}) collective-permute-start(bf16[24,4096]{1,0:T(8,128)(2,1)} %get-tuple-element.25), channel_id=1, source_target_pairs={{0,4},{1,5},{2,6},{3,7},{4,0},{5,1},{6,2},{7,3},{8,12},{9,13},{10,... | collective-permute-start | bytes 589832 | tf_op jit(solution)/shard_map/ppermute | solution.py:411
  8.2 0.4 %collective-permute-start.6 = (bf16[24,4096]{1,0:T(8,128)(2,1)}, bf16[24,4096]{1,0:T(8,128)(2,1)S(1)}, u32[]{:S(2)}, u32[]{:S(2)}) collective-permute-start(bf16[24,4096]{1,0:T(8,128)(2,1)} %get-tuple-element.26), channel_id=1, source_target_pairs={{0,1},{1,0},{2,3},{3,2},{4,8},{5,9},{6,10},{7,11},{8,4},{9,5},{10,... | collective-permute-start | bytes 589832 | tf_op jit(solution)/shard_map/ppermute | solution.py:411
  8.7 0.2 collective-permute-done.2
  8.9 0.0 collective-permute-done
  8.9 0.0 collective-permute-done.1
  8.9 0.6 %copy-done.5 = f32[16,1024]{1,0:T(8,128)} copy-done((f32[16,1024]{1,0:T(8,128)}, f32[16,1024]{1,0:T(8,128)S(1)}, u32[]{:S(2)}) %copy-start.5) | copy-done | bytes 65560
  9.5 0.0 copy-done.3
  9.6 0.0 copy-done.4
  9.6 4.3 %shard_map.96 = (f32[3,144,256]{2,1,0:T(8,128)}, bf16[24,560]{1,0:T(8,128)(2,1)}, bf16[24,560]{1,0:T(8,128)(2,1)}) custom-call(f32[1,16,1024]{2,1,0:T(8,128)} %bitcast.33, f32[1,24,1024]{2,1,0:T(8,128)} %bitcast.24, f32[1,24,1024]{2,1,0:T(8,128)} %bitcast.28, f32[1,16,1024]{2,1,0:T(8,128)} %bitcast.35, f32[1,24,1024]{2,1,0:T(8,128)} %bitcast.25, ...), custom_call_target="tpu_custom_call" | custom-call | flops 1500000000 | bytes 1500000 | tf_op jit(solution)/shard_map/pallas_call | solution.py:453
  13.9 2.4 %collective-permute-start.3 = (bf16[24,560]{1,0:T(8,128)(2,1)}, bf16[24,560]{1,0:T(8,128)(2,1)S(1)}, u32[]{:S(2)}, u32[]{:S(2)}) collective-permute-start(bf16[24,560]{1,0:T(8,128)(2,1)} %get-tuple-element.23), channel_id=1, source_target_pairs={{0,4},{1,5},{2,6},{3,7},{4,0},{5,1},{6,2},{7,3},{8,12},{9,13},{10,... | collective-permute-start | bytes 80648 | tf_op jit(solution)/shard_map/ppermute | solution.py:411
  16.3 0.0 collective-permute-start.4
  16.3 2.1 %shard_map.98 = (bf16[576,256]{1,0:T(8,128)(2,1)}, bf16[576,256]{1,0:T(8,128)(2,1)}, bf16[3,256,48]{2,1,0:T(8,128)(2,1)}, f32[48,256]{1,0:T(8,128)}) custom-call(bf16[9,32,32]{2,1,0:T(8,128)(2,1)} %bitcast.32, bf16[9,3,32]{2,1,0:T(4,128)(2,1)} %bitcast.37), custom_call_target="tpu_custom_call" | custom-call | flops 40000000 | bytes 1000000 | tf_op jit(solution)/shard_map/pallas_call | solution.py:437
  18.4 0.0 collective-permute-done.3.refs_5_
  18.4 2.9 %collective-permute-done.4.refs_6_ = bf16[24,560]{1,0:T(8,128)(2,1)S(1)} collective-permute-done((bf16[24,560]{1,0:T(8,128)(2,1)}, bf16[24,560]{1,0:T(8,128)(2,1)S(1)}, u32[]{:S(2)}, u32[]{:S(2)}) %collective-permute-start.4) | collective-permute-done | bytes 26912 | tf_op jit(solution)/shard_map/ppermute | solution.py:411
  21.3 0.0 collective-permute-done.6.refs_9_
  21.3 0.6 %copy-done.7 = bf16[24,560]{1,0:T(8,128)(2,1)} copy-done((bf16[24,560]{1,0:T(8,128)(2,1)}, bf16[24,560]{1,0:T(8,128)(2,1)S(1)}, u32[]{:S(2)}) %copy-start.7) | copy-done | bytes 26904
  21.9 0.1 copy-done.1
  22.0 0.1 copy-done.2
  22.0 11.8 %shard_map.99 = (bf16[4096,128]{1,0:T(8,128)(2,1)}, f32[1,1,1024]{2,1,0:T(1,128)}, f32[1,1,1024]{2,1,0:T(1,128)}, f32[1,1,1024]{2,1,0:T(1,128)}, f32[1,1,1024]{2,1,0:T(1,128)}) custom-call(f32[1,16,1024]{2,1,0:T(8,128)} %bitcast.34, f32[1,24,1024]{2,1,0:T(8,128)} %bitcast.26, f32[1,24,1024]{2,1,0:T(8,128)} %bitcast.30, f32[1,16,1024]{2,1,0:T(8,128)} %bitcast.36, ...), custom_call_target="tpu_custom_call" | custom-call | flops 3000000000 | bytes 4000000 | tf_op jit(solution)/shard_map/pallas_call | solution.py:468
  33.9 0.0 copy-start
  33.9 0.1 collective-permute-start.7
  34.0 1.6 %collective-permute-start.8 = (f32[1,1,1024]{2,1,0:T(1,128)}, f32[1,1,1024]{2,1,0:T(1,128)S(1)}, u32[]{:S(2)}, u32[]{:S(2)}) collective-permute-start(f32[1,1,1024]{2,1,0:T(1,128)} %get-tuple-element.34), channel_id=1, source_target_pairs={{0,3},{1,2},{2,1},{3,0},{4,7},{5,6},{6,5},{7,4},{8,11},{9,10},{10,... | collective-permute-start | bytes 12296 | tf_op jit(solution)/shard_map/ppermute | solution.py:402
  35.6 0.5 %collective-permute-start.9 = (f32[1,1,1024]{2,1,0:T(1,128)}, f32[1,1,1024]{2,1,0:T(1,128)S(1)}, u32[]{:S(2)}, u32[]{:S(2)}) collective-permute-start(f32[1,1,1024]{2,1,0:T(1,128)} %get-tuple-element.35), channel_id=1, source_target_pairs={{0,2},{1,3},{2,0},{3,1},{4,6},{5,7},{6,4},{7,5},{8,10},{9,11},{10,... | collective-permute-start | bytes 12296 | tf_op jit(solution)/shard_map/ppermute | solution.py:493
  36.1 0.0 collective-permute-done.7
  36.1 1.2 %collective-permute-done.8 = f32[1,1,1024]{2,1,0:T(1,128)S(1)} collective-permute-done((f32[1,1,1024]{2,1,0:T(1,128)}, f32[1,1,1024]{2,1,0:T(1,128)S(1)}, u32[]{:S(2)}, u32[]{:S(2)}) %collective-permute-start.8) | collective-permute-done | bytes 4128 | tf_op jit(solution)/shard_map/ppermute | solution.py:402
  37.3 2.1 %collective-permute-done.9 = f32[1,1,1024]{2,1,0:T(1,128)S(1)} collective-permute-done((f32[1,1,1024]{2,1,0:T(1,128)}, f32[1,1,1024]{2,1,0:T(1,128)S(1)}, u32[]{:S(2)}, u32[]{:S(2)}) %collective-permute-start.9) | collective-permute-done | bytes 4128 | tf_op jit(solution)/shard_map/ppermute | solution.py:493
  39.4 0.6 %add_add_fusion = f32[1,1,1024]{2,1,0:T(1,128)} fusion(f32[1,1,1024]{2,1,0:T(1,128)S(1)} %collective-permute-done.9, f32[1,1,1024]{2,1,0:T(1,128)S(1)} %collective-permute-done.8, f32[1,1,1024]{2,1,0:T(1,128)S(1)} %copy-done, f32[1,1,1024]{2,1,0:T(1,128)S(1)} %collective-permute-done.7), kind=kLoop, calls=%fused_computation | loop fusion | flops 3072 | bytes 20480 | tf_op jit(solution)/shard_map/add | solution.py:490
  (10 shorter events, 0.0 us)
Async XLA Ops:
  2.2 6.7 %collective-permute-start = (f32[24,1024]{1,0:T(8,128)}, f32[24,1024]{1,0:T(8,128)S(1)}, u32[]{:S(2)}, u32[]{:S(2)}) collective-permute-start(f32[24,1024]{1,0:T(8,128)} %get-tuple-element.20), channel_id=1, source_target_pairs={{0,1},{1,0},{2,3},{3,2},{4,5},{5,4},{6,7},{7,6},{8,9},{9,8},{10,11... | collective-permute-start | bytes 294920 | tf_op jit(solution)/shard_map/ppermute | solution.py:402
  2.2 6.7 %collective-permute-start.1 = (f32[24,1024]{1,0:T(8,128)}, f32[24,1024]{1,0:T(8,128)S(1)}, u32[]{:S(2)}, u32[]{:S(2)}) collective-permute-start(f32[24,1024]{1,0:T(8,128)} %get-tuple-element.21), channel_id=1, source_target_pairs={{0,3},{1,2},{2,1},{3,0},{4,7},{5,6},{6,5},{7,4},{8,11},{9,10},{10,... | collective-permute-start | bytes 294920 | tf_op jit(solution)/shard_map/ppermute | solution.py:402
  3.8 5.1 %collective-permute-start.2 = (f32[16,1024]{1,0:T(8,128)}, f32[16,1024]{1,0:T(8,128)S(1)}, u32[]{:S(2)}, u32[]{:S(2)}) collective-permute-start(f32[16,1024]{1,0:T(8,128)} %get-tuple-element.19), channel_id=1, source_target_pairs={{0,2},{1,3},{2,0},{3,1},{4,6},{5,7},{6,4},{7,5},{8,10},{9,11},{10,... | collective-permute-start | bytes 196616 | tf_op jit(solution)/shard_map/ppermute | solution.py:418
  6.7 14.5 %collective-permute-start.5 = (bf16[24,4096]{1,0:T(8,128)(2,1)}, bf16[24,4096]{1,0:T(8,128)(2,1)S(1)}, u32[]{:S(2)}, u32[]{:S(2)}) collective-permute-start(bf16[24,4096]{1,0:T(8,128)(2,1)} %get-tuple-element.25), channel_id=1, source_target_pairs={{0,4},{1,5},{2,6},{3,7},{4,0},{5,1},{6,2},{7,3},{8,12},{9,13},{10,... | collective-permute-start | bytes 589832 | tf_op jit(solution)/shard_map/ppermute | solution.py:411
  8.2 13.1 %collective-permute-start.6 = (bf16[24,4096]{1,0:T(8,128)(2,1)}, bf16[24,4096]{1,0:T(8,128)(2,1)S(1)}, u32[]{:S(2)}, u32[]{:S(2)}) collective-permute-start(bf16[24,4096]{1,0:T(8,128)(2,1)} %get-tuple-element.26), channel_id=1, source_target_pairs={{0,1},{1,0},{2,3},{3,2},{4,8},{5,9},{6,10},{7,11},{8,4},{9,5},{10,... | collective-permute-start | bytes 589832 | tf_op jit(solution)/shard_map/ppermute | solution.py:411
  8.9 0.6 %copy-start.5 = (f32[16,1024]{1,0:T(8,128)}, f32[16,1024]{1,0:T(8,128)S(1)}, u32[]{:S(2)}) copy-start(f32[16,1024]{1,0:T(8,128)S(1)} %collective-permute-done.2) | copy-start | bytes 196612
  8.9 0.7 %copy-start.3 = (f32[24,1024]{1,0:T(8,128)}, f32[24,1024]{1,0:T(8,128)S(1)}, u32[]{:S(2)}) copy-start(f32[24,1024]{1,0:T(8,128)S(1)} %collective-permute-done) | copy-start | bytes 294916
  8.9 0.7 %copy-start.4 = (f32[24,1024]{1,0:T(8,128)}, f32[24,1024]{1,0:T(8,128)S(1)}, u32[]{:S(2)}) copy-start(f32[24,1024]{1,0:T(8,128)S(1)} %collective-permute-done.1) | copy-start | bytes 294916
  13.9 4.5 %collective-permute-start.3 = (bf16[24,560]{1,0:T(8,128)(2,1)}, bf16[24,560]{1,0:T(8,128)(2,1)S(1)}, u32[]{:S(2)}, u32[]{:S(2)}) collective-permute-start(bf16[24,560]{1,0:T(8,128)(2,1)} %get-tuple-element.23), channel_id=1, source_target_pairs={{0,4},{1,5},{2,6},{3,7},{4,0},{5,1},{6,2},{7,3},{8,12},{9,13},{10,... | collective-permute-start | bytes 80648 | tf_op jit(solution)/shard_map/ppermute | solution.py:411
  16.3 5.0 %collective-permute-start.4 = (bf16[24,560]{1,0:T(8,128)(2,1)}, bf16[24,560]{1,0:T(8,128)(2,1)S(1)}, u32[]{:S(2)}, u32[]{:S(2)}) collective-permute-start(bf16[24,560]{1,0:T(8,128)(2,1)} %get-tuple-element.24), channel_id=1, source_target_pairs={{0,1},{1,0},{2,3},{3,2},{4,8},{5,9},{6,10},{7,11},{8,4},{9,5},{10,... | collective-permute-start | bytes 80648 | tf_op jit(solution)/shard_map/ppermute | solution.py:411
  18.4 2.9 %copy-start.6 = (bf16[24,560]{1,0:T(8,128)(2,1)}, bf16[24,560]{1,0:T(8,128)(2,1)S(1)}, u32[]{:S(2)}) copy-start(bf16[24,560]{1,0:T(8,128)(2,1)S(1)} %collective-permute-done.3.refs_5_) | copy-start | bytes 80644
  21.3 0.6 %copy-start.7 = (bf16[24,560]{1,0:T(8,128)(2,1)}, bf16[24,560]{1,0:T(8,128)(2,1)S(1)}, u32[]{:S(2)}) copy-start(bf16[24,560]{1,0:T(8,128)(2,1)S(1)} %collective-permute-done.4.refs_6_) | copy-start | bytes 80644
  21.3 0.7 %copy-start.1 = (bf16[24,4096]{1,0:T(8,128)(2,1)}, bf16[24,4096]{1,0:T(8,128)(2,1)S(1)}, u32[]{:S(2)}) copy-start(bf16[24,4096]{1,0:T(8,128)(2,1)S(1)} %collective-permute-done.5.refs_8_) | copy-start | bytes 589828
  21.3 0.8 %copy-start.2 = (bf16[24,4096]{1,0:T(8,128)(2,1)}, bf16[24,4096]{1,0:T(8,128)(2,1)S(1)}, u32[]{:S(2)}) copy-start(bf16[24,4096]{1,0:T(8,128)(2,1)S(1)} %collective-permute-done.6.refs_9_) | copy-start | bytes 589828
  33.9 5.5 %copy-start = (f32[1,1,1024]{2,1,0:T(1,128)S(1)}, f32[1,1,1024]{2,1,0:T(1,128)}, u32[]{:S(2)}) copy-start(f32[1,1,1024]{2,1,0:T(1,128)} %get-tuple-element.32) | copy-start | bytes 12292
  33.9 2.2 %collective-permute-start.7 = (f32[1,1,1024]{2,1,0:T(1,128)}, f32[1,1,1024]{2,1,0:T(1,128)S(1)}, u32[]{:S(2)}, u32[]{:S(2)}) collective-permute-start(f32[1,1,1024]{2,1,0:T(1,128)} %get-tuple-element.33), channel_id=1, source_target_pairs={{0,1},{1,0},{2,3},{3,2},{4,5},{5,4},{6,7},{7,6},{8,9},{9,8},{10,11... | collective-permute-start | bytes 12296 | tf_op jit(solution)/shard_map/ppermute | solution.py:402
  34.0 3.3 %collective-permute-start.8 = (f32[1,1,1024]{2,1,0:T(1,128)}, f32[1,1,1024]{2,1,0:T(1,128)S(1)}, u32[]{:S(2)}, u32[]{:S(2)}) collective-permute-start(f32[1,1,1024]{2,1,0:T(1,128)} %get-tuple-element.34), channel_id=1, source_target_pairs={{0,3},{1,2},{2,1},{3,0},{4,7},{5,6},{6,5},{7,4},{8,11},{9,10},{10,... | collective-permute-start | bytes 12296 | tf_op jit(solution)/shard_map/ppermute | solution.py:402
  35.6 3.8 %collective-permute-start.9 = (f32[1,1,1024]{2,1,0:T(1,128)}, f32[1,1,1024]{2,1,0:T(1,128)S(1)}, u32[]{:S(2)}, u32[]{:S(2)}) collective-permute-start(f32[1,1,1024]{2,1,0:T(1,128)} %get-tuple-element.35), channel_id=1, source_target_pairs={{0,2},{1,3},{2,0},{3,1},{4,6},{5,7},{6,4},{7,5},{8,10},{9,11},{10,... | collective-permute-start | bytes 12296 | tf_op jit(solution)/shard_map/ppermute | solution.py:493

commit v3 on v2

--- a/solution.py
+++ b/solution.py
@@ -18,7 +18,7 @@
 GROUP = 6
 WINDOW = 8
 EDGE = 24
-VMEM = 56 * 1024 * 1024
+VMEM = 24 * 1024 * 1024
 
 NN = (((1,), (0,)), ((), ()))
 NT = (((1,), (1,)), ((), ()))
@@ -57,19 +57,26 @@
 
 def pack_body(pins, box, weight, pin, first, last, to_even, to_odd, plain):
     odd = lax.axis_index("col") % 2 == 1
-    rows = [box[...].astype(F32), weight[...]]
-    rows += [pin[p].astype(F32) for p in range(pins)]
+    span = first.shape[1]
+    row0 = lax.axis_index("strip") * span
     nets = box.shape[1]
-    used = 5 + 2 * pins
-    rows.append(jnp.zeros((FIELDS - used, nets), F32))
-    fields = jnp.concatenate(rows, axis=0)
+    x0, x1, y0, y1 = (box[k : k + 1, :] for k in range(4))
+    height = (y1 - y0 + 1).astype(F32)
+    width = (x1 - x0 + 1).astype(F32)
+    rows = [x0 // BOX, x0 % BOX, y0 - row0]
+    rows = [v.astype(F32) for v in rows]
+    rows += [width, height, weight[...] / height, weight[...] / width]
+    for p in range(pins):
+        rows += [(pin[p, 0:1, :] - y0).astype(F32), (pin[p, 1:2, :] - x0).astype(F32)]
+    rows.append(jnp.zeros((FIELDS - len(rows), nets), F32))
+    fields = jnp.concatenate(rows, axis=0).astype(BF16)
     plain[...] = fields
     to_even[0:FIELDS, :] = fields
     to_odd[0:FIELDS, :] = fields
     a, b = first[...].astype(F32), last[...].astype(F32)
     for ref, e in ((to_even, jnp.where(odd, a, b)), (to_odd, jnp.where(odd, b, a))):
         for k in range(8):
-            ref[FIELDS : FIELDS + 8, 128 * k : 128 * (k + 1)] = e[8 * k : 8 * k + 8, :]
+            ref[FIELDS : FIELDS + 8, span * k : span * (k + 1)] = e[8 * k : 8 * k + 8, :].astype(BF16)
 
 
 def cot_edge_body(cot, to_even, to_odd):
@@ -96,7 +103,7 @@
     odd = c % 2 == 1
 
     def unpack(ref):
-        e = ref[0, FIELDS : FIELDS + 8, :]
+        e = ref[0, FIELDS : FIELDS + 8, :].astype(F32)
         return jnp.concatenate([e[:, span * k : span * (k + 1)] for k in range(8)], axis=0)
 
     a, b = unpack(even_ref), unpack(odd_ref)
@@ -143,17 +150,82 @@
             first_bwd[16 * r + 8 * ch : 16 * r + 8 * ch + 8, :] = acc
 
 
-def relative(ref, m, col0, row0):
-    f = ref[m, 0:FIELDS, :]
-    x = lambda v: jnp.clip(v - (col0 - 2.0), -2.0, 250.0)
-    y = lambda v: jnp.clip(v - row0, -2.0, 250.0)
-    return f, x, y
+def spread(p, block):
+    lane = iota((block, p.shape[1]), 1)
+    low = pltpu.roll(p[0:block], p.shape[1] - 1, 1)
+    high = pltpu.roll(p[2 * block :], 1, 1)
+    last = lane == p.shape[1] - 1
+    first = lane == 0
+    same = p[block : 2 * block] + jnp.where(last, 0.0, low) + jnp.where(first, 0.0, high)
+    return same, jnp.where(last, low, 0.0) + jnp.where(first, high, 0.0)
+
+
+def window_of(ref, g, cols, chans):
+    lo, hi = (GROUP * g - 2) * chans, (GROUP * g - 2 + WINDOW) * chans
+    top = cols * chans
+    parts = []
+    if lo < 0:
+        parts.append(jnp.zeros((-lo, ref.shape[1]), BF16))
+    parts.append(ref[max(lo, 0) : min(hi, top), :])
+    if hi > top:
+        parts.append(jnp.zeros((hi - top, ref.shape[1]), BF16))
+    return parts[0] if len(parts) == 1 else jnp.concatenate(parts, axis=0)
+
+
+def back_own_body(chans, cot, bwd, same_ref, other_ref):
+    cols = cot.shape[0] // chans
+    block = GROUP * chans
+    w = bwd[...]
+    for g in range(pl.cdiv(cols + 2, GROUP)):
+        same, other = spread(dot(w, window_of(cot, g, cols, chans)), block)
+        same_ref[block * g : block * (g + 1), :] = same
+        other_ref[block * g : block * (g + 1), :] = other
+
+
+def halo_place(span):
+    strip = lax.axis_index("strip")
+    odd = strip % 2
+    has_above = (strip > 0).astype(jnp.int32)
+    has_below = (strip < lax.axis_size("strip") - 1).astype(jnp.int32)
+    m = iota((2 * EDGE, LANES), 0)
+    lane = iota((2 * EDGE, LANES), 1)
+    k = m % EDGE
+    below = (m // EDGE == odd) & (has_below == 1) & (k < REACH) & (lane == span + k)
+    above = (m // EDGE != odd) & (has_above == 1) & (lane == (k - 2) % LANES)
+    return onehot((above & (k < REACH)) | below), onehot((above & (k < 2)) | below)
+
+
+def back_halo_body(chans, cot_even, cot_odd, bwd, same_ref, other_ref, back_h, halo):
+    cols = cot_even.shape[1] // chans
+    span = same_ref.shape[1]
+    place = halo_place(span)[1][:, span:]
+    step = 512
+    for k in range(cols * chans // step):
+        s = slice(step * k, step * (k + 1))
+        ends = jnp.concatenate([cot_even[:, s], cot_odd[:, s]], axis=0)
+        halo[s, :] = dot(ends, place, TN).astype(BF16)
+    block = GROUP * chans
+    w = bwd[...]
+    for g in range(pl.cdiv(cols + 2, GROUP)):
+        same, other = spread(dot(w, window_of(halo, g, cols, chans)), block)
+        rows = slice(block * g, block * (g + 1))
+        back_h[rows, 0:span] = same_ref[rows, :] + other
+        back_h[rows, span:] = same + other_ref[rows, :]
+
+
+def relative(ref, m, col0):
+    f = ref[m, 0:FIELDS, :].astype(F32)
+    x = f[0:1] * float(BOX) + f[1:2] - (col0 - 2.0)
+    y = f[2:3]
+    width, height = f[3:4], f[4:5]
+    cut = lambda v: jnp.clip(v, -2.0, 250.0)
+    return f, x, y, cut(x), cut(x + width - 1.0), y + height - 1.0, width, height, cut
 
 
 def raster_body(pins, cols, span, n_nets, *refs):
     net_refs = refs[:n_nets]
     even_ref, odd_ref, maps, to_even, to_odd = refs[n_nets:]
-    col0, row0 = (v.astype(F32) for v in block_origin(cols, span))
+    col0 = block_origin(cols, span)[0].astype(F32)
     maps[...] = jnp.zeros_like(maps)
     nets = net_refs[0].shape[2]
     step = nets
@@ -162,19 +234,17 @@
     zero = jnp.zeros((), BF16)
 
     def chunk(ref, m):
-        f, x, y = relative(ref, m, col0, row0)
-        x0, x1 = x(f[0:1]).astype(BF16), x(f[1:2]).astype(BF16)
-        y0, y1 = y(f[2:3]).astype(BF16), y(f[3:4]).astype(BF16)
-        vh = (f[4:5] / (f[3:4] - f[2:3] + 1.0)).astype(BF16)
-        vv = (f[4:5] / (f[1:2] - f[0:1] + 1.0)).astype(BF16)
+        f, x, y, x0, x1, y1, width, height, cut = relative(ref, m, col0)
+        x0, x1, y0, y1 = x0.astype(BF16), x1.astype(BF16), y.astype(BF16), y1.astype(BF16)
+        vh, vv = f[5:6].astype(BF16), f[6:7].astype(BF16)
         in_col = (x0 <= jcol) & (jcol <= x1)
         in_row = jnp.where((y0 <= jcol) & (jcol <= y1), one, zero)
         maps[0, :, 0:NROWS] += dot(jnp.where(in_col, vh, zero), in_row, NT)
         maps[1, :, 0:NROWS] += dot(jnp.where(in_col, vv, zero), in_row, NT)
         acc = jnp.zeros((JCOLS, NROWS), F32)
         for p in range(pins):
-            py = y(f[5 + 2 * p : 6 + 2 * p]).astype(BF16)
-            px = x(f[6 + 2 * p : 7 + 2 * p]).astype(BF16)
+            py = (y + f[7 + 2 * p : 8 + 2 * p]).astype(BF16)
+            px = cut(x + f[8 + 2 * p : 9 + 2 * p]).astype(BF16)
             acc += dot(
                 jnp.where(px == jcol, one, zero), jnp.where(py == jcol, one, zero), NT
             )
@@ -204,80 +274,46 @@
 ):
     net_refs = refs[:n_nets]
     (
-        maps, from_even, from_odd, cot, cot_even, cot_odd, even_ref, odd_ref,
+        maps, from_even, from_odd, back_h, even_ref, odd_ref,
         fwd, bwd, first_fwd, first_bwd, bias1, bias2,
-    ) = refs[n_nets : 14 + n_nets]
-    rest = refs[14 + n_nets :]
+    ) = refs[n_nets : 12 + n_nets]
+    rest = refs[12 + n_nets :]
     congestion = rest[0]
     grads = rest[1 : 1 + n_nets]
-    cotx, feats, back_h, hid, back_p, grad_maps = rest[1 + n_nets :]
+    feats, hid, back_p, grad_maps = rest[1 + n_nets :]
     chans = bias1.shape[1]
-    span = cot.shape[1]
-    cols = cot.shape[0] // chans
+    span = congestion.shape[1]
+    cols = congestion.shape[0] // chans
     col0, row0 = block_origin(cols, span)
     all_cols = cols * lax.axis_size("col")
     all_rows = span * lax.axis_size("strip")
-    strip = lax.axis_index("strip")
-    odd = strip % 2
-    has_above = (strip > 0).astype(jnp.int32)
-    has_below = (strip < lax.axis_size("strip") - 1).astype(jnp.int32)
     left_cols, right_cols = side_columns(even_ref, odd_ref, span)
     n = 3 * JCOLS
 
     e = jnp.concatenate([from_even[...], from_odd[...]], axis=0)
-    m = iota((2 * EDGE, LANES), 0)
-    lane = iota((2 * EDGE, LANES), 1)
-    k = m % EDGE
-    below = (m // EDGE == odd) & (has_below == 1)
-    above = (m // EDGE != odd) & (has_above == 1)
-    place = onehot(
-        (above & (k < REACH) & (lane == (k - 2) % LANES))
-        | (below & (k < REACH) & (lane == span + k))
-    )
-    side_place = onehot(
-        (above & (k < 2) & (lane == (k - 2) % LANES))
-        | (below & (k < REACH) & (lane == span + k))
-    )
+    place, side_place = halo_place(span)
     total = maps[...].reshape(n, LANES) + dot(e[:, 0:n], place, TN)
     total = total.astype(BF16).astype(F32).reshape(3, JCOLS, LANES)
     feats[1] = total
     feats[0] = pltpu.roll(total, 1, 2)
     feats[2] = pltpu.roll(total, LANES - 1, 2)
 
-    place2 = side_place[:, span:]
-    first_row = 2 * chans
-    cotx[first_row : first_row + cols * chans, 0:span] = cot[...]
-    step = 512
-    for k in range(cols * chans // step):
-        s = slice(step * k, step * (k + 1))
-        ends = jnp.concatenate([cot_even[:, s], cot_odd[:, s]], axis=0)
-        cotx[first_row + step * k : first_row + step * (k + 1), span:LANES] = dot(
-            ends, place2, TN
-        ).astype(BF16)
-    edge_place = dot(e[:, n:], side_place, TN).astype(BF16)
-    tail = first_row + cols * chans
-    cotx[0:first_row, 0:span] = left_cols
-    cotx[0:first_row, span:LANES] = edge_place[0:first_row, span:LANES]
-    cotx[tail : tail + first_row, 0:span] = right_cols
-    cotx[tail : tail + first_row, span:LANES] = edge_place[first_row : 2 * first_row, span:LANES]
-    cotx[tail + first_row :, :] = jnp.zeros((cotx.shape[0] - tail - first_row, LANES), BF16)
-
+    edge = 2 * chans
     block = GROUP * chans
     window = WINDOW * chans
-    groups = pl.cdiv(cols + 2, GROUP)
-    back_h[groups * block :, :] = jnp.zeros((back_h.shape[0] - groups * block, LANES), F32)
-
-    def step_a(g, carry):
-        lo = pl.multiple_of(g * block, block)
-        p = dot(bwd[...], cotx[pl.ds(lo, window), :])
-        back_h[pl.ds(lo, block), :] = (
-            p[block : 2 * block]
-            + pltpu.roll(p[0:block], LANES - 1, 1)
-            + pltpu.roll(p[2 * block :], 1, 1)
+    outer = dot(e[:, n:], side_place, TN).astype(BF16)
+    fixes = []
+    for k, main in enumerate((left_cols, right_cols)):
+        ext = jnp.concatenate([main, outer[edge * k : edge * (k + 1), span:]], axis=1)
+        taps = jnp.concatenate(
+            [bwd[block * r : block * r + edge, edge * k : edge * (k + 1)] for r in range(3)], axis=0
         )
-        return carry
-
-    lax.fori_loop(0, groups, step_a, 0, unroll=True)
+        p = dot(taps, ext)
+        fixes.append(
+            p[edge : 2 * edge]
+            + pltpu.roll(p[0:edge], LANES - 1, 1)
+            + pltpu.roll(p[2 * edge :], 1, 1)
+        )
 
     lanes1 = iota((1, LANES), 1)
     row_of = jnp.where(lanes1 < LANES - 64, lanes1, lanes1 - LANES)
@@ -287,13 +323,13 @@
     bias_rep = jnp.concatenate([bias_col] * 8, axis=0)
     jo_rows = iota((8 * chans, 1), 0) // chans
 
-    def step_b(g, carry):
-        lo8 = pl.multiple_of(g * 8, 8)
+    def step_b(g):
+        lo8 = g * 8
         pre = bias_rep
         for r in range(3):
             f = feats[r, :, pl.ds(lo8, 16), :].reshape(3 * 16, LANES).astype(BF16)
             pre = pre + dot(first_fwd[r], f)
-        lo = pl.multiple_of(g * 8 * chans, 8 * chans)
+        lo = g * 8 * chans
         slot = 8 * g + 1 + jo_rows
         gcol = slot - 2 + col0
         col_ok = (slot <= cols + 2) & (gcol >= 0) & (gcol < all_cols)
@@ -302,11 +338,14 @@
         h = pre * s
         slope = s + h * (1.0 - s)
         bh = back_h[pl.ds(lo, 8 * chans), :]
+        if g in (0, cols // 8):
+            fix = fixes[0 if g == 0 else 1]
+            bh = jnp.concatenate([bh[0:edge] + fix, bh[edge:]], axis=0)
         hid[pl.ds(lo, 8 * chans), :] = jnp.where(ok, h, 0.0).astype(BF16)
         back_p[pl.ds(lo, 8 * chans), :] = jnp.where(ok, bh * slope, 0.0).astype(BF16)
-        return carry
-
-    lax.fori_loop(0, pl.cdiv(cols + 2, 8), step_b, 0, unroll=True)
+
+    for g in range(pl.cdiv(cols + 2, 8)):
+        step_b(g)
 
     bias_out = jnp.concatenate([bias2[...].T] * GROUP, axis=0)
     groups_c = pl.cdiv(cols, GROUP)
@@ -344,21 +383,19 @@
     slot = jnp.where((x_rows % 8 < GROUP) & (slot < cols + 2), slot, 512).astype(F32)
     nets = net_refs[0].shape[2]
     fcol = col0.astype(F32)
-    frow = row0.astype(F32)
     rows = iota((NROWS, nets), 0).astype(F32).astype(BF16)
     one = jnp.ones((), BF16)
     zero = jnp.zeros((), BF16)
 
     def net_chunk(ref, out, k):
-        f, x, y = relative(ref, k, fcol, frow)
-        y0, y1 = y(f[2:3]).astype(BF16), y(f[3:4]).astype(BF16)
+        f, x, y, x0, x1, y1, width, height, cut = relative(ref, k, fcol)
+        y0, y1 = y.astype(BF16), y1.astype(BF16)
         in_row = jnp.where((y0 <= rows) & (rows <= y1), one, zero)
         h = dot(grad_maps[:, 0:NROWS], in_row).reshape(groups_c, 2, 8, nets)
-        x0, x1 = x(f[0:1]), x(f[1:2])
         in_col = ((x0 <= slot) & (slot <= x1)).reshape(groups_c, 8, nets)
         s0 = jnp.sum(jnp.sum(jnp.where(in_col, h[:, 0], 0.0), axis=0), axis=0, keepdims=True)
         s1 = jnp.sum(jnp.sum(jnp.where(in_col, h[:, 1], 0.0), axis=0), axis=0, keepdims=True)
-        out[k, 0:1, :] = s0 / (f[3:4] - f[2:3] + 1.0) + s1 / (f[1:2] - f[0:1] + 1.0)
+        out[k, 0:1, :] = s0 / height + s1 / width
 
     for ref, out in zip(net_refs, grads):
         if ref.shape[0] == 1:
@@ -388,9 +425,9 @@
         in_specs=[full(4, nets), full(1, nets), full(pins, 2, nets), one_block, last_block],
         out_specs=[full(FIELDS + 8, nets), full(FIELDS + 8, nets), full(FIELDS, nets)],
         out_shape=[
-            jax.ShapeDtypeStruct((FIELDS + 8, nets), F32),
-            jax.ShapeDtypeStruct((FIELDS + 8, nets), F32),
-            jax.ShapeDtypeStruct((FIELDS, nets), F32),
+            jax.ShapeDtypeStruct((FIELDS + 8, nets), BF16),
+            jax.ShapeDtypeStruct((FIELDS + 8, nets), BF16),
+            jax.ShapeDtypeStruct((FIELDS, nets), BF16),
         ],
         cost_estimate=cost(10000, 400000),
     )(net_box.T, net_weight.reshape(1, nets), pin_bin.transpose(1, 2, 0), cot, cot)
@@ -429,7 +466,7 @@
         ],
         1,
         cost=cost(40000000, 1300000),
-    )(cot)
+    )(lax.optimization_barrier((cot, plain))[0])
     cot_even = swap_strip(cot_to_even, 0)
     cot_odd = swap_strip(cot_to_odd, 1)
 
@@ -449,6 +486,13 @@
         conv_first.reshape(9, chans, cin).transpose(0, 2, 1),
     )
 
+    hidden_rows = GROUP * pl.cdiv(cols + 2, GROUP) * chans
+    own = call(
+        functools.partial(back_own_body, chans),
+        [jax.ShapeDtypeStruct((hidden_rows, span), F32)] * 2,
+        2,
+        cost=cost(2000000000, 1000000),
+    )(cot, weights[1])
     width = 3 * JCOLS + 2 * edge
     maps, edge_even, edge_odd = call(
         functools.partial(raster_body, pins, cols, span, len(groups)),
@@ -464,23 +508,29 @@
     from_even = swap_strip(edge_even, 0)
     from_odd = swap_strip(edge_odd, 1)
 
-    rows_x = (cols + 16) * chans
+    rows_x = 8 * pl.cdiv(cols + 2, 8) * chans
+    back_h = call(
+        functools.partial(back_halo_body, chans),
+        jax.ShapeDtypeStruct((rows_x, LANES), F32),
+        5,
+        scratch=[pltpu.VMEM((cols * chans, span), BF16)],
+        cost=cost(2000000000, 1000000),
+    )(cot_even, cot_odd, weights[1], *own)
+
     outs = call(
         functools.partial(network_body, pins, len(groups)),
         [jax.ShapeDtypeStruct((cols * chans, span), BF16)]
         + [jax.ShapeDtypeStruct((g.shape[0], 1, nets), F32) for g in groups],
-        len(groups) + 14,
+        len(groups) + 12,
         scratch=[
-            pltpu.VMEM((rows_x, LANES), BF16),
             pltpu.VMEM((3, 3, JCOLS, LANES), F32),
-            pltpu.VMEM((rows_x, LANES), F32),
             pltpu.VMEM((rows_x, LANES), BF16),
             pltpu.VMEM((rows_x, LANES), BF16),
             pltpu.VMEM((16 * pl.cdiv(cols, GROUP), LANES), BF16),
         ],
         cost=cost(3000000000, 4000000),
     )(
-        *groups, maps, from_even, from_odd, cot, cot_even, cot_odd, *sides, *weights,
+        *groups, maps, from_even, from_odd, back_h, *sides, *weights,
         bias_first.reshape(1, chans), bias_second.reshape(1, chans),
     )
     congestion = outs[0].reshape(cols, chans, span)

time: 40.3 us -> 32.9 us (0.82)
  Pallas kernels: 22.2 us -> 16.9 us
  local copies, waits for them, and re-layouts: 1.42 us -> 0.03 us
  waiting for transfers between devices: 6.41 us -> 5.51 us
    pallas_call x0 -> x2, Pallas kernels: none -> 4.28 us  [the longest x1 2.35 us: shards(): call(functools.partial(back_halo_body, chans), jax.ShapeDtypeStruct((rows...]
    pallas_call x1, Pallas kernels: 11.8 us -> 7.58 us  [shards(): call(functools.partial(network_body, pins, len(groups)), [jax.ShapeDtypeS...]
    pallas_call x1, Pallas kernels: 2.43 us -> 0.47 us  [shards(): call(cot_edge_body, [jax.ShapeDtypeStruct((EDGE, cols * chans), BF16), ja...]
    ppermute x4, starting transfers between devices: 3.34 us -> 1.53 us  [swap_col(): lax.ppermute(x, 'col', [(i, swapped(i, ncol, phase)) for i in range(ncol)])]
    pallas_call x1, Pallas kernels: 2.14 us -> 0.39 us  [shards(): call(weight_body, [jax.ShapeDtypeStruct((3 * GROUP * chans, WINDOW * chan...]
    pallas_call x1, Pallas kernels: 4.3 us -> 2.56 us  [shards(): call(functools.partial(raster_body, pins, cols, span, len(groups)), [jax....]
    unnamed x16 -> x12, local copies, waits for them, and re-layouts: 1.42 us -> 0.03 us
    ppermute x1, starting transfers between devices: 0.51 us -> 1.52 us  [shards(): far = lax.ppermute(plain, 'col', opposite)]
  transfers between devices with their start and end apart: 10 -> 10, of which waited for: 4 -> 4; matrix products, arithmetic and copies ran while one was open for 0% -> 0% of each run, Pallas kernels for 22% -> 24%
where the time goes in v3:
time: 32.9 us; the launch traced here: 32.7 us
  Pallas kernels  16.9 us (51%)
  starting transfers between devices  8.91 us (27%)
  waiting for transfers between devices  5.51 us (17%)
  between operations  0.75 us (2%)
  other arithmetic  0.6 us (2%)
    pallas_call x1, Pallas kernels, shards(): call(functools.partial(network_body, pins, len(groups)), [jax.ShapeDtypeS...  7.58 us
    ppermute x4, starting transfers between devices, swap_strip(): return lax.ppermute(x, ('strip', 'col'), pairs)  4.63 us
    pallas_call x1, Pallas kernels, shards(): call(functools.partial(raster_body, pins, cols, span, len(groups)), [jax....  2.56 us
    ppermute x4, waiting for transfers between devices, swap_strip(): return lax.ppermute(x, ('strip', 'col'), pairs)  2.39 us
    pallas_call x1, Pallas kernels, shards(): call(functools.partial(back_halo_body, chans), jax.ShapeDtypeStruct((rows...  2.35 us
    pallas_call x1, Pallas kernels, shards(): call(functools.partial(back_own_body, chans), [jax.ShapeDtypeStruct((hidd...  1.93 us
    ppermute x4, waiting for transfers between devices, swap_col(): lax.ppermute(x, 'col', [(i, swapped(i, ncol, phase)) for i in range(ncol)])  1.64 us
    pallas_call x1, Pallas kernels, shards(): pl.pallas_call(functools.partial(pack_body, pins), grid=(1,), in_specs=[f...  1.59 us
  transfers between devices with their start and end apart: 10, of which 4 were waited for; matrix products, arithmetic and copies ran while one was open for 0% of the time, Pallas kernels for 24%

profile of v3, /device:TPU:16, one launch (start us, length us, event | category | flops | bytes accessed | tf_op | source)
XLA Modules:
  0.0 32.7 jit_solution(8468766431753438390)
XLA Ops:
  0.7 1.6 %shard_map.95 = (bf16[24,1024]{1,0:T(8,128)(2,1)}, bf16[24,1024]{1,0:T(8,128)(2,1)}, bf16[16,1024]{1,0:T(8,128)(2,1)}) custom-call(s32[4,1024]{1,0:T(4,128)} %bitcast.37, f32[1,1024]{1,0:T(1,128)} %bitcast.38, s32[4,2,1024]{2,1,0:T(2,128)} %bitcast.36, bf16[4096,128]{1,0:T(8,128)(2,1)} %bitcast.16, bf16[4096,128]{1,0:T(8,128)(2,1)} %bitcast.17), custom_call_target="tpu_custom_call" | custom-call | flops 10000 | bytes 400000 | tf_op jit(solution)/shard_map/pallas_call | solution.py:422
  2.3 1.5 %collective-permute-start.2 = (bf16[16,1024]{1,0:T(8,128)(2,1)}, bf16[16,1024]{1,0:T(8,128)(2,1)S(1)}, u32[]{:S(2)}, u32[]{:S(2)}) collective-permute-start(bf16[16,1024]{1,0:T(8,128)(2,1)} %get-tuple-element.22), channel_id=1, source_target_pairs={{0,2},{1,3},{2,0},{3,1},{4,6},{5,7},{6,4},{7,5},{8,10},{9,11},{10,... | collective-permute-start | bytes 98312 | tf_op jit(solution)/shard_map/ppermute | solution.py:455
  3.8 0.5 %shard_map.97 = (bf16[24,4096]{1,0:T(8,128)(2,1)S(1)}, bf16[24,4096]{1,0:T(8,128)(2,1)S(1)}) custom-call(bf16[4096,128]{1,0:T(8,128)(2,1)S(1)} %bitcast.18), custom_call_target="tpu_custom_call" | custom-call | flops 40000000 | bytes 1300000 | tf_op jit(solution)/shard_map/pallas_call | solution.py:461
  4.3 1.6 %collective-permute-start.5 = (bf16[24,4096]{1,0:T(8,128)(2,1)S(1)}, bf16[24,4096]{1,0:T(8,128)(2,1)S(1)}, u32[]{:S(2)}, u32[]{:S(2)}) collective-permute-start(bf16[24,4096]{1,0:T(8,128)(2,1)S(1)} %get-tuple-element.29), channel_id=1, source_target_pairs={{0,4},{1,5},{2,6},{3,7},{4,0},{5,1},{6,2},{7,3},{8,12},{9,13},{10,... | collective-permute-start | bytes 589832 | tf_op jit(solution)/shard_map/ppermute | solution.py:448
  5.8 0.4 %collective-permute-start.6 = (bf16[24,4096]{1,0:T(8,128)(2,1)S(1)}, bf16[24,4096]{1,0:T(8,128)(2,1)S(1)}, u32[]{:S(2)}, u32[]{:S(2)}) collective-permute-start(bf16[24,4096]{1,0:T(8,128)(2,1)S(1)} %get-tuple-element.30), channel_id=1, source_target_pairs={{0,1},{1,0},{2,3},{3,2},{4,8},{5,9},{6,10},{7,11},{8,4},{9,5},{10,... | collective-permute-start | bytes 589832 | tf_op jit(solution)/shard_map/ppermute | solution.py:448
  6.2 0.0 collective-permute-start
  6.2 0.6 %collective-permute-start.1 = (bf16[24,1024]{1,0:T(8,128)(2,1)}, bf16[24,1024]{1,0:T(8,128)(2,1)S(1)}, u32[]{:S(2)}, u32[]{:S(2)}) collective-permute-start(bf16[24,1024]{1,0:T(8,128)(2,1)} %get-tuple-element.24), channel_id=1, source_target_pairs={{0,3},{1,2},{2,1},{3,0},{4,7},{5,6},{6,5},{7,4},{8,11},{9,10},{10,... | collective-permute-start | bytes 147464 | tf_op jit(solution)/shard_map/ppermute | solution.py:439
  6.9 0.0 copy-done.1
  6.9 0.4 %shard_map.98 = (bf16[576,256]{1,0:T(8,128)(2,1)S(1)}, bf16[576,256]{1,0:T(8,128)(2,1)S(1)}, bf16[3,256,48]{2,1,0:T(8,128)(2,1)S(1)}, f32[48,256]{1,0:T(8,128)S(1)}) custom-call(bf16[9,32,32]{2,1,0:T(8,128)(2,1)S(1)} %bitcast.20, bf16[9,3,32]{2,1,0:T(4,128)(2,1)S(1)} %bitcast.33), custom_call_target="tpu_custom_call" | custom-call | flops 40000000 | bytes 1000000 | tf_op jit(solution)/shard_map/pallas_call | solution.py:474
  7.3 1.9 %shard_map.99 = (f32[4224,128]{1,0:T(8,128)S(1)}, f32[4224,128]{1,0:T(8,128)S(1)}) custom-call(bf16[4096,128]{1,0:T(8,128)(2,1)S(1)} %bitcast.19, bf16[576,256]{1,0:T(8,128)(2,1)S(1)} %get-tuple-element.31.bwd.refs_11_), custom_call_target="tpu_custom_call" | custom-call | flops 2000000000 | bytes 1000000 | tf_op jit(solution)/shard_map/pallas_call | solution.py:490
  9.2 0.0 collective-permute-done.2
  9.2 0.0 collective-permute-done
  9.2 0.7 %collective-permute-done.1 = bf16[24,1024]{1,0:T(8,128)(2,1)S(1)} collective-permute-done((bf16[24,1024]{1,0:T(8,128)(2,1)}, bf16[24,1024]{1,0:T(8,128)(2,1)S(1)}, u32[]{:S(2)}, u32[]{:S(2)}) %collective-permute-start.1) | collective-permute-done | bytes 49184 | tf_op jit(solution)/shard_map/ppermute | solution.py:439
  10.0 2.6 %shard_map.96 = (f32[3,144,256]{2,1,0:T(8,128)S(1)}, bf16[24,560]{1,0:T(8,128)(2,1)S(1)}, bf16[24,560]{1,0:T(8,128)(2,1)S(1)}) custom-call(bf16[1,16,1024]{2,1,0:T(8,128)(2,1)S(1)} %bitcast.29, bf16[1,24,1024]{2,1,0:T(8,128)(2,1)S(1)} %bitcast.21, bf16[1,24,1024]{2,1,0:T(8,128)(2,1)S(1)} %bitcast.25, bf16[1,16,1024]{2,1,0:T(8,128)(2,1)S(1)} %bitcast.31, ...), custom_call_target="tpu_custom_call" | custom-call | flops 1500000000 | bytes 1500000 | tf_op jit(solution)/shard_map/pallas_call | solution.py:497
  12.5 2.7 %collective-permute-start.3 = (bf16[24,560]{1,0:T(8,128)(2,1)S(1)}, bf16[24,560]{1,0:T(8,128)(2,1)S(1)}, u32[]{:S(2)}, u32[]{:S(2)}) collective-permute-start(bf16[24,560]{1,0:T(8,128)(2,1)S(1)} %get-tuple-element.26), channel_id=1, source_target_pairs={{0,4},{1,5},{2,6},{3,7},{4,0},{5,1},{6,2},{7,3},{8,12},{9,13},{10,... | collective-permute-start | bytes 80648 | tf_op jit(solution)/shard_map/ppermute | solution.py:448
  15.2 0.0 collective-permute-start.4
  15.2 0.0 collective-permute-done.5.cot_even
  15.2 0.0 collective-permute-done.6.cot_odd
  15.2 0.0 copy-start.4
  15.2 0.0 copy-start.5
  15.2 2.4 %shard_map.100.refs_7_ = f32[4352,256]{1,0:T(8,128)S(1)} custom-call(bf16[24,4096]{1,0:T(8,128)(2,1)S(1)} %collective-permute-done.5.cot_even, bf16[24,4096]{1,0:T(8,128)(2,1)S(1)} %collective-permute-done.6.cot_odd, bf16[576,256]{1,0:T(8,128)(2,1)S(1)} %get-tuple-element.31.bwd.refs_11_, f32[4224,128]{1,0:T(8,128)S(1)} %get-tuple-element.32.same_ref, ...), custom_call_target="tpu_custom_call" | custom-call | flops 2000000000 | bytes 1000000 | tf_op jit(solution)/shard_map/pallas_call | solution.py:512
  17.6 0.0 collective-permute-done.3.refs_5_
  17.6 2.4 %collective-permute-done.4.refs_6_ = bf16[24,560]{1,0:T(8,128)(2,1)S(1)} collective-permute-done((bf16[24,560]{1,0:T(8,128)(2,1)S(1)}, bf16[24,560]{1,0:T(8,128)(2,1)S(1)}, u32[]{:S(2)}, u32[]{:S(2)}) %collective-permute-start.4) | collective-permute-done | bytes 26912 | tf_op jit(solution)/shard_map/ppermute | solution.py:448
  20.0 0.0 copy-done.5
  20.0 7.6 %shard_map.101 = (bf16[4096,128]{1,0:T(8,128)(2,1)}, f32[1,1,1024]{2,1,0:T(1,128)S(1)}, f32[1,1,1024]{2,1,0:T(1,128)S(1)}, f32[1,1,1024]{2,1,0:T(1,128)S(1)}, f32[1,1,1024]{2,1,0:T(1,128)S(1)}) custom-call(bf16[1,16,1024]{2,1,0:T(8,128)(2,1)S(1)} %bitcast.30, bf16[1,24,1024]{2,1,0:T(8,128)(2,1)S(1)} %bitcast.23, bf16[1,24,1024]{2,1,0:T(8,128)(2,1)S(1)} %bitcast.27, ...), custom_call_target="tpu_custom_call" | custom-call | flops 3000000000 | bytes 4000000 | tf_op jit(solution)/shard_map/pallas_call | solution.py:520
  27.6 0.0 collective-permute-start.7
  27.6 0.9 %collective-permute-start.8 = (f32[1,1,1024]{2,1,0:T(1,128)S(1)}, f32[1,1,1024]{2,1,0:T(1,128)S(1)}, u32[]{:S(2)}, u32[]{:S(2)}) collective-permute-start(f32[1,1,1024]{2,1,0:T(1,128)S(1)} %get-tuple-element.40), channel_id=1, source_target_pairs={{0,3},{1,2},{2,1},{3,0},{4,7},{5,6},{6,5},{7,4},{8,11},{9,10},{10,... | collective-permute-start | bytes 12296 | tf_op jit(solution)/shard_map/ppermute | solution.py:439
  28.5 1.2 %collective-permute-start.9 = (f32[1,1,1024]{2,1,0:T(1,128)S(1)}, f32[1,1,1024]{2,1,0:T(1,128)S(1)}, u32[]{:S(2)}, u32[]{:S(2)}) collective-permute-start(f32[1,1,1024]{2,1,0:T(1,128)S(1)} %get-tuple-element.41), channel_id=1, source_target_pairs={{0,2},{1,3},{2,0},{3,1},{4,6},{5,7},{6,4},{7,5},{8,10},{9,11},{10,... | collective-permute-start | bytes 12296 | tf_op jit(solution)/shard_map/ppermute | solution.py:543
  29.7 0.0 collective-permute-done.7
  29.7 0.9 %collective-permute-done.8 = f32[1,1,1024]{2,1,0:T(1,128)S(1)} collective-permute-done((f32[1,1,1024]{2,1,0:T(1,128)S(1)}, f32[1,1,1024]{2,1,0:T(1,128)S(1)}, u32[]{:S(2)}, u32[]{:S(2)}) %collective-permute-start.8) | collective-permute-done | bytes 4128 | tf_op jit(solution)/shard_map/ppermute | solution.py:439
  30.6 1.5 %collective-permute-done.9 = f32[1,1,1024]{2,1,0:T(1,128)S(1)} collective-permute-done((f32[1,1,1024]{2,1,0:T(1,128)S(1)}, f32[1,1,1024]{2,1,0:T(1,128)S(1)}, u32[]{:S(2)}, u32[]{:S(2)}) %collective-permute-start.9) | collective-permute-done | bytes 4128 | tf_op jit(solution)/shard_map/ppermute | solution.py:543
  32.1 0.6 %add_add_fusion = f32[1,1,1024]{2,1,0:T(1,128)} fusion(f32[1,1,1024]{2,1,0:T(1,128)S(1)} %collective-permute-done.9, f32[1,1,1024]{2,1,0:T(1,128)S(1)} %collective-permute-done.8, f32[1,1,1024]{2,1,0:T(1,128)S(1)} %get-tuple-element.38, f32[1,1,1024]{2,1,0:T(1,128)S(1)} %collective-permute-done.7), kind=kLoop, calls=%fused_computation | loop fusion | flops 3072 | bytes 20480 | tf_op jit(solution)/shard_map/add | solution.py:540
  (8 shorter events, 0.0 us)
Async XLA Ops:
  0.6 3.1 %copy-start = (bf16[128,32,128]{2,1,0:T(8,128)(2,1)S(1)}, bf16[128,32,128]{2,1,0:T(8,128)(2,1)}, u32[]{:S(2)}) copy-start(bf16[128,32,128]{2,1,0:T(8,128)(2,1)} %param.15) | copy-start | bytes 3145732
  0.6 6.2 %copy-start.3 = (bf16[3,3,32,3]{2,3,1,0:T(4,128)(2,1)S(1)}, bf16[3,3,32,3]{2,3,1,0:T(4,128)(2,1)}, u32[]{:S(2)}) copy-start(bf16[3,3,32,3]{2,3,1,0:T(4,128)(2,1)} %param.11) | copy-start | bytes 5188
  0.7 6.2 %copy-start.1 = (bf16[3,3,32,32]{3,2,1,0:T(8,128)(2,1)S(1)}, bf16[3,3,32,32]{3,2,1,0:T(8,128)(2,1)}, u32[]{:S(2)}) copy-start(bf16[3,3,32,32]{3,2,1,0:T(8,128)(2,1)} %param.13) | copy-start | bytes 55300
  2.3 6.9 %collective-permute-start.2 = (bf16[16,1024]{1,0:T(8,128)(2,1)}, bf16[16,1024]{1,0:T(8,128)(2,1)S(1)}, u32[]{:S(2)}, u32[]{:S(2)}) collective-permute-start(bf16[16,1024]{1,0:T(8,128)(2,1)} %get-tuple-element.22), channel_id=1, source_target_pairs={{0,2},{1,3},{2,0},{3,1},{4,6},{5,7},{6,4},{7,5},{8,10},{9,11},{10,... | collective-permute-start | bytes 98312 | tf_op jit(solution)/shard_map/ppermute | solution.py:455
  4.3 10.9 %collective-permute-start.5 = (bf16[24,4096]{1,0:T(8,128)(2,1)S(1)}, bf16[24,4096]{1,0:T(8,128)(2,1)S(1)}, u32[]{:S(2)}, u32[]{:S(2)}) collective-permute-start(bf16[24,4096]{1,0:T(8,128)(2,1)S(1)} %get-tuple-element.29), channel_id=1, source_target_pairs={{0,4},{1,5},{2,6},{3,7},{4,0},{5,1},{6,2},{7,3},{8,12},{9,13},{10,... | collective-permute-start | bytes 589832 | tf_op jit(solution)/shard_map/ppermute | solution.py:448
  5.8 9.4 %collective-permute-start.6 = (bf16[24,4096]{1,0:T(8,128)(2,1)S(1)}, bf16[24,4096]{1,0:T(8,128)(2,1)S(1)}, u32[]{:S(2)}, u32[]{:S(2)}) collective-permute-start(bf16[24,4096]{1,0:T(8,128)(2,1)S(1)} %get-tuple-element.30), channel_id=1, source_target_pairs={{0,1},{1,0},{2,3},{3,2},{4,8},{5,9},{6,10},{7,11},{8,4},{9,5},{10,... | collective-permute-start | bytes 589832 | tf_op jit(solution)/shard_map/ppermute | solution.py:448
  6.2 3.0 %collective-permute-start = (bf16[24,1024]{1,0:T(8,128)(2,1)}, bf16[24,1024]{1,0:T(8,128)(2,1)S(1)}, u32[]{:S(2)}, u32[]{:S(2)}) collective-permute-start(bf16[24,1024]{1,0:T(8,128)(2,1)} %get-tuple-element.23), channel_id=1, source_target_pairs={{0,1},{1,0},{2,3},{3,2},{4,5},{5,4},{6,7},{7,6},{8,9},{9,8},{10,11... | collective-permute-start | bytes 147464 | tf_op jit(solution)/shard_map/ppermute | solution.py:439
  6.2 3.7 %collective-permute-start.1 = (bf16[24,1024]{1,0:T(8,128)(2,1)}, bf16[24,1024]{1,0:T(8,128)(2,1)S(1)}, u32[]{:S(2)}, u32[]{:S(2)}) collective-permute-start(bf16[24,1024]{1,0:T(8,128)(2,1)} %get-tuple-element.24), channel_id=1, source_target_pairs={{0,3},{1,2},{2,1},{3,0},{4,7},{5,6},{6,5},{7,4},{8,11},{9,10},{10,... | collective-permute-start | bytes 147464 | tf_op jit(solution)/shard_map/ppermute | solution.py:439
  7.3 2.7 %copy-start.2 = (bf16[16,1024]{1,0:T(8,128)(2,1)S(1)}, bf16[16,1024]{1,0:T(8,128)(2,1)}, u32[]{:S(2)}) copy-start(bf16[16,1024]{1,0:T(8,128)(2,1)} %get-tuple-element.22) | copy-start | bytes 98308
  12.5 5.1 %collective-permute-start.3 = (bf16[24,560]{1,0:T(8,128)(2,1)S(1)}, bf16[24,560]{1,0:T(8,128)(2,1)S(1)}, u32[]{:S(2)}, u32[]{:S(2)}) collective-permute-start(bf16[24,560]{1,0:T(8,128)(2,1)S(1)} %get-tuple-element.26), channel_id=1, source_target_pairs={{0,4},{1,5},{2,6},{3,7},{4,0},{5,1},{6,2},{7,3},{8,12},{9,13},{10,... | collective-permute-start | bytes 80648 | tf_op jit(solution)/shard_map/ppermute | solution.py:448
  15.2 4.8 %collective-permute-start.4 = (bf16[24,560]{1,0:T(8,128)(2,1)S(1)}, bf16[24,560]{1,0:T(8,128)(2,1)S(1)}, u32[]{:S(2)}, u32[]{:S(2)}) collective-permute-start(bf16[24,560]{1,0:T(8,128)(2,1)S(1)} %get-tuple-element.27), channel_id=1, source_target_pairs={{0,1},{1,0},{2,3},{3,2},{4,8},{5,9},{6,10},{7,11},{8,4},{9,5},{10,... | collective-permute-start | bytes 80648 | tf_op jit(solution)/shard_map/ppermute | solution.py:448
  15.2 4.8 %copy-start.4 = (f32[32]{0:T(128)S(1)}, f32[32]{0:T(128)}, u32[]{:S(2)}) copy-start(f32[32]{0:T(128)} %param.12) | copy-start | bytes 388
  15.2 4.8 %copy-start.5 = (f32[32]{0:T(128)S(1)}, f32[32]{0:T(128)}, u32[]{:S(2)}) copy-start(f32[32]{0:T(128)} %param.14) | copy-start | bytes 388
  27.6 2.1 %collective-permute-start.7 = (f32[1,1,1024]{2,1,0:T(1,128)S(1)}, f32[1,1,1024]{2,1,0:T(1,128)S(1)}, u32[]{:S(2)}, u32[]{:S(2)}) collective-permute-start(f32[1,1,1024]{2,1,0:T(1,128)S(1)} %get-tuple-element.39), channel_id=1, source_target_pairs={{0,1},{1,0},{2,3},{3,2},{4,5},{5,4},{6,7},{7,6},{8,9},{9,8},{10,11... | collective-permute-start | bytes 12296 | tf_op jit(solution)/shard_map/ppermute | solution.py:439
  27.6 3.0 %collective-permute-start.8 = (f32[1,1,1024]{2,1,0:T(1,128)S(1)}, f32[1,1,1024]{2,1,0:T(1,128)S(1)}, u32[]{:S(2)}, u32[]{:S(2)}) collective-permute-start(f32[1,1,1024]{2,1,0:T(1,128)S(1)} %get-tuple-element.40), channel_id=1, source_target_pairs={{0,3},{1,2},{2,1},{3,0},{4,7},{5,6},{6,5},{7,4},{8,11},{9,10},{10,... | collective-permute-start | bytes 12296 | tf_op jit(solution)/shard_map/ppermute | solution.py:439
  28.5 3.6 %collective-permute-start.9 = (f32[1,1,1024]{2,1,0:T(1,128)S(1)}, f32[1,1,1024]{2,1,0:T(1,128)S(1)}, u32[]{:S(2)}, u32[]{:S(2)}) collective-permute-start(f32[1,1,1024]{2,1,0:T(1,128)S(1)} %get-tuple-element.41), channel_id=1, source_target_pairs={{0,2},{1,3},{2,0},{3,1},{4,6},{5,7},{6,4},{7,5},{8,10},{9,11},{10,... | collective-permute-start | bytes 12296 | tf_op jit(solution)/shard_map/ppermute | solution.py:543

commit v4 on v3

--- a/solution.py
+++ b/solution.py
@@ -117,8 +117,11 @@
     tile = onehot(iota((chans, WINDOW * chans), 1) % chans == iota((chans, WINDOW * chans), 0))
     lane_t = iota((chans, WINDOW * chans), 1) // chans
     cin = first.shape[1]
-    ftile = onehot(iota((cin, cin * 16), 1) // 16 == iota((cin, cin * 16), 0))
-    ft = iota((chans, cin * 16), 1) % 16
+    taps_all = 9 * 16
+    ftile = onehot(iota((cin, taps_all), 1) // 16 % cin == iota((cin, taps_all), 0))
+    flane = iota((chans, taps_all), 1)
+    fparts = [jnp.zeros((chans, taps_all), F32)] * 8
+    back_parts = []
     row8 = iota((8, WINDOW * chans), 0)
     lane8 = iota((8, WINDOW * chans), 1) // chans
     for r in range(3):
@@ -131,23 +134,23 @@
             for c in range(3):
                 acc = jnp.where(lane_t == jo + c, taps[c], acc)
                 acc2 = jnp.where(lane_t == jo + 2 - c, flipped[c], acc2)
-            fwd[lo : lo + chans, :] = acc.astype(BF16)
-            bwd[lo : lo + chans, :] = acc2.astype(BF16)
+            wide = WINDOW * chans
+            fwd[jo * chans : (jo + 1) * chans, r * wide : (r + 1) * wide] = acc.astype(BF16)
+            bwd[lo : lo + chans, :] = (0.5 * acc2).astype(BF16)
         ftaps = [dot(first[3 * r + c], ftile, TN) for c in range(3)]
-        parts = []
         for jo in range(8):
-            acc = jnp.zeros((chans, cin * 16), F32)
             for c in range(3):
-                acc = jnp.where(ft == jo + c, ftaps[c], acc)
-            parts.append(acc)
-        first_fwd[r] = jnp.concatenate(parts, axis=0).astype(BF16)
+                hit = (flane // (16 * cin) == r) & (flane % 16 == jo + c)
+                fparts[jo] = jnp.where(hit, 0.5 * ftaps[c], fparts[jo])
         fback = [dot(first[3 * r + c], tile) for c in range(3)]
         for ch in range(2):
             acc = jnp.zeros((8, WINDOW * chans), F32)
             for c in range(3):
                 row = jnp.broadcast_to(fback[c][ch : ch + 1, :], acc.shape)
                 acc = jnp.where((lane8 == row8 + 2 - c) & (row8 < GROUP), row, acc)
-            first_bwd[16 * r + 8 * ch : 16 * r + 8 * ch + 8, :] = acc
+            back_parts.append(acc)
+    first_fwd[...] = jnp.concatenate(fparts, axis=0).astype(BF16)
+    first_bwd[...] = jnp.concatenate(back_parts, axis=0).astype(BF16)
 
 
 def spread(p, block):
@@ -239,16 +242,22 @@
         vh, vv = f[5:6].astype(BF16), f[6:7].astype(BF16)
         in_col = (x0 <= jcol) & (jcol <= x1)
         in_row = jnp.where((y0 <= jcol) & (jcol <= y1), one, zero)
-        maps[0, :, 0:NROWS] += dot(jnp.where(in_col, vh, zero), in_row, NT)
-        maps[1, :, 0:NROWS] += dot(jnp.where(in_col, vv, zero), in_row, NT)
-        acc = jnp.zeros((JCOLS, NROWS), F32)
+        demand = jnp.concatenate(
+            [jnp.where(in_col, vh, zero), jnp.where(in_col, vv, zero)], axis=0
+        )
+        got = dot(demand, in_row, NT)
+        pin_cols, pin_rows = [], []
         for p in range(pins):
             py = (y + f[7 + 2 * p : 8 + 2 * p]).astype(BF16)
             px = cut(x + f[8 + 2 * p : 9 + 2 * p]).astype(BF16)
-            acc += dot(
-                jnp.where(px == jcol, one, zero), jnp.where(py == jcol, one, zero), NT
-            )
-        maps[2, :, 0:NROWS] += acc
+            pin_cols.append(jnp.where(px == jcol, one, zero))
+            pin_rows.append(jnp.where(py == jcol, one, zero))
+        pinned = dot(
+            jnp.concatenate(pin_cols, axis=1), jnp.concatenate(pin_rows, axis=1), NT
+        )
+        maps[0, :, 0:NROWS] += got[0:JCOLS]
+        maps[1, :, 0:NROWS] += got[JCOLS:]
+        maps[2, :, 0:NROWS] += pinned
 
     for ref in net_refs:
         if ref.shape[0] == 1:
@@ -315,72 +324,74 @@
             + pltpu.roll(p[2 * edge :], 1, 1)
         )
 
-    lanes1 = iota((1, LANES), 1)
-    row_of = jnp.where(lanes1 < LANES - 64, lanes1, lanes1 - LANES)
-    grow = row_of + row0
-    row_ok = (row_of >= -1) & (row_of < span + BOX) & (grow >= 0) & (grow < all_rows)
-    bias_col = bias1[...].T
-    bias_rep = jnp.concatenate([bias_col] * 8, axis=0)
+    lanes1 = iota((1, span), 1)
+    grow = jnp.where(lanes1 < BOX, lanes1 + span, lanes1 - span) + row0
+    used = (lanes1 < BOX) | (lanes1 == span - 1)
+    row_ok = used & (grow >= 0) & (grow < all_rows)
+    bias_half = jnp.concatenate([0.5 * bias1[...].T] * 8, axis=0)
     jo_rows = iota((8 * chans, 1), 0) // chans
-
-    def step_b(g):
-        lo8 = g * 8
-        pre = bias_rep
-        for r in range(3):
-            f = feats[r, :, pl.ds(lo8, 16), :].reshape(3 * 16, LANES).astype(BF16)
-            pre = pre + dot(first_fwd[r], f)
-        lo = g * 8 * chans
-        slot = 8 * g + 1 + jo_rows
-        gcol = slot - 2 + col0
-        col_ok = (slot <= cols + 2) & (gcol >= 0) & (gcol < all_cols)
-        ok = col_ok & row_ok
-        s = 0.5 + 0.5 * jnp.tanh(0.5 * pre)
-        h = pre * s
-        slope = s + h * (1.0 - s)
-        bh = back_h[pl.ds(lo, 8 * chans), :]
-        if g in (0, cols // 8):
+    last_b = cols // 8
+
+    def hidden_step(g):
+        f = [feats[r, :, 8 * g : 8 * g + 16, :].reshape(3 * 16, LANES) for r in range(3)]
+        u = dot(first_fwd[...], jnp.concatenate(f, axis=0).astype(BF16)) + bias_half
+        s = slice(g * 8 * chans, (g + 1) * 8 * chans)
+        bh = back_h[s, :]
+        if g in (0, last_b):
             fix = fixes[0 if g == 0 else 1]
             bh = jnp.concatenate([bh[0:edge] + fix, bh[edge:]], axis=0)
-        hid[pl.ds(lo, 8 * chans), :] = jnp.where(ok, h, 0.0).astype(BF16)
-        back_p[pl.ds(lo, 8 * chans), :] = jnp.where(ok, bh * slope, 0.0).astype(BF16)
-
-    for g in range(pl.cdiv(cols + 2, 8)):
-        step_b(g)
+        a = 1.0 + jnp.tanh(u)
+        h = u * a
+        b = bh * (a + h * (2.0 - a))
+        if g in (0, last_b):
+            slot = 8 * g + 1 + jo_rows
+            gcol = slot - 2 + col0
+            ok = (slot <= cols + 2) & (gcol >= 0) & (gcol < all_cols)
+            h = jnp.where(ok, h, 0.0)
+            b = jnp.where(ok, b, 0.0)
+        h2 = jnp.where(row_ok, h[:, span:], 0.0)
+        back_p[s, 0:span] = b[:, 0:span].astype(BF16)
+        back_p[s, span:] = jnp.where(row_ok, b[:, span:], 0.0).astype(BF16)
+        h = jnp.concatenate([h[:, 0:span], h2], axis=1).astype(BF16)
+        hid[0, s, :] = pltpu.roll(h, 1, 1)[:, 0:span]
+        hid[1, s, :] = h[:, 0:span]
+        hid[2, s, :] = pltpu.roll(h, LANES - 1, 1)[:, 0:span]
 
     bias_out = jnp.concatenate([bias2[...].T] * GROUP, axis=0)
     groups_c = pl.cdiv(cols, GROUP)
 
     def back(g, lo):
-        q = dot(first_bwd[...].astype(BF16), back_p[pl.ds(lo, window), :])
+        q = dot(first_bwd[...], back_p[pl.ds(lo, window), :])
         gm = q[16:32] + pltpu.roll(q[0:16], LANES - 1, 1) + pltpu.roll(q[32:48], 1, 1)
-        grad_maps[pl.ds(pl.multiple_of(16 * g, 16), 16), :] = gm.astype(BF16)
-
-    def conv(lo):
-        p = dot(fwd[...], hid[pl.ds(lo, window), :])
-        out = (
-            p[block : 2 * block]
-            + pltpu.roll(p[0:block], 1, 1)
-            + pltpu.roll(p[2 * block :], LANES - 1, 1)
-        )
-        return (out[:, 0:span] + bias_out).astype(BF16)
-
-    def step_c(g, carry):
-        lo = pl.multiple_of(g * block, block)
-        congestion[pl.ds(lo, block), :] = conv(lo)
-        back(g, lo)
-        return carry
-
-    full = cols // GROUP
-    lax.fori_loop(0, full, step_c, 0, unroll=True)
-    if groups_c > full:
-        lo = full * block
-        last = (cols - full * GROUP) * chans
-        congestion[lo : lo + last, :] = conv(lo)[0:last]
-        back(full, lo)
-
-    x_rows = iota((8 * groups_c, 1), 0)
-    slot = GROUP * (x_rows // 8) + x_rows % 8 + 2
-    slot = jnp.where((x_rows % 8 < GROUP) & (slot < cols + 2), slot, 512).astype(F32)
+        for ch in range(2):
+            grad_maps[ch, GROUP * g : GROUP * (g + 1), :] = gm[8 * ch : 8 * ch + GROUP]
+
+    def taps_of(g):
+        lo = g * block
+        return jnp.concatenate([hid[r, lo : lo + window, :] for r in range(3)], axis=0)
+
+    def output_step(g):
+        both = [k for k in (g, g + 1) if k < groups_c]
+        out = dot(fwd[...], jnp.concatenate([taps_of(k) for k in both], axis=1))
+        for n_th, k in enumerate(both):
+            rows = min(block, (cols - GROUP * k) * chans)
+            part = out[0:rows, span * n_th : span * (n_th + 1)] + bias_out[0:rows]
+            congestion[k * block : k * block + rows, :] = part.astype(BF16)
+            back(k, k * block)
+
+    done = 0
+    for g in range(last_b + 1):
+        hidden_step(g)
+        while done < groups_c and (min(done + 1, groups_c - 1) * GROUP + WINDOW) <= 8 * g:
+            output_step(done)
+            done += 2
+    for g in range(done, groups_c, 2):
+        output_step(g)
+
+    kept = grad_maps.shape[1]
+    k_rows = iota((kept, 1), 0)
+    slot = jnp.where(k_rows < cols, k_rows + 2, 512).astype(F32)
+    sources = grad_maps[...].reshape(2 * kept, LANES)[:, 0:NROWS].astype(BF16)
     nets = net_refs[0].shape[2]
     fcol = col0.astype(F32)
     rows = iota((NROWS, nets), 0).astype(F32).astype(BF16)
@@ -391,10 +402,10 @@
         f, x, y, x0, x1, y1, width, height, cut = relative(ref, k, fcol)
         y0, y1 = y.astype(BF16), y1.astype(BF16)
         in_row = jnp.where((y0 <= rows) & (rows <= y1), one, zero)
-        h = dot(grad_maps[:, 0:NROWS], in_row).reshape(groups_c, 2, 8, nets)
-        in_col = ((x0 <= slot) & (slot <= x1)).reshape(groups_c, 8, nets)
-        s0 = jnp.sum(jnp.sum(jnp.where(in_col, h[:, 0], 0.0), axis=0), axis=0, keepdims=True)
-        s1 = jnp.sum(jnp.sum(jnp.where(in_col, h[:, 1], 0.0), axis=0), axis=0, keepdims=True)
+        h = dot(sources, in_row)
+        in_col = (x0 <= slot) & (slot <= x1)
+        s0 = jnp.sum(jnp.where(in_col, h[0:kept], 0.0), axis=0, keepdims=True)
+        s1 = jnp.sum(jnp.where(in_col, h[kept:], 0.0), axis=0, keepdims=True)
         out[k, 0:1, :] = s0 / height + s1 / width
 
     for ref, out in zip(net_refs, grads):
@@ -474,10 +485,10 @@
     weights = call(
         weight_body,
         [
+            jax.ShapeDtypeStruct((GROUP * chans, 3 * WINDOW * chans), BF16),
             jax.ShapeDtypeStruct((3 * GROUP * chans, WINDOW * chans), BF16),
-            jax.ShapeDtypeStruct((3 * GROUP * chans, WINDOW * chans), BF16),
-            jax.ShapeDtypeStruct((3, 8 * chans, cin * 16), BF16),
-            jax.ShapeDtypeStruct((48, WINDOW * chans), F32),
+            jax.ShapeDtypeStruct((8 * chans, 9 * 16), BF16),
+            jax.ShapeDtypeStruct((48, WINDOW * chans), BF16),
         ],
         2,
         cost=cost(40000000, 1000000),
@@ -524,9 +535,9 @@
         len(groups) + 12,
         scratch=[
             pltpu.VMEM((3, 3, JCOLS, LANES), F32),
+            pltpu.VMEM((3, rows_x, span), BF16),
             pltpu.VMEM((rows_x, LANES), BF16),
-            pltpu.VMEM((rows_x, LANES), BF16),
-            pltpu.VMEM((16 * pl.cdiv(cols, GROUP), LANES), BF16),
+            pltpu.VMEM((2, 8 * pl.cdiv(cols + GROUP, 8), LANES), F32),
         ],
         cost=cost(3000000000, 4000000),
     )(

time: 32.9 us -> 31.1 us (0.945)
  Pallas kernels: 16.9 us -> 14.9 us
    pallas_call x1, Pallas kernels: 7.58 us -> 5.62 us  [shards(): call(functools.partial(network_body, pins, len(groups)), [jax.ShapeDtypeS...]
  transfers between devices with their start and end apart: 10 -> 10, of which waited for: 4 -> 4; matrix products, arithmetic and copies ran while one was open for 0% -> 0% of each run, Pallas kernels for 24% -> 25%
where the time goes in v4:
time: 31.1 us; the launch traced here: 30.8 us
  Pallas kernels  14.9 us (48%)
  starting transfers between devices  8.91 us (29%)
  waiting for transfers between devices  5.61 us (18%)
  between operations  0.75 us (2%)
  other arithmetic  0.6 us (2%)
    pallas_call x1, Pallas kernels, shards(): call(functools.partial(network_body, pins, len(groups)), [jax.ShapeDtypeS...  5.62 us
    ppermute x4, starting transfers between devices, swap_strip(): return lax.ppermute(x, ('strip', 'col'), pairs)  4.63 us
    pallas_call x1, Pallas kernels, shards(): call(functools.partial(raster_body, pins, cols, span, len(groups)), [jax....  2.54 us
    ppermute x4, waiting for transfers between devices, swap_strip(): return lax.ppermute(x, ('strip', 'col'), pairs)  2.48 us
    pallas_call x1, Pallas kernels, shards(): call(functools.partial(back_halo_body, chans), jax.ShapeDtypeStruct((rows...  2.27 us
    pallas_call x1, Pallas kernels, shards(): call(functools.partial(back_own_body, chans), [jax.ShapeDtypeStruct((hidd...  1.93 us
    ppermute x4, starting transfers between devices, swap_col(): lax.ppermute(x, 'col', [(i, swapped(i, ncol, phase)) for i in range(ncol)])  1.68 us
    ppermute x1, waiting for transfers between devices, shards(): lax.ppermute(for_far, 'col', opposite)  1.63 us
  transfers between devices with their start and end apart: 10, of which 4 were waited for; matrix products, arithmetic and copies ran while one was open for 0% of the time, Pallas kernels for 25%

profile of v4, /device:TPU:16, one launch (start us, length us, event | category | flops | bytes accessed | tf_op | source)
XLA Modules:
  0.0 30.8 jit_solution(16661969638659683442)
XLA Ops:
  0.7 1.6 %shard_map.95 = (bf16[24,1024]{1,0:T(8,128)(2,1)}, bf16[24,1024]{1,0:T(8,128)(2,1)}, bf16[16,1024]{1,0:T(8,128)(2,1)}) custom-call(s32[4,1024]{1,0:T(4,128)} %bitcast.37, f32[1,1024]{1,0:T(1,128)} %bitcast.38, s32[4,2,1024]{2,1,0:T(2,128)} %bitcast.36, bf16[4096,128]{1,0:T(8,128)(2,1)} %bitcast.16, bf16[4096,128]{1,0:T(8,128)(2,1)} %bitcast.17), custom_call_target="tpu_custom_call" | custom-call | flops 10000 | bytes 400000 | tf_op jit(solution)/shard_map/pallas_call | solution.py:433
  2.3 1.5 %collective-permute-start.2 = (bf16[16,1024]{1,0:T(8,128)(2,1)}, bf16[16,1024]{1,0:T(8,128)(2,1)S(1)}, u32[]{:S(2)}, u32[]{:S(2)}) collective-permute-start(bf16[16,1024]{1,0:T(8,128)(2,1)} %get-tuple-element.22), channel_id=1, source_target_pairs={{0,2},{1,3},{2,0},{3,1},{4,6},{5,7},{6,4},{7,5},{8,10},{9,11},{10,... | collective-permute-start | bytes 98312 | tf_op jit(solution)/shard_map/ppermute | solution.py:466
  3.8 0.5 %shard_map.97 = (bf16[24,4096]{1,0:T(8,128)(2,1)S(1)}, bf16[24,4096]{1,0:T(8,128)(2,1)S(1)}) custom-call(bf16[4096,128]{1,0:T(8,128)(2,1)S(1)} %bitcast.18), custom_call_target="tpu_custom_call" | custom-call | flops 40000000 | bytes 1300000 | tf_op jit(solution)/shard_map/pallas_call | solution.py:472
  4.3 1.6 %collective-permute-start.5 = (bf16[24,4096]{1,0:T(8,128)(2,1)S(1)}, bf16[24,4096]{1,0:T(8,128)(2,1)S(1)}, u32[]{:S(2)}, u32[]{:S(2)}) collective-permute-start(bf16[24,4096]{1,0:T(8,128)(2,1)S(1)} %get-tuple-element.29), channel_id=1, source_target_pairs={{0,4},{1,5},{2,6},{3,7},{4,0},{5,1},{6,2},{7,3},{8,12},{9,13},{10,... | collective-permute-start | bytes 589832 | tf_op jit(solution)/shard_map/ppermute | solution.py:459
  5.8 0.4 %collective-permute-start.6 = (bf16[24,4096]{1,0:T(8,128)(2,1)S(1)}, bf16[24,4096]{1,0:T(8,128)(2,1)S(1)}, u32[]{:S(2)}, u32[]{:S(2)}) collective-permute-start(bf16[24,4096]{1,0:T(8,128)(2,1)S(1)} %get-tuple-element.30), channel_id=1, source_target_pairs={{0,1},{1,0},{2,3},{3,2},{4,8},{5,9},{6,10},{7,11},{8,4},{9,5},{10,... | collective-permute-start | bytes 589832 | tf_op jit(solution)/shard_map/ppermute | solution.py:459
  6.2 0.0 collective-permute-start
  6.2 0.6 %collective-permute-start.1 = (bf16[24,1024]{1,0:T(8,128)(2,1)}, bf16[24,1024]{1,0:T(8,128)(2,1)S(1)}, u32[]{:S(2)}, u32[]{:S(2)}) collective-permute-start(bf16[24,1024]{1,0:T(8,128)(2,1)} %get-tuple-element.24), channel_id=1, source_target_pairs={{0,3},{1,2},{2,1},{3,0},{4,7},{5,6},{6,5},{7,4},{8,11},{9,10},{10,... | collective-permute-start | bytes 147464 | tf_op jit(solution)/shard_map/ppermute | solution.py:450
  6.9 0.0 copy-done.1
  6.9 0.5 %shard_map.98 = (bf16[192,768]{1,0:T(8,128)(2,1)S(1)}, bf16[576,256]{1,0:T(8,128)(2,1)S(1)}, bf16[256,144]{1,0:T(8,128)(2,1)S(1)}, bf16[48,256]{1,0:T(8,128)(2,1)S(1)}) custom-call(bf16[9,32,32]{2,1,0:T(8,128)(2,1)S(1)} %bitcast.20, bf16[9,3,32]{2,1,0:T(4,128)(2,1)S(1)} %bitcast.33), custom_call_target="tpu_custom_call" | custom-call | flops 40000000 | bytes 1000000 | tf_op jit(solution)/shard_map/pallas_call | solution.py:485
  7.4 0.0 copy-start.2
  7.4 1.9 %shard_map.99 = (f32[4224,128]{1,0:T(8,128)S(1)}, f32[4224,128]{1,0:T(8,128)S(1)}) custom-call(bf16[4096,128]{1,0:T(8,128)(2,1)S(1)} %bitcast.19, bf16[576,256]{1,0:T(8,128)(2,1)S(1)} %get-tuple-element.31.bwd.refs_11_), custom_call_target="tpu_custom_call" | custom-call | flops 2000000000 | bytes 1000000 | tf_op jit(solution)/shard_map/pallas_call | solution.py:501
  9.3 0.0 collective-permute-done.2
  9.3 0.0 collective-permute-done
  9.4 0.6 %collective-permute-done.1 = bf16[24,1024]{1,0:T(8,128)(2,1)S(1)} collective-permute-done((bf16[24,1024]{1,0:T(8,128)(2,1)}, bf16[24,1024]{1,0:T(8,128)(2,1)S(1)}, u32[]{:S(2)}, u32[]{:S(2)}) %collective-permute-start.1) | collective-permute-done | bytes 49184 | tf_op jit(solution)/shard_map/ppermute | solution.py:450
  10.0 2.5 %shard_map.96 = (f32[3,144,256]{2,1,0:T(8,128)S(1)}, bf16[24,560]{1,0:T(8,128)(2,1)S(1)}, bf16[24,560]{1,0:T(8,128)(2,1)S(1)}) custom-call(bf16[1,16,1024]{2,1,0:T(8,128)(2,1)S(1)} %bitcast.29, bf16[1,24,1024]{2,1,0:T(8,128)(2,1)S(1)} %bitcast.21, bf16[1,24,1024]{2,1,0:T(8,128)(2,1)S(1)} %bitcast.25, bf16[1,16,1024]{2,1,0:T(8,128)(2,1)S(1)} %bitcast.31, ...), custom_call_target="tpu_custom_call" | custom-call | flops 1500000000 | bytes 1500000 | tf_op jit(solution)/shard_map/pallas_call | solution.py:508
  12.5 2.6 %collective-permute-start.3 = (bf16[24,560]{1,0:T(8,128)(2,1)S(1)}, bf16[24,560]{1,0:T(8,128)(2,1)S(1)}, u32[]{:S(2)}, u32[]{:S(2)}) collective-permute-start(bf16[24,560]{1,0:T(8,128)(2,1)S(1)} %get-tuple-element.26), channel_id=1, source_target_pairs={{0,4},{1,5},{2,6},{3,7},{4,0},{5,1},{6,2},{7,3},{8,12},{9,13},{10,... | collective-permute-start | bytes 80648 | tf_op jit(solution)/shard_map/ppermute | solution.py:459
  15.2 0.0 collective-permute-start.4
  15.2 0.0 collective-permute-done.5.cot_even
  15.2 0.0 collective-permute-done.6.cot_odd
  15.2 0.0 copy-start.4
  15.2 0.0 copy-start.5
  15.2 2.3 %shard_map.100.refs_7_ = f32[4352,256]{1,0:T(8,128)S(1)} custom-call(bf16[24,4096]{1,0:T(8,128)(2,1)S(1)} %collective-permute-done.5.cot_even, bf16[24,4096]{1,0:T(8,128)(2,1)S(1)} %collective-permute-done.6.cot_odd, bf16[576,256]{1,0:T(8,128)(2,1)S(1)} %get-tuple-element.31.bwd.refs_11_, f32[4224,128]{1,0:T(8,128)S(1)} %get-tuple-element.32.same_ref, ...), custom_call_target="tpu_custom_call" | custom-call | flops 2000000000 | bytes 1000000 | tf_op jit(solution)/shard_map/pallas_call | solution.py:523
  17.5 0.0 collective-permute-done.3.refs_5_
  17.5 2.5 %collective-permute-done.4.refs_6_ = bf16[24,560]{1,0:T(8,128)(2,1)S(1)} collective-permute-done((bf16[24,560]{1,0:T(8,128)(2,1)S(1)}, bf16[24,560]{1,0:T(8,128)(2,1)S(1)}, u32[]{:S(2)}, u32[]{:S(2)}) %collective-permute-start.4) | collective-permute-done | bytes 26912 | tf_op jit(solution)/shard_map/ppermute | solution.py:459
  19.9 5.6 %shard_map.101 = (bf16[4096,128]{1,0:T(8,128)(2,1)}, f32[1,1,1024]{2,1,0:T(1,128)S(1)}, f32[1,1,1024]{2,1,0:T(1,128)S(1)}, f32[1,1,1024]{2,1,0:T(1,128)S(1)}, f32[1,1,1024]{2,1,0:T(1,128)S(1)}) custom-call(bf16[1,16,1024]{2,1,0:T(8,128)(2,1)S(1)} %bitcast.30, bf16[1,24,1024]{2,1,0:T(8,128)(2,1)S(1)} %bitcast.23, bf16[1,24,1024]{2,1,0:T(8,128)(2,1)S(1)} %bitcast.27, ...), custom_call_target="tpu_custom_call" | custom-call | flops 3000000000 | bytes 4000000 | tf_op jit(solution)/shard_map/pallas_call | solution.py:531
  25.6 0.0 collective-permute-start.7
  25.6 1.1 %collective-permute-start.8 = (f32[1,1,1024]{2,1,0:T(1,128)S(1)}, f32[1,1,1024]{2,1,0:T(1,128)S(1)}, u32[]{:S(2)}, u32[]{:S(2)}) collective-permute-start(f32[1,1,1024]{2,1,0:T(1,128)S(1)} %get-tuple-element.40), channel_id=1, source_target_pairs={{0,3},{1,2},{2,1},{3,0},{4,7},{5,6},{6,5},{7,4},{8,11},{9,10},{10,... | collective-permute-start | bytes 12296 | tf_op jit(solution)/shard_map/ppermute | solution.py:450
  26.6 1.1 %collective-permute-start.9 = (f32[1,1,1024]{2,1,0:T(1,128)S(1)}, f32[1,1,1024]{2,1,0:T(1,128)S(1)}, u32[]{:S(2)}, u32[]{:S(2)}) collective-permute-start(f32[1,1,1024]{2,1,0:T(1,128)S(1)} %get-tuple-element.41), channel_id=1, source_target_pairs={{0,2},{1,3},{2,0},{3,1},{4,6},{5,7},{6,4},{7,5},{8,10},{9,11},{10,... | collective-permute-start | bytes 12296 | tf_op jit(solution)/shard_map/ppermute | solution.py:554
  27.7 0.0 collective-permute-done.7
  27.7 0.9 %collective-permute-done.8 = f32[1,1,1024]{2,1,0:T(1,128)S(1)} collective-permute-done((f32[1,1,1024]{2,1,0:T(1,128)S(1)}, f32[1,1,1024]{2,1,0:T(1,128)S(1)}, u32[]{:S(2)}, u32[]{:S(2)}) %collective-permute-start.8) | collective-permute-done | bytes 4128 | tf_op jit(solution)/shard_map/ppermute | solution.py:450
  28.6 1.6 %collective-permute-done.9 = f32[1,1,1024]{2,1,0:T(1,128)S(1)} collective-permute-done((f32[1,1,1024]{2,1,0:T(1,128)S(1)}, f32[1,1,1024]{2,1,0:T(1,128)S(1)}, u32[]{:S(2)}, u32[]{:S(2)}) %collective-permute-start.9) | collective-permute-done | bytes 4128 | tf_op jit(solution)/shard_map/ppermute | solution.py:554
  30.2 0.6 %add_add_fusion = f32[1,1,1024]{2,1,0:T(1,128)} fusion(f32[1,1,1024]{2,1,0:T(1,128)S(1)} %collective-permute-done.9, f32[1,1,1024]{2,1,0:T(1,128)S(1)} %collective-permute-done.8, f32[1,1,1024]{2,1,0:T(1,128)S(1)} %get-tuple-element.38, f32[1,1,1024]{2,1,0:T(1,128)S(1)} %collective-permute-done.7), kind=kLoop, calls=%fused_computation | loop fusion | flops 3072 | bytes 20480 | tf_op jit(solution)/shard_map/add | solution.py:551
  (8 shorter events, 0.0 us)
Async XLA Ops:
  0.6 3.1 %copy-start = (bf16[128,32,128]{2,1,0:T(8,128)(2,1)S(1)}, bf16[128,32,128]{2,1,0:T(8,128)(2,1)}, u32[]{:S(2)}) copy-start(bf16[128,32,128]{2,1,0:T(8,128)(2,1)} %param.15) | copy-start | bytes 3145732
  0.6 6.2 %copy-start.3 = (bf16[3,3,32,3]{2,3,1,0:T(4,128)(2,1)S(1)}, bf16[3,3,32,3]{2,3,1,0:T(4,128)(2,1)}, u32[]{:S(2)}) copy-start(bf16[3,3,32,3]{2,3,1,0:T(4,128)(2,1)} %param.11) | copy-start | bytes 5188
  0.7 6.2 %copy-start.1 = (bf16[3,3,32,32]{3,2,1,0:T(8,128)(2,1)S(1)}, bf16[3,3,32,32]{3,2,1,0:T(8,128)(2,1)}, u32[]{:S(2)}) copy-start(bf16[3,3,32,32]{3,2,1,0:T(8,128)(2,1)} %param.13) | copy-start | bytes 55300
  2.3 7.1 %collective-permute-start.2 = (bf16[16,1024]{1,0:T(8,128)(2,1)}, bf16[16,1024]{1,0:T(8,128)(2,1)S(1)}, u32[]{:S(2)}, u32[]{:S(2)}) collective-permute-start(bf16[16,1024]{1,0:T(8,128)(2,1)} %get-tuple-element.22), channel_id=1, source_target_pairs={{0,2},{1,3},{2,0},{3,1},{4,6},{5,7},{6,4},{7,5},{8,10},{9,11},{10,... | collective-permute-start | bytes 98312 | tf_op jit(solution)/shard_map/ppermute | solution.py:466
  4.3 10.9 %collective-permute-start.5 = (bf16[24,4096]{1,0:T(8,128)(2,1)S(1)}, bf16[24,4096]{1,0:T(8,128)(2,1)S(1)}, u32[]{:S(2)}, u32[]{:S(2)}) collective-permute-start(bf16[24,4096]{1,0:T(8,128)(2,1)S(1)} %get-tuple-element.29), channel_id=1, source_target_pairs={{0,4},{1,5},{2,6},{3,7},{4,0},{5,1},{6,2},{7,3},{8,12},{9,13},{10,... | collective-permute-start | bytes 589832 | tf_op jit(solution)/shard_map/ppermute | solution.py:459
  5.8 9.4 %collective-permute-start.6 = (bf16[24,4096]{1,0:T(8,128)(2,1)S(1)}, bf16[24,4096]{1,0:T(8,128)(2,1)S(1)}, u32[]{:S(2)}, u32[]{:S(2)}) collective-permute-start(bf16[24,4096]{1,0:T(8,128)(2,1)S(1)} %get-tuple-element.30), channel_id=1, source_target_pairs={{0,1},{1,0},{2,3},{3,2},{4,8},{5,9},{6,10},{7,11},{8,4},{9,5},{10,... | collective-permute-start | bytes 589832 | tf_op jit(solution)/shard_map/ppermute | solution.py:459
  6.2 3.1 %collective-permute-start = (bf16[24,1024]{1,0:T(8,128)(2,1)}, bf16[24,1024]{1,0:T(8,128)(2,1)S(1)}, u32[]{:S(2)}, u32[]{:S(2)}) collective-permute-start(bf16[24,1024]{1,0:T(8,128)(2,1)} %get-tuple-element.23), channel_id=1, source_target_pairs={{0,1},{1,0},{2,3},{3,2},{4,5},{5,4},{6,7},{7,6},{8,9},{9,8},{10,11... | collective-permute-start | bytes 147464 | tf_op jit(solution)/shard_map/ppermute | solution.py:450
  6.2 3.7 %collective-permute-start.1 = (bf16[24,1024]{1,0:T(8,128)(2,1)}, bf16[24,1024]{1,0:T(8,128)(2,1)S(1)}, u32[]{:S(2)}, u32[]{:S(2)}) collective-permute-start(bf16[24,1024]{1,0:T(8,128)(2,1)} %get-tuple-element.24), channel_id=1, source_target_pairs={{0,3},{1,2},{2,1},{3,0},{4,7},{5,6},{6,5},{7,4},{8,11},{9,10},{10,... | collective-permute-start | bytes 147464 | tf_op jit(solution)/shard_map/ppermute | solution.py:450
  7.4 2.6 %copy-start.2 = (bf16[16,1024]{1,0:T(8,128)(2,1)S(1)}, bf16[16,1024]{1,0:T(8,128)(2,1)}, u32[]{:S(2)}) copy-start(bf16[16,1024]{1,0:T(8,128)(2,1)} %get-tuple-element.22) | copy-start | bytes 98308
  12.5 5.0 %collective-permute-start.3 = (bf16[24,560]{1,0:T(8,128)(2,1)S(1)}, bf16[24,560]{1,0:T(8,128)(2,1)S(1)}, u32[]{:S(2)}, u32[]{:S(2)}) collective-permute-start(bf16[24,560]{1,0:T(8,128)(2,1)S(1)} %get-tuple-element.26), channel_id=1, source_target_pairs={{0,4},{1,5},{2,6},{3,7},{4,0},{5,1},{6,2},{7,3},{8,12},{9,13},{10,... | collective-permute-start | bytes 80648 | tf_op jit(solution)/shard_map/ppermute | solution.py:459
  15.2 4.8 %collective-permute-start.4 = (bf16[24,560]{1,0:T(8,128)(2,1)S(1)}, bf16[24,560]{1,0:T(8,128)(2,1)S(1)}, u32[]{:S(2)}, u32[]{:S(2)}) collective-permute-start(bf16[24,560]{1,0:T(8,128)(2,1)S(1)} %get-tuple-element.27), channel_id=1, source_target_pairs={{0,1},{1,0},{2,3},{3,2},{4,8},{5,9},{6,10},{7,11},{8,4},{9,5},{10,... | collective-permute-start | bytes 80648 | tf_op jit(solution)/shard_map/ppermute | solution.py:459
  15.2 4.8 %copy-start.4 = (f32[32]{0:T(128)S(1)}, f32[32]{0:T(128)}, u32[]{:S(2)}) copy-start(f32[32]{0:T(128)} %param.12) | copy-start | bytes 388
  15.2 4.8 %copy-start.5 = (f32[32]{0:T(128)S(1)}, f32[32]{0:T(128)}, u32[]{:S(2)}) copy-start(f32[32]{0:T(128)} %param.14) | copy-start | bytes 388
  25.6 2.1 %collective-permute-start.7 = (f32[1,1,1024]{2,1,0:T(1,128)S(1)}, f32[1,1,1024]{2,1,0:T(1,128)S(1)}, u32[]{:S(2)}, u32[]{:S(2)}) collective-permute-start(f32[1,1,1024]{2,1,0:T(1,128)S(1)} %get-tuple-element.39), channel_id=1, source_target_pairs={{0,1},{1,0},{2,3},{3,2},{4,5},{5,4},{6,7},{7,6},{8,9},{9,8},{10,11... | collective-permute-start | bytes 12296 | tf_op jit(solution)/shard_map/ppermute | solution.py:450
  25.6 3.0 %collective-permute-start.8 = (f32[1,1,1024]{2,1,0:T(1,128)S(1)}, f32[1,1,1024]{2,1,0:T(1,128)S(1)}, u32[]{:S(2)}, u32[]{:S(2)}) collective-permute-start(f32[1,1,1024]{2,1,0:T(1,128)S(1)} %get-tuple-element.40), channel_id=1, source_target_pairs={{0,3},{1,2},{2,1},{3,0},{4,7},{5,6},{6,5},{7,4},{8,11},{9,10},{10,... | collective-permute-start | bytes 12296 | tf_op jit(solution)/shard_map/ppermute | solution.py:450
  26.6 3.6 %collective-permute-start.9 = (f32[1,1,1024]{2,1,0:T(1,128)S(1)}, f32[1,1,1024]{2,1,0:T(1,128)S(1)}, u32[]{:S(2)}, u32[]{:S(2)}) collective-permute-start(f32[1,1,1024]{2,1,0:T(1,128)S(1)} %get-tuple-element.41), channel_id=1, source_target_pairs={{0,2},{1,3},{2,0},{3,1},{4,6},{5,7},{6,4},{7,5},{8,10},{9,11},{10,... | collective-permute-start | bytes 12296 | tf_op jit(solution)/shard_map/ppermute | solution.py:554
